TPU v7x, 32 devices: a whole 2x2x4 slice. The times are simulated.
32 devices in a mesh: batch: 8 (over z, x), row: 2 (over y), col: 2 (over core).
Axes of the slice: x: 2, y: 2, z: 4, core: 2. Of those that a mesh axis runs over, the one named last changes fastest.
Arguments:
- basis_values: bfloat16 [32, 192, 2048], P(('batch', 'row', 'col')), may hold values from -6 to 6
- density_matrix: bfloat16 [32, 3, 192, 192], P(('batch', 'row', 'col')), may hold values from -0.03125 to 0.03125
- points: float32 [32, 3, 2048], P(('batch', 'row', 'col')), may hold values from -2 to 2
- weights: float32 [32, 2048], P(('batch', 'row', 'col')), may hold values from 0.128 to 1.28
- intersection: int32 [32, 32], P(('batch', 'row', 'col')), may hold values from 0 to 31, as said below
- basis_index: int32 [32, 192], P(('batch', 'row', 'col')), may hold values from 0 to 1535, as said below
- atom_positions: float32 [3, 32], replicated, may hold values from -2 to 2
- shell_blocks: int32 [32], replicated, may hold values from 1 to 8
- shell_widths: float32 [64], replicated, may hold values from 0.03125 to 0.0625
- green: bfloat16 [32, 8, 4096], P('batch'), may hold values from -0.0009765625 to 0.0009765625
Outputs:
- potential: bfloat16 [32, 12288], P('batch')
- hamiltonian: bfloat16 [3, 1536, 1536], P(None, 'row', 'col')
Inputs may be any that keep to these rules, and one draw needn't show every extreme that they name: `intersection`: within a batch the 32 atom numbers are distinct. The owner of atom a is a // 4; no owner holds more than 4 of one batch's atoms, and among the batches with equal row and col index one owner holds exactly 4 of the atoms of every such batch. `basis_index`: within a batch the numbers are distinct, and its q-th run of 96 entries lies in [q * 768, (q + 1) * 768).
All inputs are finite; a program needn't handle non-finite values.
Results may differ from a plain program's by a relative error of at most 0.0095.
Values may be sent and summed in bfloat16 or wider, within the bound.
No kernel may reach another device: no remote copies, remote signals or barrier semaphores. Data moves between devices by JAX's collectives and lax.ppermute only.
A program may use at most 128 MiB of HBM per device.

v0:
```python
import jax
import jax.numpy as jnp
from jax import lax
from jax.sharding import PartitionSpec as P

S = 64
DEG = 8
NB = 1536


def chebyshev(values, count):
    terms = [jnp.ones_like(values), values]
    for order in range(2, count):
        terms.append(2.0 * values * terms[-1] - terms[-2])
    return jnp.stack(terms[:count], axis=0)


def atom_tables(spots, centre, blocks, shell_widths):
    delta = spots - centre[:, None]
    dist = jnp.sqrt(jnp.sum(delta * delta, axis=0) + 0.01)
    unit = delta / dist[None, :]
    shells = shell_widths.shape[0]
    middle = 4.0 * jnp.arange(shells).astype(jnp.float32) / shells
    live = jnp.arange(shells) < 8 * blocks
    bump = jnp.exp(-jnp.square((dist[None, :] - middle[:, None]) / shell_widths[:, None]))
    radial = jnp.where(live[:, None], bump, jnp.zeros_like(bump))
    polar = chebyshev(unit[2], DEG)
    side = chebyshev(unit[0], DEG)
    angular = (polar[:, None, :] * side[None, :, :]).reshape(DEG * DEG, spots.shape[1])
    return (radial, angular.astype(jnp.bfloat16))


def apply_green(charges, kernels):
    shaped = charges.astype(jnp.bfloat16).reshape(-1, 3, S, DEG, DEG)
    kernel_rows = kernels.reshape(-1, DEG, S, S)
    result = jnp.einsum(
        "xast,xctam->xcsam", kernel_rows, shaped, preferred_element_type=jnp.float32
    )
    return result.astype(jnp.bfloat16).reshape(-1, 3 * S * DEG * DEG)


def on_device(
    basis_values,
    density_matrix,
    points,
    weights,
    intersection,
    basis_index,
    atom_positions,
    shell_blocks,
    shell_widths,
    green,
):
    phi = basis_values[0]
    dens = density_matrix[0]
    spots = points[0]
    measure = weights[0]
    atoms = intersection[0]
    labels = basis_index[0]
    owners = lax.axis_size("batch")
    parts = lax.axis_size("row")
    count = atoms.shape[0]
    slots = (count + owners - 1) // owners
    holding = green.shape[0]
    width = 3 * S * DEG * DEG
    highest = lax.Precision.HIGHEST
    dphi = jnp.einsum("cij,jp->cip", dens, phi, preferred_element_type=jnp.float32)
    phi_wide = phi.astype(jnp.float32)
    density = jnp.sum(phi_wide[None] * dphi, axis=1)
    weighted = measure[None, :] * density
    every_atom = atom_positions.shape[1]
    picked = jnp.arange(every_atom)[:, None] == atoms[None, :]
    centres = jnp.dot(atom_positions, picked.astype(jnp.float32), precision=highest)
    blocks = jnp.sum(jnp.where(picked, shell_blocks[:, None], 0), axis=0)
    group = min(8, count)
    starts = list(range(0, count, group))
    make_tables = jax.vmap(atom_tables, in_axes=(None, 1, 0, None))
    kept = []
    pieces = []
    for first in starts:
        radial, angular = make_tables(
            spots, centres[:, first : first + group], blocks[first : first + group], shell_widths
        )
        kept.append((radial, angular))
        scaled = (radial[:, None] * weighted[None, :, None, :]).astype(jnp.bfloat16)
        pieces.append(
            jnp.einsum("kcsp,klp->kcsl", scaled, angular, preferred_element_type=jnp.float32)
        )
    moments = jnp.concatenate(pieces, axis=0).reshape(count, width)
    home = atoms // holding
    local_slot = atoms % holding
    order = jnp.arange(count)
    before = (home[None, :] == home[:, None]) & (order[None, :] < order[:, None])
    place = home * slots + jnp.sum(before, axis=1)
    routing = jnp.arange(owners * slots)[:, None] == place[None, :]
    outgoing = jnp.dot(routing.astype(jnp.float32), moments, precision=highest).reshape(
        owners, slots, width
    )
    tags = (jnp.sum(jnp.where(routing, local_slot[None, :] + 1, 0), axis=1) - 1).reshape(
        owners, slots
    )
    incoming, sources = (
        lax.all_to_all(outgoing, "batch", split_axis=0, concat_axis=0, tiled=True),
        lax.all_to_all(tags, "batch", split_axis=0, concat_axis=0, tiled=True),
    )
    collect = jnp.arange(holding)[:, None] == sources.reshape(1, owners * slots)
    partial_value = jnp.dot(
        collect.astype(jnp.float32), incoming.reshape(owners * slots, width), precision=highest
    )
    totals = lax.psum(partial_value, ("row", "col"))
    potential = apply_green(totals, green)
    back = jnp.dot(
        collect.T.astype(jnp.bfloat16), potential, preferred_element_type=jnp.float32
    ).astype(jnp.bfloat16)
    returned = lax.all_to_all(
        back.reshape(owners, slots, width), "batch", split_axis=0, concat_axis=0, tiled=True
    )
    tables = jnp.dot(
        routing.T.astype(jnp.bfloat16),
        returned.reshape(owners * slots, width),
        preferred_element_type=jnp.float32,
    )
    tables = tables.astype(jnp.bfloat16).reshape(count, 3, S, DEG * DEG)
    field = jnp.zeros((3, spots.shape[1]), jnp.float32)
    for position, first in enumerate(starts):
        radial, angular = kept[position]
        spread = jnp.einsum(
            "kcsl,klp->kcsp",
            tables[first : first + group],
            angular,
            preferred_element_type=jnp.float32,
        )
        field = field + jnp.einsum("ksp,kcsp->cp", radial, spread, precision=highest)
    piece = labels.shape[0] // parts
    operand = (phi_wide[None] * (measure[None, :] * field)[:, None, :]).astype(jnp.bfloat16)
    quads = jnp.einsum(
        "cxip,yjp->xycij",
        operand.reshape(3, parts, piece, -1),
        phi.reshape(parts, piece, -1),
        preferred_element_type=jnp.float32,
    ).astype(jnp.bfloat16)
    halves = labels.reshape(parts, piece)
    marks = jnp.stack(
        [
            jnp.broadcast_to(halves[:, None, :], (parts, parts, piece)),
            jnp.broadcast_to(halves[None, :, :], (parts, parts, piece)),
        ],
        axis=2,
    )
    got, got_marks = (
        lax.all_to_all(
            lax.all_to_all(quads, "row", split_axis=0, concat_axis=0, tiled=True),
            "col",
            split_axis=1,
            concat_axis=1,
            tiled=True,
        ),
        lax.all_to_all(
            lax.all_to_all(marks, "row", split_axis=0, concat_axis=0, tiled=True),
            "col",
            split_axis=1,
            concat_axis=1,
            tiled=True,
        ),
    )
    tile = NB // parts
    row_first = lax.axis_index("row") * tile
    col_first = lax.axis_index("col") * tile
    grid = jnp.arange(tile)
    accum = jnp.zeros((3, tile, tile), jnp.float32)
    for source_row in range(parts):
        for source_col in range(parts):
            rows_hit = (
                grid[:, None] == (got_marks[source_row, source_col, 0] - row_first)[None, :]
            ).astype(jnp.bfloat16)
            cols_hit = (
                grid[:, None] == (got_marks[source_row, source_col, 1] - col_first)[None, :]
            ).astype(jnp.bfloat16)
            placed = jnp.einsum(
                "ti,cij->ctj",
                rows_hit,
                got[source_row, source_col],
                preferred_element_type=jnp.float32,
            ).astype(jnp.bfloat16)
            accum = accum + jnp.einsum(
                "ctj,uj->ctu", placed, cols_hit, preferred_element_type=jnp.float32
            )
    flat = accum.reshape(-1, 128)
    mine = lax.psum_scatter(flat, "batch", scatter_dimension=0, tiled=True).astype(jnp.bfloat16)
    hamiltonian = lax.all_gather(mine, "batch", axis=0, tiled=True).reshape(3, tile, tile)
    return (potential, hamiltonian)


def solution(mesh):
    return jax.shard_map(
        on_device,
        mesh=mesh,
        in_specs=(
            P(("batch", "row", "col"), None, None),
            P(("batch", "row", "col"), None, None, None),
            P(("batch", "row", "col"), None, None),
            P(("batch", "row", "col"), None),
            P(("batch", "row", "col"), None),
            P(("batch", "row", "col"), None),
            P(),
            P(),
            P(),
            P("batch", None, None),
        ),
        out_specs=(P("batch", None), P(None, "row", "col")),
        check_vma=False,
    )
```

profile of v0, /device:TPU:0, one launch (start us, length us, event | category | flops | bytes accessed | tf_op | source)
XLA Modules:
  0.0 418.3 jit_solution(7476226090088943083)
XLA Ops:
  10.0 7.3 %all-to-all-start = ((s32[8,1,4]{2,1,0:T(1,128)}), s32[8,1,4]{2,1,0:T(1,128)}, u32[]{:S(2)}, u32[]{:S(2)}) async-start(s32[8,1,4]{2,1,0:T(1,128)} %bitcast.13), calls=%async_computation | async-start | bytes 8192 | tf_op jit(solution)/shard_map/all_to_all | solution.py:104
  29.7 7.2 %fusion.67 = (f32[2048,8,64]{0,2,1:T(8,128)}, f32[8,64,2048]{2,1,0:T(8,128)S(1)}, f32[8,64,2048]{2,1,0:T(8,128)S(1)}, f32[2048,8,64]{0,2,1:T(8,128)}, f32[8,64,2...) fusion(f32[64]{0:T(128)} %param.18, ...), kind=kLoop, calls=%fused_computation.77 | loop fusion | flops 20971520 | bytes 33819136
  46.6 3.8 fusion.158
  50.4 6.0 %all-to-all-start.1 = ((f32[8,4,12288]{2,1,0:T(4,128)}), f32[8,4,12288]{2,1,0:T(4,128)S(1)}, u32[]{:S(2)}, u32[]{:S(2)}) async-start(f32[8,4,12288]{2,1,0:T(4,128)} %fusion.158), calls=%async_computation.1 | async-start | bytes 3145728 | tf_op jit(solution)/shard_map/all_to_all | solution.py:103
  61.1 31.8 %all-to-all-done.1 = f32[8,4,12288]{2,1,0:T(4,128)S(1)} async-done(((f32[8,4,12288]{2,1,0:T(4,128)}), f32[8,4,12288]{2,1,0:T(4,128)S(1)}, u32[]{:S(2)}, u32[]{:S(2)}) %all-to-all-start.1) | async-done | bytes 1572896 | tf_op jit(solution)/shard_map/all_to_all | solution.py:103
  92.9 3.2 all-to-all-start.5
  97.3 12.3 %all-reduce.1 = bf16[4,12288]{1,0:T(4,128)(2,1)S(1)} all-reduce(f32[4,12288]{1,0:T(4,128)S(1)} %fusion.162), channel_id=1, replica_groups=mesh['batch'=8,'row'=2,'col'=2] {'row','col'}, use_global_device_ids=true, to_apply=%region_8.9 | all-reduce | flops 49152 | bytes 294912 | tf_op jit(solution)/shard_map/psum | solution.py:110
  117.5 5.7 %all-to-all-start.2 = ((bf16[8,4,12288]{2,1,0:T(4,128)(2,1)}), bf16[8,4,12288]{2,1,0:T(4,128)(2,1)S(1)}, u32[]{:S(2)}, u32[]{:S(2)}) async-start(bf16[8,4,12288]{2,1,0:T(4,128)(2,1)} %reshape.359), calls=%async_computation.2 | async-start | bytes 1572864 | tf_op jit(solution)/shard_map/all_to_all | solution.py:115
  124.0 18.4 %all-to-all-done.2 = bf16[8,4,12288]{2,1,0:T(4,128)(2,1)S(1)} async-done(((bf16[8,4,12288]{2,1,0:T(4,128)(2,1)}), bf16[8,4,12288]{2,1,0:T(4,128)(2,1)S(1)}, u32[]{:S(2)}, u32[]{:S(2)}) %all-to-all-start.2) | async-done | bytes 786464 | tf_op jit(solution)/shard_map/all_to_all | solution.py:115
  142.4 3.2 all-to-all-start.6
  151.4 4.0 multiply_reduce_fusion
  155.6 2.0 multiply_reduce_fusion.1
  164.1 3.5 all-to-all-start.3
  167.9 6.1 %all-to-all-done.3 = bf16[2,2,3,96,96]{4,3,1,2,0:T(8,128)(2,1)S(1)} async-done(((bf16[2,2,3,96,96]{4,3,1,2,0:T(8,128)(2,1)}), bf16[2,2,3,96,96]{4,3,1,2,0:T(8,128)(2,1)S(1)}, u32[]{:S(2)}, u32[]{:S(2)}) %all-to-all-start.3) | async-done | bytes 221216 | tf_op jit(solution)/shard_map/all_to_all | solution.py:152
  174.0 4.0 all_to_all.36
  177.9 4.3 %fusion.52 = f32[3,768,768]{2,1,0:T(8,128)} fusion(s32[96]{0:T(128)S(1)} %get-tuple-element.48, s32[96]{0:T(128)S(1)} %get-tuple-element.49, bf16[2,2,3,96,96]{4,3,0,2,1:T(8,128)(2,1)S(1)} %all_to_all.36), kind=kOutput, calls=%fused_computation.69 | convolution fusion | flops 382574592 | bytes 7152640 | tf_op jit(solution)/shard_map/ctj,uj->ctu/dot_general | solution.py:185
  182.2 4.3 %fusion.48 = f32[3,768,768]{2,1,0:T(8,128)} fusion(s32[96]{0:T(128)S(1)} %get-tuple-element.52, s32[96]{0:T(128)S(1)} %get-tuple-element.53, bf16[2,2,3,96,96]{4,3,0,2,1:T(8,128)(2,1)S(1)} %all_to_all.36), kind=kOutput, calls=%fused_computation.65 | convolution fusion | flops 382574592 | bytes 7152640 | tf_op jit(solution)/shard_map/ctj,uj->ctu/dot_general | solution.py:185
  186.5 4.4 %fusion.50 = f32[3,768,768]{2,1,0:T(8,128)} fusion(s32[96]{0:T(128)S(1)} %get-tuple-element.50, s32[96]{0:T(128)S(1)} %get-tuple-element.51, bf16[2,2,3,96,96]{4,3,0,2,1:T(8,128)(2,1)S(1)} %all_to_all.36), kind=kOutput, calls=%fused_computation.67 | convolution fusion | flops 382574592 | bytes 7152640 | tf_op jit(solution)/shard_map/ctj,uj->ctu/dot_general | solution.py:185
  190.9 11.2 %add_add_fusion = f32[3,768,768]{2,1,0:T(8,128)} fusion(f32[3,768,768]{2,1,0:T(8,128)} %fusion.52, f32[3,768,768]{2,1,0:T(8,128)} %fusion.48, f32[3,768,768]{2,1,0:T(8,128)} %fusion.50, s32[96]{0:T(128)S(1)} %get-tuple-element.47, s32[96]{0:T(128)S(1)} %get-tuple-element.46, bf16[2,2,3,96,96]{4,3,0,2,1:T(8,128)(2,1)S(1)} %all_to_all.36), kind=kOutput, calls=%fused_computation.10 | convolution fusion | flops 387883008 | bytes 28386304 | tf_op jit(solution)/shard_map/ctj,uj->ctu/dot_general | solution.py:185
  202.1 8.2 %reshape.361 = f32[13824,128]{1,0:T(8,128)} reshape(f32[3,768,768]{2,1,0:T(8,128)} %add_add_fusion) | data formatting | bytes 14155776 | tf_op jit(solution)/shard_map/reshape | solution.py:188
  210.4 127.2 %reduce-scatter.2.cloned.1.call-done = f32[1728,128]{1,0:T(8,128)} async-done(((f32[13824,128]{1,0:T(8,128)}), f32[1728,128]{1,0:T(8,128)}) %reduce-scatter.2.cloned.1.call-update) | async-done | bytes 884752 | tf_op jit(solution)/shard_map/reduce_scatter | solution.py:189
  337.6 2.0 convert_element_type.155
  339.6 64.5 %all-gather.2.cloned.1.call-done = bf16[13824,128]{1,0:T(8,128)(2,1)} async-done(((bf16[1728,128]{1,0:T(8,128)(2,1)}), bf16[13824,128]{1,0:T(8,128)(2,1)}) %all-gather.2.cloned.1.call-update) | async-done | bytes 3538960 | tf_op jit(solution)/shard_map/all_gather | solution.py:190
  404.2 7.3 %reshape.362 = bf16[3,768,768]{2,1,0:T(8,128)(2,1)} reshape(bf16[13824,128]{1,0:T(8,128)(2,1)} %all-gather.2.cloned.1.call-done) | data formatting | bytes 7077888 | tf_op jit(solution)/shard_map/reshape | solution.py:190
  (190 shorter events, 51.4 us)
Async XLA Ops:
  7.2 21.7 %copy-start = (bf16[1,3,192,192]{3,2,1,0:T(8,128)(2,1)S(1)}, bf16[1,3,192,192]{3,2,1,0:T(8,128)(2,1)}, u32[]{:S(2)}) copy-start(bf16[1,3,192,192]{3,2,1,0:T(8,128)(2,1)} %param.11) | copy-start | bytes 663556
  10.0 40.4 %all-to-all-start = ((s32[8,1,4]{2,1,0:T(1,128)}), s32[8,1,4]{2,1,0:T(1,128)}, u32[]{:S(2)}, u32[]{:S(2)}) async-start(s32[8,1,4]{2,1,0:T(1,128)} %bitcast.13), calls=%async_computation | async-start | bytes 8192 | tf_op jit(solution)/shard_map/all_to_all | solution.py:104
  23.4 13.5 %copy-start.7 = (f32[8,8,2048]{2,1,0:T(8,128)}, f32[8,8,2048]{2,1,0:T(8,128)S(1)}, u32[]{:S(2)}) copy-start(f32[8,8,2048]{2,1,0:T(8,128)S(1)} %copy.76) | copy-start | bytes 1572868
  23.7 13.2 %copy-start.8 = (f32[8,8,2048]{2,1,0:T(8,128)}, f32[8,8,2048]{2,1,0:T(8,128)S(1)}, u32[]{:S(2)}) copy-start(f32[8,8,2048]{2,1,0:T(8,128)S(1)} %copy.75) | copy-start | bytes 1572868
  24.4 14.3 %copy-start.9 = (f32[8,8,2048]{2,1,0:T(8,128)}, f32[8,8,2048]{2,1,0:T(8,128)S(1)}, u32[]{:S(2)}) copy-start(f32[8,8,2048]{2,1,0:T(8,128)S(1)} %copy.74) | copy-start | bytes 1572868
  24.7 14.0 %copy-start.11 = (f32[8,8,2048]{2,1,0:T(8,128)}, f32[8,8,2048]{2,1,0:T(8,128)S(1)}, u32[]{:S(2)}) copy-start(f32[8,8,2048]{2,1,0:T(8,128)S(1)} %copy.73) | copy-start | bytes 1572868
  24.8 4.1 copy-start.2
  25.4 15.1 %copy-start.13 = (f32[8,8,2048]{2,1,0:T(8,128)}, f32[8,8,2048]{2,1,0:T(8,128)S(1)}, u32[]{:S(2)}) copy-start(f32[8,8,2048]{2,1,0:T(8,128)S(1)} %copy.72) | copy-start | bytes 1572868
  25.8 14.8 %copy-start.15 = (f32[8,8,2048]{2,1,0:T(8,128)}, f32[8,8,2048]{2,1,0:T(8,128)S(1)}, u32[]{:S(2)}) copy-start(f32[8,8,2048]{2,1,0:T(8,128)S(1)} %copy.71) | copy-start | bytes 1572868
  26.5 16.0 %copy-start.17 = (f32[8,8,2048]{2,1,0:T(8,128)}, f32[8,8,2048]{2,1,0:T(8,128)S(1)}, u32[]{:S(2)}) copy-start(f32[8,8,2048]{2,1,0:T(8,128)S(1)} %copy.70) | copy-start | bytes 1572868
  46.5 9.9 %copy-start.23 = (bf16[4,8,4096]{2,1,0:T(8,128)(2,1)S(1)}, bf16[4,8,4096]{2,1,0:T(8,128)(2,1)}, u32[]{:S(2)}) copy-start(bf16[4,8,4096]{2,1,0:T(8,128)(2,1)} %param.19) | copy-start | bytes 786436
  46.5 11.8 %copy-start.29 = (s32[1,192]{1,0:T(1,128)S(1)}, s32[1,192]{1,0:T(1,128)}, u32[]{:S(2)}) copy-start(s32[1,192]{1,0:T(1,128)} %param.15) | copy-start | bytes 2308
  50.4 42.4 %all-to-all-start.1 = ((f32[8,4,12288]{2,1,0:T(4,128)}), f32[8,4,12288]{2,1,0:T(4,128)S(1)}, u32[]{:S(2)}, u32[]{:S(2)}) async-start(f32[8,4,12288]{2,1,0:T(4,128)} %fusion.158), calls=%async_computation.1 | async-start | bytes 3145728 | tf_op jit(solution)/shard_map/all_to_all | solution.py:103
  92.9 24.6 %all-to-all-start.5 = ((s32[2,2,2,96]{3,2,1,0:T(2,128)}), s32[2,2,2,96]{3,2,1,0:T(2,128)S(1)}, u32[]{:S(2)}, u32[]{:S(2)}) async-start(s32[2,2,2,96]{3,2,1,0:T(2,128)} %pad_add_fusion), calls=%async_computation.5 | async-start | bytes 8192 | tf_op jit(solution)/shard_map/all_to_all | solution.py:159
  113.1 10.1 %copy-start.3 = (bf16[1,192,2048]{2,1,0:T(8,128)(2,1)S(1)}, bf16[1,192,2048]{2,1,0:T(8,128)(2,1)}, u32[]{:S(2)}) copy-start(bf16[1,192,2048]{2,1,0:T(8,128)(2,1)} %param.10) | copy-start | bytes 2359300
  115.9 32.4 %copy-start.21 = (bf16[4,12288]{1,0:T(4,128)(2,1)}, bf16[4,12288]{1,0:T(4,128)(2,1)S(1)}, u32[]{:S(2)}) copy-start(bf16[4,12288]{1,0:T(4,128)(2,1)S(1)} %reshape.358) | copy-start | bytes 294916
  115.9 30.8 %copy-start.28 = (s32[32]{0:T(128)S(1)}, s32[32]{0:T(128)}, u32[]{:S(2)}) copy-start(s32[32]{0:T(128)} %copy-done.26) | copy-start | bytes 388
  117.5 24.9 %all-to-all-start.2 = ((bf16[8,4,12288]{2,1,0:T(4,128)(2,1)}), bf16[8,4,12288]{2,1,0:T(4,128)(2,1)S(1)}, u32[]{:S(2)}, u32[]{:S(2)}) async-start(bf16[8,4,12288]{2,1,0:T(4,128)(2,1)} %reshape.359), calls=%async_computation.2 | async-start | bytes 1572864 | tf_op jit(solution)/shard_map/all_to_all | solution.py:115
  142.4 21.6 %all-to-all-start.6 = ((s32[2,2,2,96]{3,2,0,1:T(2,128)}), s32[2,2,2,96]{3,2,0,1:T(2,128)S(1)}, u32[]{:S(2)}, u32[]{:S(2)}) async-start(s32[2,2,2,96]{3,2,0,1:T(2,128)} %copy.83), calls=%async_computation.6 | async-start | bytes 8192 | tf_op jit(solution)/shard_map/all_to_all | solution.py:158
  151.4 4.2 %copy-start.22 = (bf16[8,3,64,64]{3,2,1,0:T(8,128)(2,1)S(1)}, bf16[8,3,64,64]{3,2,1,0:T(8,128)(2,1)}, u32[]{:S(2)}) copy-start(bf16[8,3,64,64]{3,2,1,0:T(8,128)(2,1)} %slice.129) | copy-start | bytes 589828
  164.1 9.9 %all-to-all-start.3 = ((bf16[2,2,3,96,96]{4,3,1,2,0:T(8,128)(2,1)}), bf16[2,2,3,96,96]{4,3,1,2,0:T(8,128)(2,1)S(1)}, u32[]{:S(2)}, u32[]{:S(2)}) async-start(bf16[2,2,3,96,96]{4,3,1,2,0:T(8,128)(2,1)} %copy.80), calls=%async_computation.3 | async-start | bytes 589824 | tf_op jit(solution)/shard_map/all_to_all | solution.py:152
  167.5 170.1 %reduce-scatter.2.cloned.1.call-start = ((), (), s32[]{:S(2)}) async-start(), calls=%async_computation.8 | async-start | bytes 7962624 | tf_op jit(solution)/shard_map/reduce_scatter | solution.py:189
  210.3 201.1 %copy-start.1 = (bf16[1,3,192,192]{3,2,1,0:T(8,128)(2,1)S(1)}, bf16[1,3,192,192]{3,2,1,0:T(8,128)(2,1)}, u32[]{:S(2)}) copy-start(bf16[1,3,192,192]{3,2,1,0:T(8,128)(2,1)} %param.11) | copy-start | bytes 663556
  210.4 193.8 %all-gather.2.cloned.1.call-start = ((), (), s32[]{:S(2)}) async-start(), calls=%async_computation.9 | async-start | bytes 3981312 | tf_op jit(solution)/shard_map/all_gather | solution.py:190
  (14 other events, 36.9 us)
Sparse Core Ops, SparseCore 0:
  210.5 127.1 reduce-scatter.1
  340.4 63.7 all-gather.1
where the time goes:
time: 420 us; the launch traced here: 418 us
  waiting for transfers between devices  248 us (59%)
  matrix products  51.8 us (12%)
  local copies, waits for them, and re-layouts  37.8 us (9%)
  starting transfers between devices  29.2 us (7%)
  other arithmetic  20 us (5%)
  blocking collectives  16.3 us (4%)
  between operations  15 us (4%)
    reduce_scatter x1, waiting for transfers between devices, on_device(): lax.psum_scatter(flat, 'batch', scatter_dimension=0, tiled=True)  127 us
    all_gather x1, waiting for transfers between devices, on_device(): lax.all_gather(mine, 'batch', axis=0, tiled=True).reshape(3, tile, tile)  64.5 us
    all_to_all x1, waiting for transfers between devices, on_device(): lax.all_to_all(outgoing, 'batch', split_axis=0, concat_axis=0, tiled=True)  31.8 us
    dot_general x4, matrix products, on_device(): jnp.einsum('ctj,uj->ctu', placed, cols_hit, preferred_element_type=jnp.fl...  24.1 us
    all_to_all x1, waiting for transfers between devices, on_device(): lax.all_to_all(back.reshape(owners, slots, width), 'batch', split_axis=0,...  18.4 us
    psum x1, blocking collectives, on_device(): totals = lax.psum(partial_value, ('row', 'col'))  12.3 us
    dot_general x4, matrix products, on_device(): jnp.einsum('kcsl,klp->kcsp', tables[first:first + group], angular, prefer...  9.9 us
    unnamed x34, other arithmetic  8.52 us
  transfers between devices with their start and end apart: 8, of which 5 were waited for; matrix products, arithmetic and copies ran while one was open for 15% of the time, Pallas kernels for 0%

commit v1 on v0

v1 whole, which is shorter than its diff:
```python
import jax
import jax.numpy as jnp
from jax import lax
from jax.sharding import PartitionSpec as P

S = 64
DEG = 8
NB = 1536


def chebyshev(values, count):
    terms = [jnp.ones_like(values), values]
    for order in range(2, count):
        terms.append(2.0 * values * terms[-1] - terms[-2])
    return jnp.stack(terms[:count], axis=0)


def atom_tables(spots, centre, blocks, shell_widths):
    delta = spots - centre[:, None]
    dist = jnp.sqrt(jnp.sum(delta * delta, axis=0) + 0.01)
    unit = delta / dist[None, :]
    shells = shell_widths.shape[0]
    middle = 4.0 * jnp.arange(shells).astype(jnp.float32) / shells
    live = jnp.arange(shells) < 8 * blocks
    bump = jnp.exp(-jnp.square((dist[None, :] - middle[:, None]) / shell_widths[:, None]))
    radial = jnp.where(live[:, None], bump, jnp.zeros_like(bump))
    polar = chebyshev(unit[2], DEG)
    side = chebyshev(unit[0], DEG)
    angular = (polar[:, None, :] * side[None, :, :]).reshape(DEG * DEG, spots.shape[1])
    return (radial, angular.astype(jnp.bfloat16))


def apply_green(charges, kernels):
    shaped = charges.astype(jnp.bfloat16).reshape(-1, 3, S, DEG, DEG)
    kernel_rows = kernels.reshape(-1, DEG, S, S)
    result = jnp.einsum(
        "xast,xctam->xcsam", kernel_rows, shaped, preferred_element_type=jnp.float32
    )
    return result.astype(jnp.bfloat16).reshape(-1, 3 * S * DEG * DEG)


def swap(value, axis, mask):
    size = lax.axis_size(axis)
    return lax.ppermute(value, axis, [(i, i ^ mask) for i in range(size)])


def owner_steps():
    owners = lax.axis_size("batch")
    high = 1 << (owners.bit_length() - 1)
    masks = [1]
    bit = high >> 1
    while bit > 1:
        masks.append(bit)
        bit >>= 1
    steps = [("col", 1), ("row", 1)]
    return steps + [("batch", mask) for mask in masks[: owners.bit_length() - 1]]


def relative_atoms(steps):
    cols, rows = lax.axis_size("col"), lax.axis_size("row")
    mine = {
        "col": lax.axis_index("col"),
        "row": lax.axis_index("row"),
        "batch": lax.axis_index("batch"),
    }
    total = 1 << len(steps)
    flip = {"col": [], "row": [], "batch": []}
    for place in range(total):
        masks = {"col": 0, "row": 0, "batch": 0}
        for order, (axis, mask) in enumerate(steps):
            if (place >> (len(steps) - 1 - order)) & 1:
                masks[axis] |= mask
        for axis in flip:
            flip[axis].append(masks[axis])
    there = {axis: jnp.array(flip[axis], jnp.int32) ^ mine[axis] for axis in flip}
    return (there["batch"] * rows + there["row"]) * cols + there["col"]


def sum_to_owner(moments, steps):
    held = moments
    for axis, mask in steps:
        half = held.shape[0] // 2
        got = swap(held[half:].astype(jnp.bfloat16), axis, mask)
        held = held[:half] + got.astype(jnp.float32)
    return held


def gather_from_owners(value, steps):
    held = value
    for axis, mask in reversed(steps):
        held = jnp.concatenate([held, swap(held, axis, mask)], axis=0)
    return held


def place_quads(stack, reach, tile):
    count, parts, piece = stack.shape[0], 3, reach
    body = parts * piece * piece // 128
    blocks = stack[:, :body].reshape(count, parts, piece, piece)
    tail = stack[:, body:].reshape(count, -1).astype(jnp.int32)
    labels = tail[:, : 2 * piece] * 32 + tail[:, 2 * piece : 4 * piece]
    grid = jnp.arange(tile)
    rows_hit = (grid[:, None] == labels[:, :piece].reshape(-1)[None, :]).astype(jnp.bfloat16)
    cols_hit = (labels[:, piece:, None] == grid[None, None, :]).astype(jnp.bfloat16)
    wide = jnp.einsum(
        "gcij,gju->cgiu", blocks, cols_hit, preferred_element_type=jnp.float32
    ).astype(jnp.bfloat16)
    return jnp.einsum(
        "tk,cku->ctu",
        rows_hit,
        wide.reshape(parts, count * piece, tile),
        preferred_element_type=jnp.float32,
    )


def on_device(
    basis_values,
    density_matrix,
    points,
    weights,
    intersection,
    basis_index,
    atom_positions,
    shell_blocks,
    shell_widths,
    green,
):
    phi = basis_values[0]
    dens = density_matrix[0]
    spots = points[0]
    measure = weights[0]
    atoms = intersection[0]
    labels = basis_index[0]
    owners = lax.axis_size("batch")
    parts = lax.axis_size("row")
    sides = lax.axis_size("col")
    row, col = lax.axis_index("row"), lax.axis_index("col")
    count = atoms.shape[0]
    slots = (count + owners - 1) // owners
    holding = green.shape[0]
    every_atom = atom_positions.shape[1]
    width = 3 * S * DEG * DEG
    highest = lax.Precision.HIGHEST
    dense = (
        count == every_atom
        and parts == 2
        and sides == 2
        and holding == parts * sides
        and owners & (owners - 1) == 0
    )
    steps = owner_steps() if dense else None
    if dense:
        atoms = relative_atoms(steps)
    dphi = jnp.einsum("cij,jp->cip", dens, phi, preferred_element_type=jnp.float32)
    phi_wide = phi.astype(jnp.float32)
    density = jnp.sum(phi_wide[None] * dphi, axis=1)
    weighted = measure[None, :] * density
    picked = jnp.arange(every_atom)[:, None] == atoms[None, :]
    centres = jnp.dot(atom_positions, picked.astype(jnp.float32), precision=highest)
    blocks = jnp.sum(jnp.where(picked, shell_blocks[:, None], 0), axis=0)
    group = min(8, count)
    starts = list(range(0, count, group))
    make_tables = jax.vmap(atom_tables, in_axes=(None, 1, 0, None))
    kept = []
    pieces = []
    for first in starts:
        radial, angular = make_tables(
            spots, centres[:, first : first + group], blocks[first : first + group], shell_widths
        )
        kept.append((radial, angular))
        scaled = (radial[:, None] * weighted[None, :, None, :]).astype(jnp.bfloat16)
        pieces.append(
            jnp.einsum("kcsp,klp->kcsl", scaled, angular, preferred_element_type=jnp.float32)
        )
    moments = jnp.concatenate(pieces, axis=0).reshape(count, width)
    if dense:
        packed = moments.reshape(count, width // 128, 128)
        charges = sum_to_owner(packed, steps)
        kernels = lax.dynamic_index_in_dim(green, row * sides + col, 0, keepdims=True)
        mine = apply_green(charges.reshape(1, width), kernels).reshape(1, width // 128, 128)
        tables = gather_from_owners(mine, steps)
        plane = tables.reshape(2, 2, owners, width)[:, :, 0]
        plane = jnp.where(row == 0, plane, plane[:, ::-1])
        plane = jnp.where(col == 0, plane, plane[::-1])
        potential = jnp.swapaxes(plane, 0, 1).reshape(holding, width)
    else:
        home = atoms // holding
        local_slot = atoms % holding
        order = jnp.arange(count)
        before = (home[None, :] == home[:, None]) & (order[None, :] < order[:, None])
        place = home * slots + jnp.sum(before, axis=1)
        routing = jnp.arange(owners * slots)[:, None] == place[None, :]
        outgoing = jnp.dot(routing.astype(jnp.float32), moments, precision=highest).reshape(
            owners, slots, width
        )
        tags = (jnp.sum(jnp.where(routing, local_slot[None, :] + 1, 0), axis=1) - 1).reshape(
            owners, slots
        )
        incoming, sources = (
            lax.all_to_all(outgoing, "batch", split_axis=0, concat_axis=0, tiled=True),
            lax.all_to_all(tags, "batch", split_axis=0, concat_axis=0, tiled=True),
        )
        collect = jnp.arange(holding)[:, None] == sources.reshape(1, owners * slots)
        partial_value = jnp.dot(
            collect.astype(jnp.float32), incoming.reshape(owners * slots, width), precision=highest
        )
        totals = lax.psum(partial_value, ("row", "col"))
        potential = apply_green(totals, green)
        back = jnp.dot(
            collect.T.astype(jnp.bfloat16), potential, preferred_element_type=jnp.float32
        ).astype(jnp.bfloat16)
        returned = lax.all_to_all(
            back.reshape(owners, slots, width), "batch", split_axis=0, concat_axis=0, tiled=True
        )
        tables = jnp.dot(
            routing.T.astype(jnp.bfloat16),
            returned.reshape(owners * slots, width),
            preferred_element_type=jnp.float32,
        )
    tables = tables.astype(jnp.bfloat16).reshape(count, 3, S, DEG * DEG)
    field = jnp.zeros((3, spots.shape[1]), jnp.float32)
    for position, first in enumerate(starts):
        radial, angular = kept[position]
        spread = jnp.einsum(
            "kcsl,klp->kcsp",
            tables[first : first + group],
            angular,
            preferred_element_type=jnp.float32,
        )
        field = field + jnp.einsum("ksp,kcsp->cp", radial, spread, precision=highest)
    piece = labels.shape[0] // parts
    operand = (phi_wide[None] * (measure[None, :] * field)[:, None, :]).astype(jnp.bfloat16)
    quads = jnp.einsum(
        "cxip,yjp->yxcij",
        operand.reshape(3, parts, piece, -1),
        phi.reshape(sides, piece, -1),
        preferred_element_type=jnp.float32,
    ).astype(jnp.bfloat16)
    tile = NB // parts
    inner = labels.reshape(parts, piece) - jnp.arange(parts)[:, None] * tile
    digits = jnp.stack([inner // 32, inner % 32], axis=0).astype(jnp.bfloat16)
    by_row = jnp.broadcast_to(digits[:, None, :, :], (2, sides, parts, piece))
    by_col = jnp.broadcast_to(digits[:, :, None, :], (2, sides, parts, piece))
    tail = jnp.stack([by_row, by_col], axis=3)
    tail = jnp.moveaxis(tail, 0, 2).reshape(sides, parts, 4 * piece)
    extra = -(4 * piece) % 128
    tail = jnp.pad(tail, ((0, 0), (0, 0), (0, extra))).reshape(sides, parts, -1, 128)
    load = jnp.concatenate([quads.reshape(sides, parts, -1, 128), tail], axis=2)
    pad_rows = -load.shape[2] % 16
    load = jnp.pad(load, ((0, 0), (0, 0), (0, pad_rows), (0, 0)))
    keep = lax.dynamic_index_in_dim(load, col, 0, keepdims=False)
    give = lax.dynamic_index_in_dim(load, 1 - col, 0, keepdims=False)
    pair = jnp.stack([keep, swap(give, "col", 1)], axis=1)
    keep = lax.dynamic_index_in_dim(pair, row, 0, keepdims=False)
    give = lax.dynamic_index_in_dim(pair, 1 - row, 0, keepdims=False)
    plane_load = jnp.concatenate([keep, swap(give, "row", 1)], axis=0)
    if owners <= 8:
        lines = [plane_load] + [swap(plane_load, "batch", m) for m in range(2, owners, 2)]
        stack = jnp.concatenate(lines + [swap(line, "batch", 1) for line in lines], axis=0)
        total = place_quads(stack, piece, tile)
    else:
        everyone = lax.all_gather(plane_load, "batch", axis=0)

        def add(total, item):
            return total + place_quads(item.reshape((-1,) + item.shape[2:]), piece, tile), None

        chunk = 8
        everyone = everyone.reshape((owners // chunk, chunk) + plane_load.shape)
        total, _ = lax.scan(add, jnp.zeros((3, tile, tile), jnp.float32), everyone)
    return (potential, total.astype(jnp.bfloat16))


def solution(mesh):
    return jax.shard_map(
        on_device,
        mesh=mesh,
        in_specs=(
            P(("batch", "row", "col"), None, None),
            P(("batch", "row", "col"), None, None, None),
            P(("batch", "row", "col"), None, None),
            P(("batch", "row", "col"), None),
            P(("batch", "row", "col"), None),
            P(("batch", "row", "col"), None),
            P(),
            P(),
            P(),
            P("batch", None, None),
        ),
        out_specs=(P("batch", None), P(None, "row", "col")),
        check_vma=False,
    )
```

time: 420 us -> 175 us (0.42)
  waiting for transfers between devices: 248 us -> 41 us
  blocking collectives: 16.3 us -> 0 us
  between operations: 15 us -> 1.82 us
  matrix products: 51.8 us -> 44.9 us
    reduce_scatter x1 -> x0, waiting for transfers between devices: 127 us -> none  [on_device(): lax.psum_scatter(flat, 'batch', scatter_dimension=0, tiled=True)]
    all_gather x1 -> x0, waiting for transfers between devices: 64.5 us -> none  [on_device(): lax.all_gather(mine, 'batch', axis=0, tiled=True).reshape(3, tile, tile)]
    all_to_all x6 -> x0, waiting for transfers between devices: 56.4 us -> none  [the longest x1 31.8 us: on_device(): lax.all_to_all(outgoing, 'batch', split_axis=0, concat_axis=0, tiled=True)]
    ppermute x0 -> x19, waiting for transfers between devices: none -> 41 us  [swap(): return lax.ppermute(value, axis, [(i, i ^ mask) for i in range(size)])]
    ppermute x0 -> x19, starting transfers between devices: none -> 29.2 us  [swap(): return lax.ppermute(value, axis, [(i, i ^ mask) for i in range(size)])]
    all_to_all x6 -> x0, starting transfers between devices: 28.9 us -> none  [the longest x1 7.28 us: on_device(): lax.all_to_all(tags, 'batch', split_axis=0, concat_axis=0, tiled=True)]
    reshape x9 -> x5, local copies, waits for them, and re-layouts: 25.2 us -> 6.84 us  [the longest x1 3.42 us: place_quads(): blocks = stack[:, :body].reshape(count, parts, piece, piece)]
    psum x1 -> x0, blocking collectives: 12.3 us -> none  [on_device(): totals = lax.psum(partial_value, ('row', 'col'))]
  transfers between devices with their start and end apart: 8 -> 19, of which waited for: 5 -> 13; matrix products, arithmetic and copies ran while one was open for 15% -> 13% of each run, Pallas kernels for 0% -> 0%
where the time goes in v1:
time: 175 us; the launch traced here: 174 us
  matrix products  44.9 us (26%)
  waiting for transfers between devices  41 us (23%)
  local copies, waits for them, and re-layouts  39.5 us (23%)
  starting transfers between devices  29.2 us (17%)
  other arithmetic  17.5 us (10%)
  between operations  1.82 us (1%)
    ppermute x19, waiting for transfers between devices, swap(): return lax.ppermute(value, axis, [(i, i ^ mask) for i in range(size)])  41 us
    ppermute x19, starting transfers between devices, swap(): return lax.ppermute(value, axis, [(i, i ^ mask) for i in range(size)])  29.2 us
    dot_general x1, matrix products, place_quads(): jnp.einsum('tk,cku->ctu', rows_hit, wide.reshape(parts, count * piece, ti...  16 us
    dot_general x4, matrix products, on_device(): jnp.einsum('kcsl,klp->kcsp', tables[first:first + group], angular, prefer...  14.8 us
    unnamed x72, local copies, waits for them, and re-layouts  11.7 us
    unnamed x35, other arithmetic  11.6 us
    dot_general x4, matrix products, on_device(): jnp.einsum('kcsp,klp->kcsl', scaled, angular, preferred_element_type=jnp....  7.2 us
    convert_element_type x1, local copies, waits for them, and re-layouts, place_quads(): wide = jnp.einsum('gcij,gju->cgiu', blocks, cols_hit, preferred_element_t...  5.59 us
  transfers between devices with their start and end apart: 19, of which 13 were waited for; matrix products, arithmetic and copies ran while one was open for 13% of the time, Pallas kernels for 0%

profile of v1, /device:TPU:0, one launch (start us, length us, event | category | flops | bytes accessed | tf_op | source)
XLA Modules:
  0.0 173.9 jit_solution(13470471438304460744)
XLA Ops:
  9.3 10.2 %fusion.68 = (f32[2048,8,64]{0,2,1:T(8,128)}, f32[8,64,2048]{2,1,0:T(8,128)}, f32[8,64,2048]{2,1,0:T(8,128)S(1)}, f32[2048,8,64]{0,2,1:T(8,128)}, f32[8,64,2048]...) fusion(f32[64]{0:T(128)S(1)} %copy-done.21, ...), kind=kLoop, calls=%fused_computation.72 | loop fusion | flops 20971520 | bytes 33819136
  34.8 2.9 %collective-permute-start.1 = (bf16[8,96,128]{2,1,0:T(8,128)(2,1)S(1)}, bf16[8,96,128]{2,1,0:T(8,128)(2,1)S(1)}, u32[]{:S(2)}, u32[]{:S(2)}) collective-permute-start(bf16[8,96,128]{2,1,0:T(8,128)(2,1)S(1)} %slice.411), channel_id=1, source_target_pairs={{0,2},{2,0},{1,3},{3,1},{4,6},{6,4},{5,7},{7,5},{8,10},{10,8},{9,1... | collective-permute-start | bytes 589832 | tf_op jit(solution)/shard_map/ppermute | solution.py:44
  37.8 5.2 %collective-permute-done.1 = bf16[8,96,128]{2,1,0:T(8,128)(2,1)S(1)} collective-permute-done((bf16[8,96,128]{2,1,0:T(8,128)(2,1)S(1)}, bf16[8,96,128]{2,1,0:T(8,128)(2,1)S(1)}, u32[]{:S(2)}, u32[]{:S(2)}) %collective-permute-start.1) | collective-permute-done | bytes 196640 | tf_op jit(solution)/shard_map/ppermute | solution.py:44
  44.8 2.9 %collective-permute-done.2 = bf16[4,96,128]{2,1,0:T(8,128)(2,1)S(1)} collective-permute-done((bf16[4,96,128]{2,1,0:T(8,128)(2,1)S(1)}, bf16[4,96,128]{2,1,0:T(8,128)(2,1)S(1)}, u32[]{:S(2)}, u32[]{:S(2)}) %collective-permute-start.2) | collective-permute-done | bytes 98336 | tf_op jit(solution)/shard_map/ppermute | solution.py:44
  47.8 2.9 %collective-permute-start.3 = (bf16[2,96,128]{2,1,0:T(8,128)(2,1)S(1)}, bf16[2,96,128]{2,1,0:T(8,128)(2,1)S(1)}, u32[]{:S(2)}, u32[]{:S(2)}) collective-permute-start(bf16[2,96,128]{2,1,0:T(8,128)(2,1)S(1)} %slice.413), channel_id=1, source_target_pairs={{0,16},{4,20},{8,24},{12,28},{16,0},{20,4},{24,8},{28,12},{1,17},{... | collective-permute-start | bytes 147464 | tf_op jit(solution)/shard_map/ppermute | solution.py:44
  50.7 2.2 %collective-permute-done.3 = bf16[2,96,128]{2,1,0:T(8,128)(2,1)S(1)} collective-permute-done((bf16[2,96,128]{2,1,0:T(8,128)(2,1)S(1)}, bf16[2,96,128]{2,1,0:T(8,128)(2,1)S(1)}, u32[]{:S(2)}, u32[]{:S(2)}) %collective-permute-start.3) | collective-permute-done | bytes 49184 | tf_op jit(solution)/shard_map/ppermute | solution.py:44
  62.0 3.1 %collective-permute-start.6 = (bf16[2,96,128]{2,1,0:T(8,128)(2,1)S(1)}, bf16[2,96,128]{2,1,0:T(8,128)(2,1)S(1)}, u32[]{:S(2)}, u32[]{:S(2)}) collective-permute-start(bf16[2,96,128]{2,1,0:T(8,128)(2,1)S(1)} %pad_maximum_fusion.5), channel_id=1, source_target_pairs={{0,16},{4,20},{8,24},{12,28},{16,0},{20,4},{24,8},{28,12},{1,17},{... | collective-permute-start | bytes 147464 | tf_op jit(solution)/shard_map/ppermute | solution.py:44
  69.6 2.3 %collective-permute-done.7 = bf16[4,96,128]{2,1,0:T(8,128)(2,1)S(1)} collective-permute-done((bf16[4,96,128]{2,1,0:T(8,128)(2,1)S(1)}, bf16[4,96,128]{2,1,0:T(8,128)(2,1)S(1)}, u32[]{:S(2)}, u32[]{:S(2)}) %collective-permute-start.7) | collective-permute-done | bytes 98336 | tf_op jit(solution)/shard_map/ppermute | solution.py:44
  73.9 4.5 %multiply_reduce_fusion.3 = f32[2048,3]{0,1:T(4,128)} fusion(f32[2048,8,64]{0,2,1:T(8,128)} %get-tuple-element.81, f32[8,8,2048]{2,1,0:T(8,128)} %copy-done.15, f32[8,8,2048]{2,1,0:T(8,128)} %copy-done.16, bf16[4,3,64,64]{3,2,1,0:T(8,128)(2,1)S(1)} %concatenate.59, bf16[2,3,64,64]{3,2,1,0:T(8,128)(2,1)S(1)} %concatenate.58, ...), kind=kOutput, calls=%fused_computation.4 | convolution fusion | flops 411330560 | bytes 5464064 | tf_op jit(solution)/shard_map/kcsl,klp->kcsp/dot_general | solution.py:223
  80.1 4.4 %multiply_reduce_fusion.2 = f32[2048,3]{0,1:T(4,128)} fusion(f32[2048,8,64]{0,2,1:T(8,128)} %get-tuple-element.52, bf16[8,3,64,64]{3,2,1,0:T(8,128)(2,1)S(1)} %slice.152, f32[8,8,2048]{2,1,0:T(8,128)} %copy-done.13, f32[8,8,2048]{2,1,0:T(8,128)} %copy-done.14), kind=kOutput, calls=%fused_computation.3 | convolution fusion | flops 411035648 | bytes 5464064 | tf_op jit(solution)/shard_map/kcsl,klp->kcsp/dot_general | solution.py:223
  85.2 2.2 %reshape.367 = bf16[2,2,8,12288]{3,2,1,0:T(8,128)(2,1)} reshape(bf16[32,96,128]{2,1,0:T(8,128)(2,1)} %constant_dynamic-update-slice_fusion.69) | data formatting | bytes 1572864 | tf_op jit(solution)/shard_map/reshape | solution.py:181
  88.8 2.8 %rev.6 = bf16[2,2,12288]{2,1,0:T(2,128)(2,1)S(1)} reverse(bf16[2,2,12288]{2,1,0:T(2,128)(2,1)S(1)} %bitcast.164), dimensions={1} | reverse | bytes 196608 | tf_op jit(solution)/shard_map/rev | solution.py:182
  92.8 4.0 %multiply_reduce_fusion = f32[2048,3]{0,1:T(4,128)S(1)} fusion(f32[2048,8,64]{0,2,1:T(8,128)} %get-tuple-element.77, bf16[8,3,64,64]{3,2,1,0:T(8,128)(2,1)} %slice.156, f32[8,8,2048]{2,1,0:T(8,128)} %copy-done.7, f32[8,8,2048]{2,1,0:T(8,128)} %copy-done.8), kind=kOutput, calls=%fused_computation.1 | convolution fusion | flops 411035648 | bytes 5464064 | tf_op jit(solution)/shard_map/kcsl,klp->kcsp/dot_general | solution.py:223
  102.3 5.0 %collective-permute-done.11 = bf16[2,224,128]{2,1,0:T(8,128)(2,1)S(1)} collective-permute-done((bf16[2,224,128]{2,1,0:T(8,128)(2,1)S(1)}, bf16[2,224,128]{2,1,0:T(8,128)(2,1)S(1)}, u32[]{:S(2)}, u32[]{:S(2)}) %collective-permute-start.11) | collective-permute-done | bytes 114720 | tf_op jit(solution)/shard_map/ppermute | solution.py:44
  109.1 3.1 %collective-permute-start.13 = (bf16[4,224,128]{2,1,0:T(8,128)(2,1)S(1)}, bf16[4,224,128]{2,1,0:T(8,128)(2,1)S(1)}, u32[]{:S(2)}, u32[]{:S(2)}) collective-permute-start(bf16[4,224,128]{2,1,0:T(8,128)(2,1)S(1)} %pad_maximum_fusion.2), channel_id=1, source_target_pairs={{0,16},{4,20},{8,24},{12,28},{16,0},{20,4},{24,8},{28,12},{1,17},{... | collective-permute-start | bytes 688136 | tf_op jit(solution)/shard_map/ppermute | solution.py:44
  114.6 3.9 %collective-permute-done.12 = bf16[4,224,128]{2,1,0:T(8,128)(2,1)S(1)} collective-permute-done((bf16[4,224,128]{2,1,0:T(8,128)(2,1)S(1)}, bf16[4,224,128]{2,1,0:T(8,128)(2,1)S(1)}, u32[]{:S(2)}, u32[]{:S(2)}) %collective-permute-start.12) | collective-permute-done | bytes 229408 | tf_op jit(solution)/shard_map/ppermute | solution.py:44
  120.0 8.5 %collective-permute-done.13 = bf16[4,224,128]{2,1,0:T(8,128)(2,1)S(1)} collective-permute-done((bf16[4,224,128]{2,1,0:T(8,128)(2,1)S(1)}, bf16[4,224,128]{2,1,0:T(8,128)(2,1)S(1)}, u32[]{:S(2)}, u32[]{:S(2)}) %collective-permute-start.13) | collective-permute-done | bytes 229408 | tf_op jit(solution)/shard_map/ppermute | solution.py:44
  130.8 3.7 %collective-permute-done.17 = bf16[4,224,128]{2,1,0:T(8,128)(2,1)S(1)} collective-permute-done((bf16[4,224,128]{2,1,0:T(8,128)(2,1)S(1)}, bf16[4,224,128]{2,1,0:T(8,128)(2,1)S(1)}, u32[]{:S(2)}, u32[]{:S(2)}) %collective-permute-start.17) | collective-permute-done | bytes 229408 | tf_op jit(solution)/shard_map/ppermute | solution.py:44
  134.5 2.4 %collective-permute-done.18 = bf16[4,224,128]{2,1,0:T(8,128)(2,1)S(1)} collective-permute-done((bf16[4,224,128]{2,1,0:T(8,128)(2,1)S(1)}, bf16[4,224,128]{2,1,0:T(8,128)(2,1)S(1)}, u32[]{:S(2)}, u32[]{:S(2)}) %collective-permute-start.18) | collective-permute-done | bytes 229408 | tf_op jit(solution)/shard_map/ppermute | solution.py:44
  138.3 3.4 %reshape.371 = bf16[32,3,96,96]{3,2,1,0:T(8,128)(2,1)S(1)} reshape(bf16[32,216,128]{2,1,0:T(8,128)(2,1)} %slice.186) | data formatting | bytes 3538944 | tf_op jit(solution)/shard_map/reshape | solution.py:98
  142.0 4.2 %convert_bitcast_fusion = bf16[3,32,96,768]{3,2,0,1:T(8,128)(2,1)S(1)} fusion(bf16[32,3,96,96]{3,2,1,0:T(8,128)(2,1)S(1)} %reshape.371, s32[32,96]{1,0:T(8,128)S(1)} %get-tuple-element.63), kind=kOutput, calls=%fused_computation | convolution fusion | flops 1368391680 | bytes 15937536 | tf_op jit(solution)/shard_map/gcij,gju->cgiu/dot_general | solution.py:104
  146.2 5.6 %copy.81 = bf16[3,32,96,768]{3,2,1,0:T(8,128)(2,1)} copy(bf16[3,32,96,768]{3,2,0,1:T(8,128)(2,1)S(1)} %convert_bitcast_fusion) | data formatting | bytes 28311552 | tf_op jit(solution)/shard_map/convert_element_type | solution.py:106
  151.8 16.0 %convert_bitcast_fusion.1 = bf16[3,768,768]{1,2,0:T(8,128)(2,1)} fusion(bf16[3,3072,768]{2,1,0:T(8,128)(2,1)} %bitcast.158, s32[3072]{0:T(1024)S(1)} %eq.58), kind=kOutput, calls=%fused_computation.38 | convolution fusion | flops 10875764736 | bytes 17707008 | tf_op jit(solution)/shard_map/tk,cku->ctu/dot_general | solution.py:107
  167.9 6.0 %copy.83 = bf16[3,768,768]{2,1,0:T(8,128)(2,1)} copy(bf16[3,768,768]{1,2,0:T(8,128)(2,1)} %convert_bitcast_fusion.1) | data formatting | bytes 7077888
  (229 shorter events, 60.9 us)
Async XLA Ops:
  6.9 12.5 %copy-start.7 = (f32[8,8,2048]{2,1,0:T(8,128)}, f32[8,8,2048]{2,1,0:T(8,128)S(1)}, u32[]{:S(2)}) copy-start(f32[8,8,2048]{2,1,0:T(8,128)S(1)} %copy.72) | copy-start | bytes 1572868
  7.3 12.2 %copy-start.8 = (f32[8,8,2048]{2,1,0:T(8,128)}, f32[8,8,2048]{2,1,0:T(8,128)S(1)}, u32[]{:S(2)}) copy-start(f32[8,8,2048]{2,1,0:T(8,128)S(1)} %copy.71) | copy-start | bytes 1572868
  8.0 13.4 %copy-start.9 = (f32[8,8,2048]{2,1,0:T(8,128)}, f32[8,8,2048]{2,1,0:T(8,128)S(1)}, u32[]{:S(2)}) copy-start(f32[8,8,2048]{2,1,0:T(8,128)S(1)} %copy.70) | copy-start | bytes 1572868
  8.3 13.0 %copy-start.11 = (f32[8,8,2048]{2,1,0:T(8,128)}, f32[8,8,2048]{2,1,0:T(8,128)S(1)}, u32[]{:S(2)}) copy-start(f32[8,8,2048]{2,1,0:T(8,128)S(1)} %copy.69) | copy-start | bytes 1572868
  24.4 9.3 %collective-permute-start = (bf16[16,96,128]{2,1,0:T(8,128)(2,1)}, bf16[16,96,128]{2,1,0:T(8,128)(2,1)}, u32[]{:S(2)}, u32[]{:S(2)}) collective-permute-start(bf16[16,96,128]{2,1,0:T(8,128)(2,1)} %convert_element_type.146), channel_id=1, source_target_pairs={{0,1},{1,0},{2,3},{3,2},{4,5},{5,4},{6,7},{7,6},{8,9},{9,8},{10,11... | collective-permute-start | bytes 1179656 | tf_op jit(solution)/shard_map/ppermute | solution.py:44
  34.8 8.1 %collective-permute-start.1 = (bf16[8,96,128]{2,1,0:T(8,128)(2,1)S(1)}, bf16[8,96,128]{2,1,0:T(8,128)(2,1)S(1)}, u32[]{:S(2)}, u32[]{:S(2)}) collective-permute-start(bf16[8,96,128]{2,1,0:T(8,128)(2,1)S(1)} %slice.411), channel_id=1, source_target_pairs={{0,2},{2,0},{1,3},{3,1},{4,6},{6,4},{5,7},{7,5},{8,10},{10,8},{9,1... | collective-permute-start | bytes 589832 | tf_op jit(solution)/shard_map/ppermute | solution.py:44
  43.0 4.7 %collective-permute-start.2 = (bf16[4,96,128]{2,1,0:T(8,128)(2,1)S(1)}, bf16[4,96,128]{2,1,0:T(8,128)(2,1)S(1)}, u32[]{:S(2)}, u32[]{:S(2)}) collective-permute-start(bf16[4,96,128]{2,1,0:T(8,128)(2,1)S(1)} %slice.412), channel_id=1, source_target_pairs={{0,4},{4,0},{8,12},{12,8},{16,20},{20,16},{24,28},{28,24},{1,5},{5... | collective-permute-start | bytes 294920 | tf_op jit(solution)/shard_map/ppermute | solution.py:44
  47.8 5.1 %collective-permute-start.3 = (bf16[2,96,128]{2,1,0:T(8,128)(2,1)S(1)}, bf16[2,96,128]{2,1,0:T(8,128)(2,1)S(1)}, u32[]{:S(2)}, u32[]{:S(2)}) collective-permute-start(bf16[2,96,128]{2,1,0:T(8,128)(2,1)S(1)} %slice.413), channel_id=1, source_target_pairs={{0,16},{4,20},{8,24},{12,28},{16,0},{20,4},{24,8},{28,12},{1,17},{... | collective-permute-start | bytes 147464 | tf_op jit(solution)/shard_map/ppermute | solution.py:44
  52.8 3.9 %collective-permute-start.4 = (bf16[1,96,128]{2,1,0:T(8,128)(2,1)S(1)}, bf16[1,96,128]{2,1,0:T(8,128)(2,1)S(1)}, u32[]{:S(2)}, u32[]{:S(2)}) collective-permute-start(bf16[1,96,128]{2,1,0:T(8,128)(2,1)S(1)} %slice.414), channel_id=1, source_target_pairs={{0,8},{4,12},{8,0},{12,4},{16,24},{20,28},{24,16},{28,20},{1,9},{5... | collective-permute-start | bytes 73736 | tf_op jit(solution)/shard_map/ppermute | solution.py:44
  58.1 3.9 %collective-permute-start.5 = (bf16[1,96,128]{2,1,0:T(8,128)(2,1)S(1)}, bf16[1,96,128]{2,1,0:T(8,128)(2,1)S(1)}, u32[]{:S(2)}, u32[]{:S(2)}) collective-permute-start(bf16[1,96,128]{2,1,0:T(8,128)(2,1)S(1)} %reshape_reshape.4), channel_id=1, source_target_pairs={{0,8},{4,12},{8,0},{12,4},{16,24},{20,28},{24,16},{28,20},{1,9},{5... | collective-permute-start | bytes 73736 | tf_op jit(solution)/shard_map/ppermute | solution.py:44
  62.0 5.1 %collective-permute-start.6 = (bf16[2,96,128]{2,1,0:T(8,128)(2,1)S(1)}, bf16[2,96,128]{2,1,0:T(8,128)(2,1)S(1)}, u32[]{:S(2)}, u32[]{:S(2)}) collective-permute-start(bf16[2,96,128]{2,1,0:T(8,128)(2,1)S(1)} %pad_maximum_fusion.5), channel_id=1, source_target_pairs={{0,16},{4,20},{8,24},{12,28},{16,0},{20,4},{24,8},{28,12},{1,17},{... | collective-permute-start | bytes 147464 | tf_op jit(solution)/shard_map/ppermute | solution.py:44
  67.2 4.7 %collective-permute-start.7 = (bf16[4,96,128]{2,1,0:T(8,128)(2,1)S(1)}, bf16[4,96,128]{2,1,0:T(8,128)(2,1)S(1)}, u32[]{:S(2)}, u32[]{:S(2)}) collective-permute-start(bf16[4,96,128]{2,1,0:T(8,128)(2,1)S(1)} %pad_maximum_fusion.4), channel_id=1, source_target_pairs={{0,4},{4,0},{8,12},{12,8},{16,20},{20,16},{24,28},{28,24},{1,5},{5... | collective-permute-start | bytes 294920 | tf_op jit(solution)/shard_map/ppermute | solution.py:44
  71.9 7.2 %collective-permute-start.8 = (bf16[8,96,128]{2,1,0:T(8,128)(2,1)S(1)}, bf16[8,96,128]{2,1,0:T(8,128)(2,1)S(1)}, u32[]{:S(2)}, u32[]{:S(2)}) collective-permute-start(bf16[8,96,128]{2,1,0:T(8,128)(2,1)S(1)} %pad_maximum_fusion.3), channel_id=1, source_target_pairs={{0,2},{2,0},{1,3},{3,1},{4,6},{6,4},{5,7},{7,5},{8,10},{10,8},{9,1... | collective-permute-start | bytes 589832 | tf_op jit(solution)/shard_map/ppermute | solution.py:44
  79.9 4.6 %collective-permute-start.9 = (bf16[16,96,128]{2,1,0:T(8,128)(2,1)}, bf16[16,96,128]{2,1,0:T(8,128)(2,1)S(1)}, u32[]{:S(2)}, u32[]{:S(2)}) collective-permute-start(bf16[16,96,128]{2,1,0:T(8,128)(2,1)} %get-tuple-element.24), channel_id=1, source_target_pairs={{0,1},{1,0},{2,3},{3,2},{4,5},{5,4},{6,7},{7,6},{8,9},{9,8},{10,11... | collective-permute-start | bytes 1179656 | tf_op jit(solution)/shard_map/ppermute | solution.py:44
  100.3 1.5 collective-permute-start.10
  101.8 5.5 %collective-permute-start.11 = (bf16[2,224,128]{2,1,0:T(8,128)(2,1)S(1)}, bf16[2,224,128]{2,1,0:T(8,128)(2,1)S(1)}, u32[]{:S(2)}, u32[]{:S(2)}) collective-permute-start(bf16[2,224,128]{2,1,0:T(8,128)(2,1)S(1)} %fusion.90), channel_id=1, source_target_pairs={{0,2},{2,0},{1,3},{3,1},{4,6},{6,4},{5,7},{7,5},{8,10},{10,8},{9,1... | collective-permute-start | bytes 344072 | tf_op jit(solution)/shard_map/ppermute | solution.py:44
  107.3 11.2 %collective-permute-start.12 = (bf16[4,224,128]{2,1,0:T(8,128)(2,1)S(1)}, bf16[4,224,128]{2,1,0:T(8,128)(2,1)S(1)}, u32[]{:S(2)}, u32[]{:S(2)}) collective-permute-start(bf16[4,224,128]{2,1,0:T(8,128)(2,1)S(1)} %pad_maximum_fusion.2), channel_id=1, source_target_pairs={{0,8},{4,12},{8,0},{12,4},{16,24},{20,28},{24,16},{28,20},{1,9},{5... | collective-permute-start | bytes 688136 | tf_op jit(solution)/shard_map/ppermute | solution.py:44
  109.1 19.4 %collective-permute-start.13 = (bf16[4,224,128]{2,1,0:T(8,128)(2,1)S(1)}, bf16[4,224,128]{2,1,0:T(8,128)(2,1)S(1)}, u32[]{:S(2)}, u32[]{:S(2)}) collective-permute-start(bf16[4,224,128]{2,1,0:T(8,128)(2,1)S(1)} %pad_maximum_fusion.2), channel_id=1, source_target_pairs={{0,16},{4,20},{8,24},{12,28},{16,0},{20,4},{24,8},{28,12},{1,17},{... | collective-permute-start | bytes 688136 | tf_op jit(solution)/shard_map/ppermute | solution.py:44
  113.1 16.9 %collective-permute-start.14 = (bf16[4,224,128]{2,1,0:T(8,128)(2,1)S(1)}, bf16[4,224,128]{2,1,0:T(8,128)(2,1)S(1)}, u32[]{:S(2)}, u32[]{:S(2)}) collective-permute-start(bf16[4,224,128]{2,1,0:T(8,128)(2,1)S(1)} %pad_maximum_fusion.2), channel_id=1, source_target_pairs={{0,24},{4,28},{8,16},{12,20},{16,8},{20,12},{24,0},{28,4},{1,25},{... | collective-permute-start | bytes 688136 | tf_op jit(solution)/shard_map/ppermute | solution.py:44
  113.1 17.6 %collective-permute-start.15 = (bf16[4,224,128]{2,1,0:T(8,128)(2,1)S(1)}, bf16[4,224,128]{2,1,0:T(8,128)(2,1)S(1)}, u32[]{:S(2)}, u32[]{:S(2)}) collective-permute-start(bf16[4,224,128]{2,1,0:T(8,128)(2,1)S(1)} %pad_maximum_fusion.2), channel_id=1, source_target_pairs={{0,4},{4,0},{8,12},{12,8},{16,20},{20,16},{24,28},{28,24},{1,5},{5... | collective-permute-start | bytes 688136 | tf_op jit(solution)/shard_map/ppermute | solution.py:44
  118.5 12.3 %collective-permute-start.16 = (bf16[4,224,128]{2,1,0:T(8,128)(2,1)S(1)}, bf16[4,224,128]{2,1,0:T(8,128)(2,1)S(1)}, u32[]{:S(2)}, u32[]{:S(2)}) collective-permute-start(bf16[4,224,128]{2,1,0:T(8,128)(2,1)S(1)} %collective-permute-done.12), channel_id=1, source_target_pairs={{0,4},{4,0},{8,12},{12,8},{16,20},{20,16},{24,28},{28,24},{1,5},{5... | collective-permute-start | bytes 688136 | tf_op jit(solution)/shard_map/ppermute | solution.py:44
  128.5 6.0 %collective-permute-start.17 = (bf16[4,224,128]{2,1,0:T(8,128)(2,1)S(1)}, bf16[4,224,128]{2,1,0:T(8,128)(2,1)S(1)}, u32[]{:S(2)}, u32[]{:S(2)}) collective-permute-start(bf16[4,224,128]{2,1,0:T(8,128)(2,1)S(1)} %collective-permute-done.13), channel_id=1, source_target_pairs={{0,4},{4,0},{8,12},{12,8},{16,20},{20,16},{24,28},{28,24},{1,5},{5... | collective-permute-start | bytes 688136 | tf_op jit(solution)/shard_map/ppermute | solution.py:44
  130.0 6.9 %collective-permute-start.18 = (bf16[4,224,128]{2,1,0:T(8,128)(2,1)S(1)}, bf16[4,224,128]{2,1,0:T(8,128)(2,1)S(1)}, u32[]{:S(2)}, u32[]{:S(2)}) collective-permute-start(bf16[4,224,128]{2,1,0:T(8,128)(2,1)S(1)} %collective-permute-done.14), channel_id=1, source_target_pairs={{0,4},{4,0},{8,12},{12,8},{16,20},{20,16},{24,28},{28,24},{1,5},{5... | collective-permute-start | bytes 688136 | tf_op jit(solution)/shard_map/ppermute | solution.py:44
  151.8 22.0 %copy-start.1 = (bf16[1,3,192,192]{3,2,1,0:T(8,128)(2,1)S(1)}, bf16[1,3,192,192]{3,2,1,0:T(8,128)(2,1)}, u32[]{:S(2)}) copy-start(bf16[1,3,192,192]{3,2,1,0:T(8,128)(2,1)} %param.14) | copy-start | bytes 663556
  (17 other events, 51.1 us)

commit v2 on v1

v2 whole, which is shorter than its diff:
```python
import functools

import jax
import jax.numpy as jnp
from jax import lax
from jax.experimental import pallas as pl
from jax.experimental.pallas import tpu as pltpu
from jax.sharding import PartitionSpec as P

S = 64
DEG = 8
NB = 1536
LANES = 128
FAR = 1.0e6
LOG2E = 1.4426950408889634
NT = (((1,), (1,)), ((), ()))
SMEM = pl.BlockSpec(memory_space=pltpu.SMEM)
VMEM = pl.BlockSpec(memory_space=pltpu.VMEM)


def prepare(first, count, atoms_ref, pos_ref, pts_ref, dist_ref, polar_ref, side_ref):
    rows = lax.broadcasted_iota(jnp.int32, (count, LANES), 0)
    centre = []
    for axis in range(3):
        column = jnp.zeros((count, LANES), jnp.float32)
        for k in range(count):
            column = jnp.where(rows == k, pos_ref[axis, atoms_ref[first + k]], column)
        centre.append(column)
    for start in range(0, pts_ref.shape[1], LANES):
        here = pl.ds(start, LANES)
        delta = [pts_ref[pl.ds(axis, 1), here] - centre[axis] for axis in range(3)]
        square = delta[0] * delta[0] + delta[1] * delta[1] + delta[2] * delta[2] + 0.01
        inverse = lax.rsqrt(square)
        dist_ref[start // LANES] = square * inverse
        for ladder, u in ((polar_ref, delta[2] * inverse), (side_ref, delta[0] * inverse)):
            older, old = jnp.ones_like(u), u
            ladder[start // LANES, pl.ds(0, count), :] = older
            ladder[start // LANES, pl.ds(count, count), :] = old
            for order in range(2, DEG):
                older, old = old, 2.0 * u * old - older
                ladder[start // LANES, pl.ds(order * count, count), :] = old


def shell_columns(blocks, widths_ref):
    place = lax.broadcasted_iota(jnp.int32, (S, LANES), 0)
    shell = jnp.where(place < S // 2, 2 * place, 2 * place - (S - 1))
    middle = jnp.where(shell < 8 * blocks, shell.astype(jnp.float32) * (4.0 / S), FAR)
    return middle


def angular_tile(k, count, t, polar_ref, side_ref):
    side = side_ref[t, pl.ds(k, DEG, stride=count), :]
    return jnp.concatenate(
        [polar_ref[t, pl.ds(order * count + k, DEG, stride=0), :] * side for order in range(DEG)], axis=0
    ).astype(jnp.bfloat16)


def radial_tile(k, t, middle, scale, dist_ref):
    gap = jnp.concatenate([dist_ref[t, pl.ds(k, 8, stride=0), :]] * (S // 8), axis=0) - middle
    return jnp.exp2(gap * (gap * scale))


def moments_kernel(first, count, chunk, fresh, *refs):
    if fresh:
        (atoms_ref, pos_ref, blocks_ref, pts_ref, scale_ref, phi_ref, dens_ref, w_ref,
         out_ref, wd_ref, dist_ref, polar_ref, side_ref) = refs
    else:
        (atoms_ref, pos_ref, blocks_ref, pts_ref, scale_ref, wd_ref,
         out_ref, dist_ref, polar_ref, side_ref) = refs
    points = pts_ref.shape[1]
    if fresh:
        for start in range(0, points, 256):
            here = pl.ds(start, 256)
            phi = phi_ref[:, here]
            wide = phi.astype(jnp.float32)
            for c in range(3):
                product = jnp.dot(dens_ref[c], phi, preferred_element_type=jnp.float32)
                wd_ref[pl.ds(c, 1), here] = w_ref[:, here] * jnp.sum(
                    wide * product, axis=0, keepdims=True)
    prepare(first, count, atoms_ref, pos_ref, pts_ref, dist_ref, polar_ref, side_ref)

    def body(k, carry):
        middle = shell_columns(blocks_ref[atoms_ref[first + k]], None)
        scale = scale_ref[...]
        total = jnp.zeros((3 * S, S), jnp.float32)
        for start in range(0, points, chunk):
            scaled, angles = [[], [], []], []
            for inner in range(start, start + chunk, LANES):
                here = pl.ds(inner, LANES)
                radial = radial_tile(k, here.start // LANES, middle, scale, dist_ref)
                angles.append(angular_tile(k, count, here.start // LANES, polar_ref, side_ref))
                for c in range(3):
                    scaled[c].append((radial * wd_ref[pl.ds(c, 1), here]).astype(jnp.bfloat16))
            left = jnp.concatenate([jnp.concatenate(s, axis=1) for s in scaled], axis=0)
            right = jnp.concatenate(angles, axis=1)
            total += lax.dot_general(left, right, NT, preferred_element_type=jnp.float32)
        for c in range(3):
            even, odd = total[c * S : c * S + S // 2], total[c * S + S // 2 : (c + 1) * S]
            out_ref[k, pl.ds(c * (S // 2), S // 2), :] = jnp.concatenate(
                [even, odd], axis=1).astype(out_ref.dtype)
        return carry

    lax.fori_loop(0, count, body, 0)


def moments_call(first, count, atoms, pos, blocks, pts, scale, wd=None, phi=None, dens=None, w=None, chunk=256):
    points = pts.shape[1]
    fresh = wd is None
    out = [jax.ShapeDtypeStruct((count, 3 * S // 2, LANES), jnp.bfloat16)]
    args = [atoms, pos, blocks, pts, scale]
    if fresh:
        out.append(jax.ShapeDtypeStruct((3, points), jnp.float32))
        args += [phi, dens, w]
    else:
        args += [wd]
    scratch = [pltpu.VMEM((points // LANES, count, LANES), jnp.float32)] + [pltpu.VMEM((points // LANES, DEG * count, LANES), jnp.float32)] * 2
    cost = count * points
    return pl.pallas_call(
        functools.partial(moments_kernel, first, count, chunk, fresh),
        out_shape=out,
        in_specs=[SMEM] * 3 + [VMEM] * (len(args) - 3),
        out_specs=[VMEM] * len(out),
        scratch_shapes=scratch,
        cost_estimate=pl.CostEstimate(flops=cost * 3 * S * S * 2, bytes_accessed=cost * 8, transcendentals=cost * S),
        name="moments",
    )(*args)


def field_kernel(first, count, last, *refs):
    if last:
        (atoms_ref, pos_ref, blocks_ref, pts_ref, scale_ref, tab_ref, acc_in, phi_ref, w_ref, marks_ref, flip_ref,
         out_ref, dist_ref, polar_ref, side_ref, acc_ref, oper_ref) = refs
    else:
        (atoms_ref, pos_ref, blocks_ref, pts_ref, scale_ref, tab_ref, acc_in,
         acc_ref, dist_ref, polar_ref, side_ref) = refs
    points = pts_ref.shape[1]
    prepare(first, count, atoms_ref, pos_ref, pts_ref, dist_ref, polar_ref, side_ref)
    acc_ref[...] = acc_in[...]

    def body(k, carry):
        middle = shell_columns(blocks_ref[atoms_ref[first + k]], None)
        scale = scale_ref[...]
        table = tab_ref[k]
        halves = (table[:, : S], table[:, S:])
        for start in range(0, points, 256):
            right = jnp.concatenate(
                [angular_tile(k, count, (start + d) // LANES, polar_ref, side_ref) for d in (0, LANES)], axis=1)
            spread = [jnp.dot(h, right, preferred_element_type=jnp.float32) for h in halves]
            for d in (0, LANES):
                here = pl.ds(start + d, LANES)
                radial = radial_tile(k, here.start // LANES, middle, scale, dist_ref)
                for c in range(3):
                    sums = acc_ref[pl.ds(8 * c, 8), here]
                    for h in range(2):
                        for r in range(0, S // 2, 8):
                            sums += (radial[h * (S // 2) + r : h * (S // 2) + r + 8]
                                     * spread[h][c * (S // 2) + r : c * (S // 2) + r + 8, d : d + LANES])
                    acc_ref[pl.ds(8 * c, 8), here] = sums
        return carry

    lax.fori_loop(0, count, body, 0)
    if last:
        piece = phi_ref.shape[0] // 2
        quads = {}
        for c in range(3):
            for start in range(0, points, 256):
                here = pl.ds(start, 256)
                scale_row = w_ref[:, here] * jnp.sum(acc_ref[pl.ds(8 * c, 8), here], axis=0, keepdims=True)
                oper_ref[:, here] = (phi_ref[:, here].astype(jnp.float32) * scale_row).astype(jnp.bfloat16)
            for x in range(2):
                for y in range(2):
                    quads[c, x, y] = lax.dot_general(
                        oper_ref[pl.ds(x * piece, piece), :], phi_ref[pl.ds(y * piece, piece), :], NT,
                        preferred_element_type=jnp.float32)
        for x in range(2):
            for y in range(2):
                q0, q1, q2 = (quads[c, x, y] for c in range(3))
                third = piece // 3
                there = (y ^ flip_ref[0], x ^ flip_ref[1])
                marks = jnp.concatenate(
                    [marks_ref[x], marks_ref[y], jnp.zeros((third - 16, third), jnp.float32)], axis=0)
                parts = [q2[b * third : (b + 1) * third, 2 * third :] for b in range(3)] + [marks]
                blocks = [
                    jnp.concatenate([q0, q2[:, :third]], axis=1),
                    jnp.concatenate([q1, q2[:, third : 2 * third]], axis=1),
                    jnp.concatenate(parts, axis=1),
                ]
                out_ref[there[0], there[1]] = jnp.concatenate(blocks, axis=0).astype(jnp.bfloat16)


def field_call(first, count, atoms, pos, blocks, pts, scale, tables, acc, phi=None, w=None, marks=None, flip=None):
    points = pts.shape[1]
    last = phi is not None
    args = [atoms, pos, blocks, pts, scale, tables, acc]
    scratch = [pltpu.VMEM((points // LANES, count, LANES), jnp.float32)] + [pltpu.VMEM((points // LANES, DEG * count, LANES), jnp.float32)] * 2
    if last:
        args += [phi, w, marks, flip]
        third = phi.shape[0] // 6
        out = jax.ShapeDtypeStruct((2, 2, 7 * third, LANES), jnp.bfloat16)
        scratch += [pltpu.VMEM((24, points), jnp.float32), pltpu.VMEM(phi.shape, jnp.bfloat16)]
    else:
        out = jax.ShapeDtypeStruct((24, points), jnp.float32)
    cost = count * points
    return pl.pallas_call(
        functools.partial(field_kernel, first, count, last),
        out_shape=out,
        in_specs=[SMEM] * 3 + [VMEM] * (len(args) - 3 - last) + [SMEM] * last,
        out_specs=VMEM,
        scratch_shapes=scratch,
        cost_estimate=pl.CostEstimate(flops=cost * 3 * S * S * 2, bytes_accessed=cost * 8, transcendentals=cost * S),
        name="field",
    )(*args)


def place_kernel(pieces, carried, final, piece, tile, *refs):
    stacks, refs = refs[:pieces], refs[pieces:]
    if carried:
        acc_in, refs = refs[0], refs[1:]
    out_ref, rows_ref, wide_ref = refs
    third = piece // 3
    group = 4
    total = rows_ref.shape[1] // piece
    lane = lax.broadcasted_iota(jnp.int32, (piece, LANES), 1)
    sub = lax.broadcasted_iota(jnp.int32, (tile, LANES), 0)
    per = total // pieces
    for first in range(0, total, group):
        strips = []
        for g in range(first, first + group):
            ref, at = stacks[g // per], g % per
            tail = ref[at, pl.ds(2 * piece, third), :].astype(jnp.float32)
            marks = tail[: third // 2, 3 * third :]
            row_mark = marks[0:3] * 32.0 + marks[3:6]
            col_mark = marks[8:11] * 32.0 + marks[11:14]
            strips += [row_mark[b : b + 1] for b in range(3)]
            flat = jnp.concatenate([col_mark[b : b + 1] for b in range(3)] + [col_mark[0:1]], axis=1)
            column = jnp.transpose(jnp.broadcast_to(flat, (LANES, LANES)))[:piece].astype(jnp.int32)
            hits = jnp.concatenate(
                [(column == lane + u).astype(jnp.float32).astype(jnp.bfloat16) for u in range(0, tile, LANES)], axis=1)
            upper = ref[at, pl.ds(0, piece), :].astype(jnp.float32)
            lower = ref[at, pl.ds(piece, piece), :].astype(jnp.float32)
            rest = jnp.concatenate([tail[:, b * third : (b + 1) * third] for b in range(3)], axis=0)
            third_part = jnp.concatenate([upper[:, piece:], lower[:, piece:], rest], axis=1)
            quads = jnp.concatenate([upper[:, :piece], lower[:, :piece], third_part], axis=0).astype(jnp.bfloat16)
            spread = jnp.dot(quads, hits, preferred_element_type=jnp.float32).astype(jnp.bfloat16)
            for c in range(3):
                wide_ref[c, pl.ds(g * piece, piece), :] = spread[c * piece : (c + 1) * piece]
        strip = jnp.concatenate(strips, axis=1).astype(jnp.int32)
        for start in range(0, group * piece, LANES):
            rows_ref[:, pl.ds(first * piece + start, LANES)] = (
                sub == strip[:, start : start + LANES]).astype(jnp.float32).astype(jnp.bfloat16)

    step = 256
    def body(i, carry):
        c, t = i // (tile // step), (i % (tile // step)) * step
        here = pl.ds(pl.multiple_of(t, step), step)
        value = jnp.dot(rows_ref[here, :], wide_ref[c], preferred_element_type=jnp.float32)
        if carried:
            value += acc_in[c, here, :]
        out_ref[c, here, :] = value.astype(out_ref.dtype)
        return carry
    lax.fori_loop(0, 3 * (tile // step), body, 0)

def place_call(stacks, piece, tile, acc=None, final=True):
    total = sum(s.shape[0] for s in stacks)
    depth = total * piece
    args = list(stacks) + ([acc] if acc is not None else [])
    return pl.pallas_call(
        functools.partial(place_kernel, len(stacks), acc is not None, final, piece, tile),
        out_shape=jax.ShapeDtypeStruct((3, tile, tile), jnp.bfloat16 if final else jnp.float32),
        in_specs=[VMEM] * len(args), out_specs=VMEM,
        scratch_shapes=[pltpu.VMEM((tile, depth), jnp.bfloat16), pltpu.VMEM((3, depth, tile), jnp.bfloat16)],
        compiler_params=pltpu.CompilerParams(vmem_limit_bytes=60 << 20),
        cost_estimate=pl.CostEstimate(flops=2 * 3 * depth * tile * tile, bytes_accessed=12 * tile * tile, transcendentals=0),
        name="place",
    )(*args)


def apply_green(charges, kernels):
    shaped = charges.astype(jnp.bfloat16).reshape(-1, 3, S, DEG, DEG)
    kernel_rows = kernels.reshape(-1, DEG, S, S)
    result = jnp.einsum(
        "xast,xctam->xcsam", kernel_rows, shaped, preferred_element_type=jnp.float32
    )
    return result.astype(jnp.bfloat16).reshape(-1, 3 * S * DEG * DEG)


def swap(value, axis, mask=1):
    size = lax.axis_size(axis)
    return lax.ppermute(value, axis, [(i, i ^ mask) for i in range(size)])


def plane_atoms(owners, row, col):
    flips = jnp.arange(4)
    inner = ((flips & 1) ^ row) * 2 + ((flips >> 1) ^ col)
    return (jnp.arange(owners)[None, :] * 4 + inner[:, None]).reshape(-1)


def on_device(
    basis_values,
    density_matrix,
    points,
    weights,
    intersection,
    basis_index,
    atom_positions,
    shell_blocks,
    shell_widths,
    green,
):
    phi = basis_values[0]
    dens = density_matrix[0]
    spots = points[0]
    atoms = intersection[0]
    labels = basis_index[0]
    owners = lax.axis_size("batch")
    parts = lax.axis_size("row")
    sides = lax.axis_size("col")
    row, col = lax.axis_index("row"), lax.axis_index("col")
    count = atoms.shape[0]
    slots = (count + owners - 1) // owners
    holding = green.shape[0]
    every_atom = atom_positions.shape[1]
    width = 3 * S * DEG * DEG
    lines = width // LANES
    highest = lax.Precision.HIGHEST
    dense = count == every_atom and holding == parts * sides
    if dense:
        atoms = plane_atoms(owners, row, col)
    group = count // 4
    ordered = jnp.concatenate([shell_widths[0::2], shell_widths[1::2]])
    scale = jnp.broadcast_to((-LOG2E / (ordered * ordered))[:, None], (S, LANES))
    shared = (atoms, atom_positions, shell_blocks, spots, scale)

    def moments_of(place, weighted):
        return moments_call(place * group, group, *shared, wd=weighted)[0]

    third, weighted = moments_call(
        3 * group, group, *shared, phi=phi, dens=dens, w=weights
    )
    if dense:
        from_third = swap(third, "col")
        first = moments_of(1, weighted) + from_third
        from_first = swap(first, "row")
        from_second = swap(moments_of(2, weighted), "col")
        held = (
            moments_of(0, weighted).astype(jnp.float32)
            + from_second.astype(jnp.float32)
            + from_first.astype(jnp.float32)
        ).astype(jnp.bfloat16)
        shares = lax.all_to_all(held, "batch", split_axis=0, concat_axis=0, tiled=True)
        charges = jnp.sum(shares.astype(jnp.float32), axis=0)
        kernels = lax.dynamic_index_in_dim(green, row * sides + col, 0, keepdims=True)
        mine = apply_green(charges.reshape(1, width), kernels).reshape(1, lines, LANES)
        own = lax.all_to_all(
            jnp.broadcast_to(mine, (owners, lines, LANES)),
            "batch",
            split_axis=0,
            concat_axis=0,
            tiled=True,
        )
        beside = swap(own, "row")
        tables = [own, beside, swap(own, "col"), swap(beside, "col")]
        here = lax.axis_index("batch")
        plane = jnp.stack(
            [lax.dynamic_index_in_dim(table, here, 0, keepdims=False) for table in tables]
        )
        places = [(j // sides ^ row) + 2 * (j % sides ^ col) for j in range(holding)]
        potential = jnp.concatenate(
            [lax.dynamic_index_in_dim(plane, place, 0) for place in places]
        ).reshape(holding, width)
    else:
        moments = jnp.concatenate([moments_of(place, weighted) for place in range(3)] + [third])
        moments = moments.astype(jnp.float32).reshape(count, width)
        home = atoms // holding
        local_slot = atoms % holding
        order = jnp.arange(count)
        before = (home[None, :] == home[:, None]) & (order[None, :] < order[:, None])
        place = home * slots + jnp.sum(before, axis=1)
        routing = jnp.arange(owners * slots)[:, None] == place[None, :]
        outgoing = jnp.dot(routing.astype(jnp.float32), moments, precision=highest).reshape(
            owners, slots, width
        )
        tags = (jnp.sum(jnp.where(routing, local_slot[None, :] + 1, 0), axis=1) - 1).reshape(
            owners, slots
        )
        incoming, sources = (
            lax.all_to_all(outgoing, "batch", split_axis=0, concat_axis=0, tiled=True),
            lax.all_to_all(tags, "batch", split_axis=0, concat_axis=0, tiled=True),
        )
        collect = jnp.arange(holding)[:, None] == sources.reshape(1, owners * slots)
        partial_value = jnp.dot(
            collect.astype(jnp.float32), incoming.reshape(owners * slots, width), precision=highest
        )
        totals = lax.psum(partial_value, ("row", "col"))
        potential = apply_green(totals, green)
        back = jnp.dot(
            collect.T.astype(jnp.bfloat16), potential, preferred_element_type=jnp.float32
        ).astype(jnp.bfloat16)
        returned = lax.all_to_all(
            back.reshape(owners, slots, width), "batch", split_axis=0, concat_axis=0, tiled=True
        )
        table = jnp.dot(
            routing.T.astype(jnp.bfloat16),
            returned.reshape(owners * slots, width),
            preferred_element_type=jnp.float32,
        )
        table = table.astype(jnp.bfloat16).reshape(count, lines, LANES)
        tables = [table[place * group : (place + 1) * group] for place in range(4)]
    piece = labels.shape[0] // parts
    tile = NB // parts
    inner = labels.reshape(parts, 3, piece // 3) - jnp.arange(parts)[:, None, None] * tile
    marks = jnp.concatenate([inner // 32, inner % 32, inner[:, :2] * 0], axis=1)
    marks = marks.astype(jnp.float32)
    field = jnp.zeros((24, spots.shape[1]), jnp.float32)
    for place in (0, 2, 1):
        field = field_call(place * group, group, *shared, tables[place], field)
    flip = jnp.stack([col, row])
    load = field_call(
        3 * group, group, *shared, tables[3], field, phi=phi, w=weights, marks=marks, flip=flip
    )
    fresh = swap(load[1], "col")
    got = swap(jnp.stack([load[0, 1], fresh[1]]), "row")
    plane_load = jnp.concatenate([load[0, :1], fresh[:1], got], axis=0)
    if owners <= 8:
        near = [plane_load] + [swap(plane_load, "batch", m) for m in range(2, owners, 2)]
        far = [swap(line, "batch") for line in near]
        total = place_call(near, piece, tile, final=False)
        hamiltonian = place_call(far, piece, tile, acc=total)
    else:
        everyone = lax.all_gather(plane_load, "batch", axis=0)
        chunk = 4
        everyone = everyone.reshape((owners // chunk, chunk * 4) + plane_load.shape[1:])

        def add(total, item):
            return place_call([item], piece, tile, acc=total, final=False), None

        total, _ = lax.scan(add, jnp.zeros((3, tile, tile), jnp.float32), everyone)
        hamiltonian = total.astype(jnp.bfloat16)
    return (potential, hamiltonian)


def solution(mesh):
    return jax.shard_map(
        on_device,
        mesh=mesh,
        in_specs=(
            P(("batch", "row", "col"), None, None),
            P(("batch", "row", "col"), None, None, None),
            P(("batch", "row", "col"), None, None),
            P(("batch", "row", "col"), None),
            P(("batch", "row", "col"), None),
            P(("batch", "row", "col"), None),
            P(),
            P(),
            P(),
            P("batch", None, None),
        ),
        out_specs=(P("batch", None), P(None, "row", "col")),
        check_vma=False,
    )
```

time: 175 us -> 154 us (0.88)
  Pallas kernels: 0 us -> 74.3 us
  matrix products: 44.9 us -> 0.26 us
  local copies, waits for them, and re-layouts: 39.5 us -> 16 us
  other arithmetic: 17.5 us -> 5.68 us
  waiting for transfers between devices: 41 us -> 31.9 us
  starting transfers between devices: 29.2 us -> 24 us
    pallas_call x0 -> x10, Pallas kernels: none -> 74.3 us  [the longest x2 29.9 us: place_call(): pl.pallas_call(functools.partial(place_kernel, len(stacks), acc is not No...]
    dot_general x13 -> x0, matrix products: 44.7 us -> none  [the longest x1 16 us: place_quads(): jnp.einsum('tk,cku->ctu', rows_hit, wide.reshape(parts, count * piece, ti...]
    ppermute x19 -> x15, waiting for transfers between devices: 41 us -> 17.5 us  [swap(): return lax.ppermute(value, axis, [(i, i ^ mask) for i in range(size)])]
    ppermute x19 -> x15, starting transfers between devices: 29.2 us -> 14.6 us  [swap(): return lax.ppermute(value, axis, [(i, i ^ mask) for i in range(size)])]
    all_to_all x0 -> x2, waiting for transfers between devices: none -> 14.4 us  [the longest x1 7.62 us: on_device(): lax.all_to_all(held, 'batch', split_axis=0, concat_axis=0, tiled=True)]
    unnamed x35 -> x2, other arithmetic: 11.6 us -> 1.36 us
    all_to_all x0 -> x2, starting transfers between devices: none -> 9.37 us  [the longest x1 5.8 us: on_device(): lax.all_to_all(held, 'batch', split_axis=0, concat_axis=0, tiled=True)]
    reshape x5 -> x0, local copies, waits for them, and re-layouts: 6.84 us -> none  [the longest x1 3.42 us: place_quads(): blocks = stack[:, :body].reshape(count, parts, piece, piece)]
  transfers between devices with their start and end apart: 19 -> 17, of which waited for: 13 -> 6; matrix products, arithmetic and copies ran while one was open for 13% -> 6% of each run, Pallas kernels for 0% -> 30%
where the time goes in v2:
time: 154 us; the launch traced here: 153 us
  Pallas kernels  74.3 us (48%)
  waiting for transfers between devices  31.9 us (21%)
  starting transfers between devices  24 us (16%)
  local copies, waits for them, and re-layouts  16 us (10%)
  other arithmetic  5.68 us (4%)
    pallas_call x2, Pallas kernels, place_call(): pl.pallas_call(functools.partial(place_kernel, len(stacks), acc is not No...  29.9 us
    pallas_call x4, Pallas kernels, moments_call(): pl.pallas_call(functools.partial(moments_kernel, first, count, chunk, fre...  22.5 us
    pallas_call x4, Pallas kernels, field_call(): pl.pallas_call(functools.partial(field_kernel, first, count, last), out_s...  21.9 us
    ppermute x15, waiting for transfers between devices, swap(): return lax.ppermute(value, axis, [(i, i ^ mask) for i in range(size)])  17.5 us
    ppermute x15, starting transfers between devices, swap(): return lax.ppermute(value, axis, [(i, i ^ mask) for i in range(size)])  14.6 us
    all_to_all x1, waiting for transfers between devices, on_device(): lax.all_to_all(held, 'batch', split_axis=0, concat_axis=0, tiled=True)  7.62 us
    all_to_all x1, waiting for transfers between devices, on_device(): lax.all_to_all(jnp.broadcast_to(mine, (owners, lines, LANES)), 'batch', s...  6.8 us
    all_to_all x1, starting transfers between devices, on_device(): lax.all_to_all(held, 'batch', split_axis=0, concat_axis=0, tiled=True)  5.8 us
  transfers between devices with their start and end apart: 17, of which 6 were waited for; matrix products, arithmetic and copies ran while one was open for 6% of the time, Pallas kernels for 30%

profile of v2, /device:TPU:0, one launch (start us, length us, event | category | flops | bytes accessed | tf_op | source)
XLA Modules:
  0.0 152.9 jit_solution(13315231523502751225)
XLA Ops:
  2.9 1.4 copy.21
  5.1 6.5 %moments.4 = (bf16[8,96,128]{2,1,0:T(8,128)(2,1)}, f32[3,2048]{1,0:T(4,128)}) custom-call(s32[32]{0:T(128)} %add.83.refs_0_, f32[3,32]{1,0:T(4,128)} %refs_1_.15, s32[32]{0:T(128)} %refs_2_.15, f32[3,2048]{1,0:T(4,128)} %bitcast.28, f32[64,128]{1,0:T(8,128)} %broadcast_in_dim.8.refs_4_, bf16[192,2048]{1,0:T(8,128)(2,1)} %bitcast.36, ...), custom_call_target="tpu_custom_call" | custom-call | flops 402653184 | bytes 131072 | tf_op jit(solution)/shard_map/moments/pallas_call | solution.py:118
  12.1 5.3 %moments.6 = bf16[8,96,128]{2,1,0:T(8,128)(2,1)} custom-call(s32[32]{0:T(128)} %add.83.refs_0_, f32[3,32]{1,0:T(4,128)} %refs_1_.15, s32[32]{0:T(128)} %refs_2_.15, f32[3,2048]{1,0:T(4,128)} %bitcast.29, f32[64,128]{1,0:T(8,128)} %broadcast_in_dim.8.refs_4_, f32[3,2048]{1,0:T(4,128)} %get-tuple-element.4.refs_5_), custom_call_target="tpu_custom_call" | custom-call | flops 402653184 | bytes 131072 | tf_op jit(solution)/shard_map/moments/pallas_call | solution.py:118
  17.5 5.3 %moments.7 = bf16[8,96,128]{2,1,0:T(8,128)(2,1)} custom-call(s32[32]{0:T(128)} %add.83.refs_0_, f32[3,32]{1,0:T(4,128)} %refs_1_.15, s32[32]{0:T(128)} %refs_2_.15, f32[3,2048]{1,0:T(4,128)} %bitcast.30, f32[64,128]{1,0:T(8,128)} %broadcast_in_dim.8.refs_4_, f32[3,2048]{1,0:T(4,128)} %get-tuple-element.4.refs_5_), custom_call_target="tpu_custom_call" | custom-call | flops 402653184 | bytes 131072 | tf_op jit(solution)/shard_map/moments/pallas_call | solution.py:118
  23.8 3.1 %collective-permute-start.2 = (bf16[8,96,128]{2,1,0:T(8,128)(2,1)S(1)}, bf16[8,96,128]{2,1,0:T(8,128)(2,1)S(1)}, u32[]{:S(2)}, u32[]{:S(2)}) collective-permute-start(bf16[8,96,128]{2,1,0:T(8,128)(2,1)S(1)} %add.85), channel_id=1, source_target_pairs={{0,2},{2,0},{1,3},{3,1},{4,6},{6,4},{5,7},{7,5},{8,10},{10,8},{9,1... | collective-permute-start | bytes 589832 | tf_op jit(solution)/shard_map/ppermute | solution.py:289
  27.5 1.3 reduce.4
  28.9 5.3 %moments.5 = bf16[8,96,128]{2,1,0:T(8,128)(2,1)} custom-call(s32[32]{0:T(128)} %add.83.refs_0_, f32[3,32]{1,0:T(4,128)} %refs_1_.15, s32[32]{0:T(128)} %refs_2_.15, f32[3,2048]{1,0:T(4,128)} %bitcast.31, f32[64,128]{1,0:T(8,128)} %broadcast_in_dim.8.refs_4_, f32[3,2048]{1,0:T(4,128)} %get-tuple-element.4.refs_5_), custom_call_target="tpu_custom_call" | custom-call | flops 402653184 | bytes 131072 | tf_op jit(solution)/shard_map/moments/pallas_call | solution.py:118
  34.2 1.7 %add_convert_fusion = bf16[8,96,128]{2,1,0:T(8,128)(2,1)} fusion(bf16[8,96,128]{2,1,0:T(8,128)(2,1)S(1)} %collective-permute-done.2, bf16[8,96,128]{2,1,0:T(8,128)(2,1)S(1)} %collective-permute-done, bf16[8,96,128]{2,1,0:T(8,128)(2,1)} %moments.5), kind=kLoop, calls=%fused_computation.3 | loop fusion | flops 589824 | bytes 786432 | tf_op jit(solution)/shard_map/convert_element_type | solution.py:349
  35.9 5.8 %all-to-all-start = ((bf16[8,96,128]{2,1,0:T(8,128)(2,1)}), bf16[8,96,128]{2,1,0:T(8,128)(2,1)S(1)}, u32[]{:S(2)}, u32[]{:S(2)}) async-start(bf16[8,96,128]{2,1,0:T(8,128)(2,1)} %add_convert_fusion), calls=%async_computation | async-start | bytes 393216 | tf_op jit(solution)/shard_map/all_to_all | solution.py:350
  41.9 7.6 %all-to-all-done = bf16[8,96,128]{2,1,0:T(8,128)(2,1)S(1)} async-done(((bf16[8,96,128]{2,1,0:T(8,128)(2,1)}), bf16[8,96,128]{2,1,0:T(8,128)(2,1)S(1)}, u32[]{:S(2)}, u32[]{:S(2)}) %all-to-all-start) | async-done | bytes 196640 | tf_op jit(solution)/shard_map/all_to_all | solution.py:350
  51.7 3.6 %all-to-all-start.1 = ((bf16[8,96,128]{2,1,0:T(8,128)(2,1)}), bf16[8,96,128]{2,1,0:T(8,128)(2,1)S(1)}, u32[]{:S(2)}, u32[]{:S(2)}) async-start(bf16[8,96,128]{2,1,0:T(8,128)(2,1)} %broadcast_in_dim.10), calls=%async_computation.1 | async-start | bytes 393216 | tf_op jit(solution)/shard_map/all_to_all | solution.py:354
  56.0 6.8 %all-to-all-done.1.refs_5_ = bf16[8,96,128]{2,1,0:T(8,128)(2,1)S(1)} async-done(((bf16[8,96,128]{2,1,0:T(8,128)(2,1)}), bf16[8,96,128]{2,1,0:T(8,128)(2,1)S(1)}, u32[]{:S(2)}, u32[]{:S(2)}) %all-to-all-start.1) | async-done | bytes 196640 | tf_op jit(solution)/shard_map/all_to_all | solution.py:354
  64.7 5.0 %field.4.refs_6_ = f32[24,2048]{1,0:T(8,128)} custom-call(s32[32]{0:T(128)} %add.83.refs_0_, f32[3,32]{1,0:T(4,128)} %refs_1_.15, s32[32]{0:T(128)} %refs_2_.15, f32[3,2048]{1,0:T(4,128)} %bitcast.32, f32[64,128]{1,0:T(8,128)} %broadcast_in_dim.8.refs_4_, bf16[8,96,128]{2,1,0:T(8,128)(2,1)} %copy-done.1, f32[24,2048]{1,0:T(8,128)} %broadcast_in_dim.22.refs_6_), custom_call_target="tpu_custom_call" | custom-call | flops 402653184 | bytes 131072 | tf_op jit(solution)/shard_map/field/pallas_call | solution.py:204
  71.3 5.0 %field.5.refs_6_ = f32[24,2048]{1,0:T(8,128)} custom-call(s32[32]{0:T(128)} %add.83.refs_0_, f32[3,32]{1,0:T(4,128)} %refs_1_.15, s32[32]{0:T(128)} %refs_2_.15, f32[3,2048]{1,0:T(4,128)} %bitcast.33, f32[64,128]{1,0:T(8,128)} %broadcast_in_dim.8.refs_4_, bf16[8,96,128]{2,1,0:T(8,128)(2,1)} %copy-done.3, f32[24,2048]{1,0:T(8,128)} %field.4.refs_6_), custom_call_target="tpu_custom_call" | custom-call | flops 402653184 | bytes 131072 | tf_op jit(solution)/shard_map/field/pallas_call | solution.py:204
  76.4 5.0 %field.6.refs_6_ = f32[24,2048]{1,0:T(8,128)} custom-call(s32[32]{0:T(128)} %add.83.refs_0_, f32[3,32]{1,0:T(4,128)} %refs_1_.15, s32[32]{0:T(128)} %refs_2_.15, f32[3,2048]{1,0:T(4,128)} %bitcast.34, f32[64,128]{1,0:T(8,128)} %broadcast_in_dim.8.refs_4_, bf16[8,96,128]{2,1,0:T(8,128)(2,1)} %copy-done.4, f32[24,2048]{1,0:T(8,128)} %field.5.refs_6_), custom_call_target="tpu_custom_call" | custom-call | flops 402653184 | bytes 131072 | tf_op jit(solution)/shard_map/field/pallas_call | solution.py:204
  83.5 6.8 %field.7 = bf16[2,2,224,128]{3,2,1,0:T(8,128)(2,1)} custom-call(s32[32]{0:T(128)} %add.83.refs_0_, f32[3,32]{1,0:T(4,128)} %refs_1_.15, s32[32]{0:T(128)} %refs_2_.15, f32[3,2048]{1,0:T(4,128)} %bitcast.35, f32[64,128]{1,0:T(8,128)} %broadcast_in_dim.8.refs_4_, bf16[8,96,128]{2,1,0:T(8,128)(2,1)} %copy-done.5, f32[24,2048]{1,0:T(8,128)} %field.6.refs_6_, ...), custom_call_target="tpu_custom_call" | custom-call | flops 402653184 | bytes 131072 | tf_op jit(solution)/shard_map/field/pallas_call | solution.py:204
  92.6 1.6 %collective-permute-start.7 = (bf16[2,224,128]{2,1,0:T(8,128)(2,1)S(1)}, bf16[2,224,128]{2,1,0:T(8,128)(2,1)S(1)}, u32[]{:S(2)}, u32[]{:S(2)}) collective-permute-start(bf16[2,224,128]{2,1,0:T(8,128)(2,1)S(1)} %pad_maximum_fusion.1), channel_id=1, source_target_pairs={{0,2},{2,0},{1,3},{3,1},{4,6},{6,4},{5,7},{7,5},{8,10},{10,8},{9,1... | collective-permute-start | bytes 344072 | tf_op jit(solution)/shard_map/ppermute | solution.py:289
  95.0 3.1 %collective-permute-done.7 = bf16[2,224,128]{2,1,0:T(8,128)(2,1)S(1)} collective-permute-done((bf16[2,224,128]{2,1,0:T(8,128)(2,1)S(1)}, bf16[2,224,128]{2,1,0:T(8,128)(2,1)S(1)}, u32[]{:S(2)}, u32[]{:S(2)}) %collective-permute-start.7) | collective-permute-done | bytes 114720 | tf_op jit(solution)/shard_map/ppermute | solution.py:289
  99.8 2.8 %collective-permute-start.9 = (bf16[4,224,128]{2,1,0:T(8,128)(2,1)S(1)}, bf16[4,224,128]{2,1,0:T(8,128)(2,1)S(1)}, u32[]{:S(2)}, u32[]{:S(2)}) collective-permute-start(bf16[4,224,128]{2,1,0:T(8,128)(2,1)S(1)} %pad_maximum_fusion.refs_0_), channel_id=1, source_target_pairs={{0,8},{4,12},{8,0},{12,4},{16,24},{20,28},{24,16},{28,20},{1,9},{5... | collective-permute-start | bytes 688136 | tf_op jit(solution)/shard_map/ppermute | solution.py:289
  104.2 4.3 %collective-permute-done.13.refs_3_ = bf16[4,224,128]{2,1,0:T(8,128)(2,1)S(1)} collective-permute-done((bf16[4,224,128]{2,1,0:T(8,128)(2,1)S(1)}, bf16[4,224,128]{2,1,0:T(8,128)(2,1)S(1)}, u32[]{:S(2)}, u32[]{:S(2)}) %collective-permute-start.13) | collective-permute-done | bytes 229408 | tf_op jit(solution)/shard_map/ppermute | solution.py:289
  109.5 9.9 %collective-permute-done.11.refs_2_ = bf16[4,224,128]{2,1,0:T(8,128)(2,1)S(1)} collective-permute-done((bf16[4,224,128]{2,1,0:T(8,128)(2,1)S(1)}, bf16[4,224,128]{2,1,0:T(8,128)(2,1)S(1)}, u32[]{:S(2)}, u32[]{:S(2)}) %collective-permute-start.11) | collective-permute-done | bytes 229408 | tf_op jit(solution)/shard_map/ppermute | solution.py:289
  119.4 1.2 collective-permute-start.12
  121.5 14.4 %place.2.refs_4_ = f32[3,768,768]{2,1,0:T(8,128)} custom-call(bf16[4,224,128]{2,1,0:T(8,128)(2,1)} %copy-done.2, bf16[4,224,128]{2,1,0:T(8,128)(2,1)} %copy-done.8, bf16[4,224,128]{2,1,0:T(8,128)(2,1)} %copy-done.7, bf16[4,224,128]{2,1,0:T(8,128)(2,1)} %copy-done.6), custom_call_target="tpu_custom_call" | custom-call | flops 5435817984 | bytes 7077888 | tf_op jit(solution)/shard_map/place/pallas_call | solution.py:267
  137.4 15.5 %place.3 = bf16[3,768,768]{2,1,0:T(8,128)(2,1)} custom-call(bf16[4,224,128]{2,1,0:T(8,128)(2,1)} %copy-done.9, bf16[4,224,128]{2,1,0:T(8,128)(2,1)} %copy-done.12, bf16[4,224,128]{2,1,0:T(8,128)(2,1)} %copy-done.11, bf16[4,224,128]{2,1,0:T(8,128)(2,1)} %copy-done.10, f32[3,768,768]{2,1,0:T(8,128)} %place.2.refs_4_), custom_call_target="tpu_custom_call" | custom-call | flops 5435817984 | bytes 7077888 | tf_op jit(solution)/shard_map/place/pallas_call | solution.py:267
  (88 shorter events, 23.7 us)
Async XLA Ops:
  0.6 41.1 %copy-start = (bf16[4,8,4096]{2,1,0:T(8,128)(2,1)S(1)}, bf16[4,8,4096]{2,1,0:T(8,128)(2,1)}, u32[]{:S(2)}) copy-start(bf16[4,8,4096]{2,1,0:T(8,128)(2,1)} %param.18) | copy-start | bytes 786436
  11.6 11.2 %collective-permute-start.1 = (bf16[8,96,128]{2,1,0:T(8,128)(2,1)}, bf16[8,96,128]{2,1,0:T(8,128)(2,1)S(1)}, u32[]{:S(2)}, u32[]{:S(2)}) collective-permute-start(bf16[8,96,128]{2,1,0:T(8,128)(2,1)} %get-tuple-element.5), channel_id=1, source_target_pairs={{0,1},{1,0},{2,3},{3,2},{4,5},{5,4},{6,7},{7,6},{8,9},{9,8},{10,11... | collective-permute-start | bytes 589832 | tf_op jit(solution)/shard_map/ppermute | solution.py:289
  17.5 16.8 %collective-permute-start = (bf16[8,96,128]{2,1,0:T(8,128)(2,1)}, bf16[8,96,128]{2,1,0:T(8,128)(2,1)S(1)}, u32[]{:S(2)}, u32[]{:S(2)}) collective-permute-start(bf16[8,96,128]{2,1,0:T(8,128)(2,1)} %moments.6), channel_id=1, source_target_pairs={{0,1},{1,0},{2,3},{3,2},{4,5},{5,4},{6,7},{7,6},{8,9},{9,8},{10,11... | collective-permute-start | bytes 589832 | tf_op jit(solution)/shard_map/ppermute | solution.py:289
  23.8 10.4 %collective-permute-start.2 = (bf16[8,96,128]{2,1,0:T(8,128)(2,1)S(1)}, bf16[8,96,128]{2,1,0:T(8,128)(2,1)S(1)}, u32[]{:S(2)}, u32[]{:S(2)}) collective-permute-start(bf16[8,96,128]{2,1,0:T(8,128)(2,1)S(1)} %add.85), channel_id=1, source_target_pairs={{0,2},{2,0},{1,3},{3,1},{4,6},{6,4},{5,7},{7,5},{8,10},{10,8},{9,1... | collective-permute-start | bytes 589832 | tf_op jit(solution)/shard_map/ppermute | solution.py:289
  35.9 13.6 %all-to-all-start = ((bf16[8,96,128]{2,1,0:T(8,128)(2,1)}), bf16[8,96,128]{2,1,0:T(8,128)(2,1)S(1)}, u32[]{:S(2)}, u32[]{:S(2)}) async-start(bf16[8,96,128]{2,1,0:T(8,128)(2,1)} %add_convert_fusion), calls=%async_computation | async-start | bytes 393216 | tf_op jit(solution)/shard_map/all_to_all | solution.py:350
  51.7 11.1 %all-to-all-start.1 = ((bf16[8,96,128]{2,1,0:T(8,128)(2,1)}), bf16[8,96,128]{2,1,0:T(8,128)(2,1)S(1)}, u32[]{:S(2)}, u32[]{:S(2)}) async-start(bf16[8,96,128]{2,1,0:T(8,128)(2,1)} %broadcast_in_dim.10), calls=%async_computation.1 | async-start | bytes 393216 | tf_op jit(solution)/shard_map/all_to_all | solution.py:354
  62.8 1.9 %copy-start.1 = (bf16[8,96,128]{2,1,0:T(8,128)(2,1)}, bf16[8,96,128]{2,1,0:T(8,128)(2,1)S(1)}, u32[]{:S(2)}) copy-start(bf16[8,96,128]{2,1,0:T(8,128)(2,1)S(1)} %all-to-all-done.1.refs_5_) | copy-start | bytes 589828
  62.8 7.8 %collective-permute-start.4 = (bf16[8,96,128]{2,1,0:T(8,128)(2,1)S(1)}, bf16[8,96,128]{2,1,0:T(8,128)(2,1)S(1)}, u32[]{:S(2)}, u32[]{:S(2)}) collective-permute-start(bf16[8,96,128]{2,1,0:T(8,128)(2,1)S(1)} %all-to-all-done.1.refs_5_), channel_id=1, source_target_pairs={{0,1},{1,0},{2,3},{3,2},{4,5},{5,4},{6,7},{7,6},{8,9},{9,8},{10,11... | collective-permute-start | bytes 589832 | tf_op jit(solution)/shard_map/ppermute | solution.py:289
  62.8 7.6 %collective-permute-start.3 = (bf16[8,96,128]{2,1,0:T(8,128)(2,1)S(1)}, bf16[8,96,128]{2,1,0:T(8,128)(2,1)S(1)}, u32[]{:S(2)}, u32[]{:S(2)}) collective-permute-start(bf16[8,96,128]{2,1,0:T(8,128)(2,1)S(1)} %all-to-all-done.1.refs_5_), channel_id=1, source_target_pairs={{0,2},{2,0},{1,3},{3,1},{4,6},{6,4},{5,7},{7,5},{8,10},{10,8},{9,1... | collective-permute-start | bytes 589832 | tf_op jit(solution)/shard_map/ppermute | solution.py:289
  70.4 5.9 %copy-start.4 = (bf16[8,96,128]{2,1,0:T(8,128)(2,1)}, bf16[8,96,128]{2,1,0:T(8,128)(2,1)S(1)}, u32[]{:S(2)}) copy-start(bf16[8,96,128]{2,1,0:T(8,128)(2,1)S(1)} %collective-permute-done.3.refs_5_) | copy-start | bytes 589828
  70.4 12.4 %collective-permute-start.5 = (bf16[8,96,128]{2,1,0:T(8,128)(2,1)S(1)}, bf16[8,96,128]{2,1,0:T(8,128)(2,1)S(1)}, u32[]{:S(2)}, u32[]{:S(2)}) collective-permute-start(bf16[8,96,128]{2,1,0:T(8,128)(2,1)S(1)} %collective-permute-done.3.refs_5_), channel_id=1, source_target_pairs={{0,1},{1,0},{2,3},{3,2},{4,5},{5,4},{6,7},{7,6},{8,9},{9,8},{10,11... | collective-permute-start | bytes 589832 | tf_op jit(solution)/shard_map/ppermute | solution.py:289
  91.3 1.3 collective-permute-start.6
  92.6 5.4 %collective-permute-start.7 = (bf16[2,224,128]{2,1,0:T(8,128)(2,1)S(1)}, bf16[2,224,128]{2,1,0:T(8,128)(2,1)S(1)}, u32[]{:S(2)}, u32[]{:S(2)}) collective-permute-start(bf16[2,224,128]{2,1,0:T(8,128)(2,1)S(1)} %pad_maximum_fusion.1), channel_id=1, source_target_pairs={{0,2},{2,0},{1,3},{3,1},{4,6},{6,4},{5,7},{7,5},{8,10},{10,8},{9,1... | collective-permute-start | bytes 344072 | tf_op jit(solution)/shard_map/ppermute | solution.py:289
  98.0 23.4 %copy-start.2 = (bf16[4,224,128]{2,1,0:T(8,128)(2,1)}, bf16[4,224,128]{2,1,0:T(8,128)(2,1)S(1)}, u32[]{:S(2)}) copy-start(bf16[4,224,128]{2,1,0:T(8,128)(2,1)S(1)} %pad_maximum_fusion.refs_0_) | copy-start | bytes 688132
  98.1 10.4 %collective-permute-start.13 = (bf16[4,224,128]{2,1,0:T(8,128)(2,1)S(1)}, bf16[4,224,128]{2,1,0:T(8,128)(2,1)S(1)}, u32[]{:S(2)}, u32[]{:S(2)}) collective-permute-start(bf16[4,224,128]{2,1,0:T(8,128)(2,1)S(1)} %pad_maximum_fusion.refs_0_), channel_id=1, source_target_pairs={{0,24},{4,28},{8,16},{12,20},{16,8},{20,12},{24,0},{28,4},{1,25},{... | collective-permute-start | bytes 688136 | tf_op jit(solution)/shard_map/ppermute | solution.py:289
  98.9 20.5 %collective-permute-start.11 = (bf16[4,224,128]{2,1,0:T(8,128)(2,1)S(1)}, bf16[4,224,128]{2,1,0:T(8,128)(2,1)S(1)}, u32[]{:S(2)}, u32[]{:S(2)}) collective-permute-start(bf16[4,224,128]{2,1,0:T(8,128)(2,1)S(1)} %pad_maximum_fusion.refs_0_), channel_id=1, source_target_pairs={{0,16},{4,20},{8,24},{12,28},{16,0},{20,4},{24,8},{28,12},{1,17},{... | collective-permute-start | bytes 688136 | tf_op jit(solution)/shard_map/ppermute | solution.py:289
  99.8 20.9 %collective-permute-start.9 = (bf16[4,224,128]{2,1,0:T(8,128)(2,1)S(1)}, bf16[4,224,128]{2,1,0:T(8,128)(2,1)S(1)}, u32[]{:S(2)}, u32[]{:S(2)}) collective-permute-start(bf16[4,224,128]{2,1,0:T(8,128)(2,1)S(1)} %pad_maximum_fusion.refs_0_), channel_id=1, source_target_pairs={{0,8},{4,12},{8,0},{12,4},{16,24},{20,28},{24,16},{28,20},{1,9},{5... | collective-permute-start | bytes 688136 | tf_op jit(solution)/shard_map/ppermute | solution.py:289
  103.2 32.6 %collective-permute-start.8 = (bf16[4,224,128]{2,1,0:T(8,128)(2,1)S(1)}, bf16[4,224,128]{2,1,0:T(8,128)(2,1)S(1)}, u32[]{:S(2)}, u32[]{:S(2)}) collective-permute-start(bf16[4,224,128]{2,1,0:T(8,128)(2,1)S(1)} %pad_maximum_fusion.refs_0_), channel_id=1, source_target_pairs={{0,4},{4,0},{8,12},{12,8},{16,20},{20,16},{24,28},{28,24},{1,5},{5... | collective-permute-start | bytes 688136 | tf_op jit(solution)/shard_map/ppermute | solution.py:289
  108.5 13.0 %copy-start.6 = (bf16[4,224,128]{2,1,0:T(8,128)(2,1)}, bf16[4,224,128]{2,1,0:T(8,128)(2,1)S(1)}, u32[]{:S(2)}) copy-start(bf16[4,224,128]{2,1,0:T(8,128)(2,1)S(1)} %collective-permute-done.13.refs_3_) | copy-start | bytes 688132
  108.5 27.3 %collective-permute-start.14 = (bf16[4,224,128]{2,1,0:T(8,128)(2,1)S(1)}, bf16[4,224,128]{2,1,0:T(8,128)(2,1)S(1)}, u32[]{:S(2)}, u32[]{:S(2)}) collective-permute-start(bf16[4,224,128]{2,1,0:T(8,128)(2,1)S(1)} %collective-permute-done.13.refs_3_), channel_id=1, source_target_pairs={{0,4},{4,0},{8,12},{12,8},{16,20},{20,16},{24,28},{28,24},{1,5},{5... | collective-permute-start | bytes 688136 | tf_op jit(solution)/shard_map/ppermute | solution.py:289
  119.4 2.0 %copy-start.7 = (bf16[4,224,128]{2,1,0:T(8,128)(2,1)}, bf16[4,224,128]{2,1,0:T(8,128)(2,1)S(1)}, u32[]{:S(2)}) copy-start(bf16[4,224,128]{2,1,0:T(8,128)(2,1)S(1)} %collective-permute-done.11.refs_2_) | copy-start | bytes 688132
  119.4 16.4 %collective-permute-start.12 = (bf16[4,224,128]{2,1,0:T(8,128)(2,1)S(1)}, bf16[4,224,128]{2,1,0:T(8,128)(2,1)S(1)}, u32[]{:S(2)}, u32[]{:S(2)}) collective-permute-start(bf16[4,224,128]{2,1,0:T(8,128)(2,1)S(1)} %collective-permute-done.11.refs_2_), channel_id=1, source_target_pairs={{0,4},{4,0},{8,12},{12,8},{16,20},{20,16},{24,28},{28,24},{1,5},{5... | collective-permute-start | bytes 688136 | tf_op jit(solution)/shard_map/ppermute | solution.py:289
  120.6 15.2 %collective-permute-start.10 = (bf16[4,224,128]{2,1,0:T(8,128)(2,1)S(1)}, bf16[4,224,128]{2,1,0:T(8,128)(2,1)S(1)}, u32[]{:S(2)}, u32[]{:S(2)}) collective-permute-start(bf16[4,224,128]{2,1,0:T(8,128)(2,1)S(1)} %collective-permute-done.9.refs_1_), channel_id=1, source_target_pairs={{0,4},{4,0},{8,12},{12,8},{16,20},{20,16},{24,28},{28,24},{1,5},{5... | collective-permute-start | bytes 688136 | tf_op jit(solution)/shard_map/ppermute | solution.py:289
  135.9 0.9 copy-start.11
  (6 other events, 4.3 us)

commit v3 on v2

v3 whole, which is shorter than its diff:
```python
import functools

import jax
import jax.numpy as jnp
from jax import lax
from jax.experimental import pallas as pl
from jax.experimental.pallas import tpu as pltpu
from jax.sharding import PartitionSpec as P

S = 64
DEG = 8
NB = 1536
LANES = 128
FAR = 1.0e6
LOG2E = 1.4426950408889634
NT = (((1,), (1,)), ((), ()))
SMEM = pl.BlockSpec(memory_space=pltpu.SMEM)
VMEM = pl.BlockSpec(memory_space=pltpu.VMEM)


def prepare(first, count, atoms_ref, pos_ref, pts_ref, dist_ref, polar_ref, side_ref):
    rows = lax.broadcasted_iota(jnp.int32, (count, LANES), 0)
    centre = []
    for axis in range(3):
        column = jnp.zeros((count, LANES), jnp.float32)
        for k in range(count):
            column = jnp.where(rows == k, pos_ref[axis, atoms_ref[first + k]], column)
        centre.append(column)
    for t in range(pts_ref.shape[2] // LANES):
        here = pl.ds(t * LANES, LANES)
        delta = [pts_ref[0, pl.ds(axis, 1), here] - centre[axis] for axis in range(3)]
        square = delta[0] * delta[0] + delta[1] * delta[1] + delta[2] * delta[2] + 0.01
        inverse = lax.rsqrt(square)
        dist_ref[t] = square * inverse
        for ladder, u in ((polar_ref, delta[2] * inverse), (side_ref, delta[0] * inverse)):
            older, old = jnp.ones_like(u), u
            ladder[t, pl.ds(0, count), :] = older
            ladder[t, pl.ds(count, count), :] = old
            for order in range(2, DEG):
                older, old = old, 2.0 * u * old - older
                ladder[t, pl.ds(order * count, count), :] = old


def prepare_shells(widths_ref, scale_ref):
    rows = lax.broadcasted_iota(jnp.int32, (8, LANES), 0)
    for start in range(0, S, 8):
        column = jnp.zeros((8, LANES), jnp.float32)
        for j in range(8):
            place = start + j
            shell = 2 * place if place < S // 2 else 2 * place - (S - 1)
            column = jnp.where(rows == j, widths_ref[shell], column)
        scale_ref[pl.ds(start, 8), :] = -LOG2E / (column * column)


def shell_columns(blocks, live, scale_ref):
    half = live // 2
    place = lax.broadcasted_iota(jnp.int32, (live, LANES), 0)
    shell = jnp.where(place < half, 2 * place, 2 * place - (live - 1))
    middle = jnp.where(shell < 8 * blocks, shell.astype(jnp.float32) * (4.0 / S), FAR)
    scale = jnp.concatenate(
        [scale_ref[pl.ds(0, half), :], scale_ref[pl.ds(S // 2, half), :]], axis=0
    )
    return middle, scale


def angular_tile(k, count, t, polar_ref, side_ref):
    side = side_ref[t, pl.ds(k, DEG, stride=count), :]
    return jnp.concatenate(
        [
            polar_ref[t, pl.ds(order * count + k, DEG, stride=0), :] * side
            for order in range(DEG)
        ],
        axis=0,
    ).astype(jnp.bfloat16)


def radial_tile(k, t, middle, scale, dist_ref):
    dist = dist_ref[t, pl.ds(k, 8, stride=0), :]
    gap = jnp.concatenate([dist] * (middle.shape[0] // 8), axis=0) - middle
    return jnp.exp2(gap * (gap * scale))


def by_live(blocks, run):
    for live in range(16, S + 1, 16):

        @pl.when((blocks * 8 > live - 16) & (blocks * 8 <= live))
        def _(live=live):
            run(live)


def moments_kernel(first, count, fresh, *refs):
    if fresh:
        (
            atoms_ref, pos_ref, blocks_ref, widths_ref, pts_ref, phi_ref, dens_ref, w_ref,
            out_ref, wd_ref, dist_ref, polar_ref, side_ref, scale_ref,
        ) = refs
    else:
        (
            atoms_ref, pos_ref, blocks_ref, widths_ref, pts_ref, wd_ref,
            out_ref, dist_ref, polar_ref, side_ref, scale_ref,
        ) = refs
    points = pts_ref.shape[2]
    if fresh:
        for start in range(0, points, 256):
            here = pl.ds(start, 256)
            phi = phi_ref[0, :, here]
            wide = phi.astype(jnp.float32)
            for c in range(3):
                product = jnp.dot(dens_ref[0, c], phi, preferred_element_type=jnp.float32)
                density = jnp.sum(wide * product, axis=0, keepdims=True)
                wd_ref[pl.ds(c, 1), here] = w_ref[:, here] * density
    prepare(first, count, atoms_ref, pos_ref, pts_ref, dist_ref, polar_ref, side_ref)
    prepare_shells(widths_ref, scale_ref)

    def body(k, carry):
        blocks = blocks_ref[atoms_ref[first + k]]

        def run(live):
            middle, scale = shell_columns(blocks, live, scale_ref)
            total = jnp.zeros((3 * live, S), jnp.float32)
            for start in range(0, points, 256):
                scaled, angles = [[], [], []], []
                for inner in (start, start + LANES):
                    t = inner // LANES
                    radial = radial_tile(k, t, middle, scale, dist_ref).astype(jnp.bfloat16)
                    angles.append(angular_tile(k, count, t, polar_ref, side_ref))
                    for c in range(3):
                        row = jnp.broadcast_to(wd_ref[pl.ds(c, 1), pl.ds(inner, LANES)], (16, LANES))
                        row = jnp.concatenate([row.astype(jnp.bfloat16)] * (live // 16), axis=0)
                        scaled[c].append(radial * row)
                left = jnp.concatenate([jnp.concatenate(s, axis=1) for s in scaled], axis=0)
                right = jnp.concatenate(angles, axis=1)
                total += lax.dot_general(left, right, NT, preferred_element_type=jnp.float32)
            half = live // 2
            for c in range(3):
                even = total[c * live : c * live + half]
                odd = total[c * live + half : (c + 1) * live]
                block = jnp.concatenate([even, odd], axis=1)
                if live < S:
                    rest = jnp.zeros((S // 2 - half, LANES), jnp.float32)
                    block = jnp.concatenate([block, rest], axis=0)
                out_ref[k, pl.ds(c * (S // 2), S // 2), :] = block.astype(out_ref.dtype)

        by_live(blocks, run)
        return carry

    lax.fori_loop(0, count, body, 0)


def table_scratch(count, points):
    tiles = points // LANES
    return [
        pltpu.VMEM((tiles, count, LANES), jnp.float32),
        pltpu.VMEM((tiles, DEG * count, LANES), jnp.float32),
        pltpu.VMEM((tiles, DEG * count, LANES), jnp.float32),
        pltpu.VMEM((S, LANES), jnp.float32),
    ]


def table_cost(count, points):
    cells = count * points * S
    return pl.CostEstimate(flops=cells * 3 * S * 2, bytes_accessed=cells, transcendentals=cells)


def moments_call(first, count, shared, wd=None, phi=None, dens=None, w=None):
    points = shared[-1].shape[2]
    fresh = wd is None
    out = [jax.ShapeDtypeStruct((count, 3 * S // 2, LANES), jnp.bfloat16)]
    args = list(shared)
    if fresh:
        out.append(jax.ShapeDtypeStruct((3, points), jnp.float32))
        args += [phi, dens, w]
    else:
        args += [wd]
    return pl.pallas_call(
        functools.partial(moments_kernel, first, count, fresh),
        out_shape=out,
        in_specs=[SMEM] * 4 + [VMEM] * (len(args) - 4),
        out_specs=[VMEM] * len(out),
        scratch_shapes=table_scratch(count, points),
        cost_estimate=table_cost(count, points),
        name="moments",
    )(*args)


def field_kernel(first, count, carried, last, *refs):
    (atoms_ref, pos_ref, blocks_ref, widths_ref, pts_ref, tab_ref), refs = refs[:6], refs[6:]
    if carried:
        acc_in, refs = refs[0], refs[1:]
    if last:
        (
            phi_ref, w_ref, marks_ref, flip_ref,
            out_ref, dist_ref, polar_ref, side_ref, scale_ref, acc_ref, oper_ref,
        ) = refs
    else:
        acc_ref, dist_ref, polar_ref, side_ref, scale_ref = refs
    points = pts_ref.shape[2]
    prepare(first, count, atoms_ref, pos_ref, pts_ref, dist_ref, polar_ref, side_ref)
    prepare_shells(widths_ref, scale_ref)
    acc_ref[...] = acc_in[...] if carried else jnp.zeros_like(acc_ref)

    def body(k, carry):
        blocks = blocks_ref[atoms_ref[first + k]]

        def run(live):
            half = live // 2
            middle, scale = shell_columns(blocks, live, scale_ref)
            table = tab_ref[k].astype(jnp.float32)
            lines = []
            for c in range(3):
                block = table[c * (S // 2) : c * (S // 2) + half]
                lines += [block[:, :S], block[:, S:]]
            left = jnp.concatenate(lines, axis=0).astype(jnp.bfloat16)
            for start in range(0, points, 256):
                t = start // LANES
                right = jnp.concatenate(
                    [angular_tile(k, count, t + d, polar_ref, side_ref) for d in range(2)], axis=1
                )
                spread = jnp.dot(left, right, preferred_element_type=jnp.float32)
                for d in range(2):
                    here = pl.ds(start + d * LANES, LANES)
                    radial = radial_tile(k, t + d, middle, scale, dist_ref)
                    for c in range(3):
                        sums = acc_ref[pl.ds(8 * c, 8), here]
                        for r in range(0, live, 8):
                            at = c * live + r
                            sums += radial[r : r + 8] * spread[at : at + 8, d * LANES : (d + 1) * LANES]
                        acc_ref[pl.ds(8 * c, 8), here] = sums

        by_live(blocks, run)
        return carry

    lax.fori_loop(0, count, body, 0)
    if last:
        piece = phi_ref.shape[1] // 2
        third = piece // 3
        quads = {}
        for c in range(3):
            for start in range(0, points, 256):
                here = pl.ds(start, 256)
                total = jnp.sum(acc_ref[pl.ds(8 * c, 8), here], axis=0, keepdims=True)
                wide = phi_ref[0, :, here].astype(jnp.float32)
                oper_ref[:, here] = (wide * (w_ref[:, here] * total)).astype(jnp.bfloat16)
            for x in range(2):
                for y in range(2):
                    quads[c, x, y] = lax.dot_general(
                        oper_ref[pl.ds(x * piece, piece), :],
                        phi_ref[0, pl.ds(y * piece, piece), :],
                        NT,
                        preferred_element_type=jnp.float32,
                    )
        for x in range(2):
            for y in range(2):
                q0, q1, q2 = (quads[c, x, y] for c in range(3))
                marks = jnp.concatenate(
                    [marks_ref[x], marks_ref[y], jnp.zeros((third - 16, third), jnp.float32)], axis=0
                )
                parts = [q2[b * third : (b + 1) * third, 2 * third :] for b in range(3)] + [marks]
                blocks = [
                    jnp.concatenate([q0, q2[:, :third]], axis=1),
                    jnp.concatenate([q1, q2[:, third : 2 * third]], axis=1),
                    jnp.concatenate(parts, axis=1),
                ]
                packed = jnp.concatenate(blocks, axis=0).astype(jnp.bfloat16)
                out_ref[y ^ flip_ref[0], x ^ flip_ref[1]] = packed


def field_call(first, count, shared, tables, acc=None, ends=None):
    points = shared[-1].shape[2]
    last = ends is not None
    args = list(shared) + [tables] + ([] if acc is None else [acc])
    plain = len(args)
    scratch = table_scratch(count, points)
    if last:
        args += ends
        third = ends[0].shape[1] // 6
        out = jax.ShapeDtypeStruct((2, 2, 7 * third, LANES), jnp.bfloat16)
        scratch += [pltpu.VMEM((24, points), jnp.float32), pltpu.VMEM(ends[0].shape[1:], jnp.bfloat16)]
    else:
        out = jax.ShapeDtypeStruct((24, points), jnp.float32)
    specs = [SMEM] * 4 + [VMEM] * (plain - 4)
    if last:
        specs += [VMEM] * 3 + [SMEM]
    return pl.pallas_call(
        functools.partial(field_kernel, first, count, acc is not None, last),
        out_shape=out,
        in_specs=specs,
        out_specs=VMEM,
        scratch_shapes=scratch,
        cost_estimate=table_cost(count, points),
        name="field",
    )(*args)


def place_kernel(pieces, carried, piece, tile, *refs):
    stacks, refs = refs[:pieces], refs[pieces:]
    if carried:
        acc_in, refs = refs[0], refs[1:]
    out_ref, rows_ref, wide_ref = refs
    third = piece // 3
    group = 4
    total = rows_ref.shape[1] // piece
    lane = lax.broadcasted_iota(jnp.int32, (piece, LANES), 1)
    sub = lax.broadcasted_iota(jnp.int32, (tile, LANES), 0)
    per = total // pieces
    for first in range(0, total, group):
        strips = []
        for g in range(first, first + group):
            ref, at = stacks[g // per], g % per
            tail = ref[at, pl.ds(2 * piece, third), :].astype(jnp.float32)
            marks = tail[: third // 2, 3 * third :]
            row_mark = marks[0:3] * 32.0 + marks[3:6]
            col_mark = marks[8:11] * 32.0 + marks[11:14]
            strips += [row_mark[b : b + 1] for b in range(3)]
            flat = jnp.concatenate([col_mark[b : b + 1] for b in range(3)] + [col_mark[0:1]], axis=1)
            column = jnp.transpose(jnp.broadcast_to(flat, (LANES, LANES)))[:piece].astype(jnp.int32)
            hits = jnp.concatenate(
                [
                    (column == lane + u).astype(jnp.float32).astype(jnp.bfloat16)
                    for u in range(0, tile, LANES)
                ],
                axis=1,
            )
            upper = ref[at, pl.ds(0, piece), :].astype(jnp.float32)
            lower = ref[at, pl.ds(piece, piece), :].astype(jnp.float32)
            rest = jnp.concatenate([tail[:, b * third : (b + 1) * third] for b in range(3)], axis=0)
            shared = jnp.concatenate([upper[:, piece:], lower[:, piece:], rest], axis=1)
            quads = jnp.concatenate([upper[:, :piece], lower[:, :piece], shared], axis=0)
            spread = jnp.dot(
                quads.astype(jnp.bfloat16), hits, preferred_element_type=jnp.float32
            ).astype(jnp.bfloat16)
            for c in range(3):
                wide_ref[c, pl.ds(g * piece, piece), :] = spread[c * piece : (c + 1) * piece]
        strip = jnp.concatenate(strips, axis=1).astype(jnp.int32)
        for start in range(0, group * piece, LANES):
            rows_ref[:, pl.ds(first * piece + start, LANES)] = (
                (sub == strip[:, start : start + LANES]).astype(jnp.float32).astype(jnp.bfloat16)
            )

    step = 256

    def body(i, carry):
        c, t = i // (tile // step), (i % (tile // step)) * step
        here = pl.ds(pl.multiple_of(t, step), step)
        value = jnp.dot(rows_ref[here, :], wide_ref[c], preferred_element_type=jnp.float32)
        if carried:
            value += acc_in[c, here, :]
        out_ref[c, here, :] = value.astype(out_ref.dtype)
        return carry

    lax.fori_loop(0, 3 * (tile // step), body, 0)


def place_call(stacks, piece, tile, acc=None, final=True):
    total = sum(stack.shape[0] for stack in stacks)
    depth = total * piece
    args = list(stacks) + ([] if acc is None else [acc])
    return pl.pallas_call(
        functools.partial(place_kernel, len(stacks), acc is not None, piece, tile),
        out_shape=jax.ShapeDtypeStruct((3, tile, tile), jnp.bfloat16 if final else jnp.float32),
        in_specs=[VMEM] * len(args),
        out_specs=VMEM,
        scratch_shapes=[
            pltpu.VMEM((tile, depth), jnp.bfloat16),
            pltpu.VMEM((3, depth, tile), jnp.bfloat16),
        ],
        input_output_aliases={} if acc is None or final else {len(stacks): 0},
        compiler_params=pltpu.CompilerParams(vmem_limit_bytes=28 << 20),
        cost_estimate=pl.CostEstimate(
            flops=2 * 3 * depth * tile * tile, bytes_accessed=12 * tile * tile, transcendentals=0
        ),
        name="place",
    )(*args)


def apply_green(charges, kernels):
    shaped = charges.astype(jnp.bfloat16).reshape(-1, 3, S, DEG, DEG)
    kernel_rows = kernels.reshape(-1, DEG, S, S)
    result = jnp.einsum(
        "xast,xctam->xcsam", kernel_rows, shaped, preferred_element_type=jnp.float32
    )
    return result.astype(jnp.bfloat16).reshape(-1, 3 * S * DEG * DEG)


def swap(value, axis, mask=1):
    size = lax.axis_size(axis)
    return lax.ppermute(value, axis, [(i, i ^ mask) for i in range(size)])


def plane_atoms(owners, row, col):
    flips = jnp.arange(4)
    inner = ((flips & 1) ^ row) * 2 + ((flips >> 1) ^ col)
    return (jnp.arange(owners)[None, :] * 4 + inner[:, None]).reshape(-1)


def on_device(
    basis_values,
    density_matrix,
    points,
    weights,
    intersection,
    basis_index,
    atom_positions,
    shell_blocks,
    shell_widths,
    green,
):
    atoms = intersection[0]
    labels = basis_index[0]
    owners = lax.axis_size("batch")
    parts = lax.axis_size("row")
    sides = lax.axis_size("col")
    row, col = lax.axis_index("row"), lax.axis_index("col")
    count = atoms.shape[0]
    slots = (count + owners - 1) // owners
    holding = green.shape[0]
    every_atom = atom_positions.shape[1]
    width = 3 * S * DEG * DEG
    lines = width // LANES
    highest = lax.Precision.HIGHEST
    dense = count == every_atom and holding == parts * sides
    if dense:
        atoms = plane_atoms(owners, row, col)
    group = count // 4
    shared = (atoms, atom_positions, shell_blocks, shell_widths, points)

    def moments_of(place, weighted):
        return moments_call(place * group, group, shared, wd=weighted)[0]

    third, weighted = moments_call(
        3 * group, group, shared, phi=basis_values, dens=density_matrix, w=weights
    )
    if dense:
        from_third = swap(third, "col")
        first = moments_of(1, weighted) + from_third
        from_first = swap(first, "row")
        from_second = swap(moments_of(2, weighted), "col")
        held = (
            moments_of(0, weighted).astype(jnp.float32)
            + from_second.astype(jnp.float32)
            + from_first.astype(jnp.float32)
        ).astype(jnp.bfloat16)
        shares = lax.all_to_all(held, "batch", split_axis=0, concat_axis=0, tiled=True)
        charges = jnp.sum(shares.astype(jnp.float32), axis=0)
        kernels = lax.dynamic_index_in_dim(green, row * sides + col, 0, keepdims=True)
        mine = apply_green(charges.reshape(1, width), kernels).reshape(1, lines, LANES)
        own = lax.all_to_all(
            jnp.broadcast_to(mine, (owners, lines, LANES)),
            "batch",
            split_axis=0,
            concat_axis=0,
            tiled=True,
        )
        beside = swap(own, "row")
        tables = [own, beside, swap(own, "col"), swap(beside, "col")]
        here = lax.axis_index("batch")
        plane = jnp.stack(
            [lax.dynamic_index_in_dim(table, here, 0, keepdims=False) for table in tables]
        )
        places = [(j // sides ^ row) + 2 * (j % sides ^ col) for j in range(holding)]
        potential = jnp.concatenate(
            [lax.dynamic_index_in_dim(plane, place, 0) for place in places]
        ).reshape(holding, width)
    else:
        moments = jnp.concatenate([moments_of(place, weighted) for place in range(3)] + [third])
        moments = moments.astype(jnp.float32).reshape(count, width)
        home = atoms // holding
        local_slot = atoms % holding
        order = jnp.arange(count)
        before = (home[None, :] == home[:, None]) & (order[None, :] < order[:, None])
        place = home * slots + jnp.sum(before, axis=1)
        routing = jnp.arange(owners * slots)[:, None] == place[None, :]
        outgoing = jnp.dot(routing.astype(jnp.float32), moments, precision=highest).reshape(
            owners, slots, width
        )
        tags = (jnp.sum(jnp.where(routing, local_slot[None, :] + 1, 0), axis=1) - 1).reshape(
            owners, slots
        )
        incoming, sources = (
            lax.all_to_all(outgoing, "batch", split_axis=0, concat_axis=0, tiled=True),
            lax.all_to_all(tags, "batch", split_axis=0, concat_axis=0, tiled=True),
        )
        collect = jnp.arange(holding)[:, None] == sources.reshape(1, owners * slots)
        partial_value = jnp.dot(
            collect.astype(jnp.float32), incoming.reshape(owners * slots, width), precision=highest
        )
        totals = lax.psum(partial_value, ("row", "col"))
        potential = apply_green(totals, green)
        back = jnp.dot(
            collect.T.astype(jnp.bfloat16), potential, preferred_element_type=jnp.float32
        ).astype(jnp.bfloat16)
        returned = lax.all_to_all(
            back.reshape(owners, slots, width), "batch", split_axis=0, concat_axis=0, tiled=True
        )
        table = jnp.dot(
            routing.T.astype(jnp.bfloat16),
            returned.reshape(owners * slots, width),
            preferred_element_type=jnp.float32,
        )
        table = table.astype(jnp.bfloat16).reshape(count, lines, LANES)
        tables = [table[place * group : (place + 1) * group] for place in range(4)]
    piece = labels.shape[0] // parts
    tile = NB // parts
    inner = labels.reshape(parts, 3, piece // 3) - jnp.arange(parts)[:, None, None] * tile
    marks = jnp.concatenate([inner // 32, inner % 32, inner[:, :2] * 0], axis=1)
    marks = marks.astype(jnp.float32)
    field = None
    for place in (0, 2, 1):
        field = field_call(place * group, group, shared, tables[place], field)
    ends = [basis_values, weights, marks, jnp.stack([col, row])]
    load = field_call(3 * group, group, shared, tables[3], field, ends)
    plane = ("row", "col")
    across = [(i, i ^ 3) for i in range(parts * sides)]
    diagonal = lax.ppermute(load[1, 1:], plane, across)
    plane_load = jnp.concatenate(
        [load[0, :1], swap(load[1, :1], "col"), swap(load[0, 1:], "row"), diagonal], axis=0
    )
    if owners <= 8:
        near = [plane_load] + [swap(plane_load, "batch", m) for m in range(2, owners, 2)]
        far = [swap(line, "batch") for line in near]
        total = None
        for first in range(0, len(near), 2):
            for lines in (near, far):
                last = lines is far and first + 2 >= len(near)
                total = place_call(lines[first : first + 2], piece, tile, total, final=last)
        hamiltonian = total
    else:
        everyone = lax.all_gather(plane_load, "batch", axis=0)
        chunk = 4
        everyone = everyone.reshape((owners // chunk, chunk * 4) + plane_load.shape[1:])

        def add(total, item):
            return place_call([item], piece, tile, total, final=False), None

        total, _ = lax.scan(add, jnp.zeros((3, tile, tile), jnp.float32), everyone)
        hamiltonian = total.astype(jnp.bfloat16)
    return (potential, hamiltonian)


def solution(mesh):
    return jax.shard_map(
        on_device,
        mesh=mesh,
        in_specs=(
            P(("batch", "row", "col"), None, None),
            P(("batch", "row", "col"), None, None, None),
            P(("batch", "row", "col"), None, None),
            P(("batch", "row", "col"), None),
            P(("batch", "row", "col"), None),
            P(("batch", "row", "col"), None),
            P(),
            P(),
            P(),
            P("batch", None, None),
        ),
        out_specs=(P("batch", None), P(None, "row", "col")),
        check_vma=False,
    )
```

time: 154 us -> 143 us (0.929)
  Pallas kernels: 74.3 us -> 67.4 us
  local copies, waits for them, and re-layouts: 16 us -> 10.6 us
  waiting for transfers between devices: 31.9 us -> 33.5 us
    pallas_call x8, Pallas kernels: 44.4 us -> 39.9 us  [the longest x4 20.6 us: field_call(): pl.pallas_call(functools.partial(field_kernel, first, count, acc is not N...]
    pallas_call x2 -> x4, Pallas kernels: 29.9 us -> 27.4 us  [place_call(): pl.pallas_call(functools.partial(place_kernel, len(stacks), acc is not No...]
    ppermute x15, starting transfers between devices: 14.6 us -> 12.8 us  [swap(): return lax.ppermute(value, axis, [(i, i ^ mask) for i in range(size)])]
    slice x3 -> x0, local copies, waits for them, and re-layouts: 1.59 us -> none  [the longest x2 1.58 us: on_device(): ordered = jnp.concatenate([shell_widths[0::2], shell_widths[1::2]])]
    unnamed x29 -> x13, local copies, waits for them, and re-layouts: 5.49 us -> 3.97 us
  transfers between devices with their start and end apart: 17 -> 18, of which waited for: 6 -> 7; matrix products, arithmetic and copies ran while one was open for 6% -> 6% of each run, Pallas kernels for 30% -> 33%
where the time goes in v3:
time: 143 us; the launch traced here: 142 us
  Pallas kernels  67.4 us (47%)
  waiting for transfers between devices  33.5 us (23%)
  starting transfers between devices  23.5 us (16%)
  local copies, waits for them, and re-layouts  10.6 us (7%)
  other arithmetic  5.53 us (4%)
    pallas_call x4, Pallas kernels, place_call(): pl.pallas_call(functools.partial(place_kernel, len(stacks), acc is not No...  27.4 us
    pallas_call x4, Pallas kernels, field_call(): pl.pallas_call(functools.partial(field_kernel, first, count, acc is not N...  20.6 us
    pallas_call x4, Pallas kernels, moments_call(): pl.pallas_call(functools.partial(moments_kernel, first, count, fresh), ou...  19.4 us
    ppermute x15, waiting for transfers between devices, swap(): return lax.ppermute(value, axis, [(i, i ^ mask) for i in range(size)])  18.6 us
    ppermute x15, starting transfers between devices, swap(): return lax.ppermute(value, axis, [(i, i ^ mask) for i in range(size)])  12.8 us
    all_to_all x1, waiting for transfers between devices, on_device(): lax.all_to_all(held, 'batch', split_axis=0, concat_axis=0, tiled=True)  7.57 us
    all_to_all x1, waiting for transfers between devices, on_device(): lax.all_to_all(jnp.broadcast_to(mine, (owners, lines, LANES)), 'batch', s...  6.79 us
    all_to_all x1, starting transfers between devices, on_device(): lax.all_to_all(held, 'batch', split_axis=0, concat_axis=0, tiled=True)  5.81 us
  transfers between devices with their start and end apart: 18, of which 7 were waited for; matrix products, arithmetic and copies ran while one was open for 6% of the time, Pallas kernels for 33%

profile of v3, /device:TPU:0, one launch (start us, length us, event | category | flops | bytes accessed | tf_op | source)
XLA Modules:
  0.0 141.6 jit_solution(6991124007244122548)
XLA Ops:
  1.3 1.4 copy.22.refs_4_
  2.7 6.0 %moments.4 = (bf16[8,96,128]{2,1,0:T(8,128)(2,1)}, f32[3,2048]{1,0:T(4,128)}) custom-call(s32[32]{0:T(128)} %add.83.refs_0_, f32[3,32]{1,0:T(4,128)} %refs_1_.15, s32[32]{0:T(128)} %refs_2_.15, f32[64]{0:T(128)} %refs_3_.15, f32[1,3,2048]{2,1,0:T(4,128)} %copy.22.refs_4_, bf16[1,192,2048]{2,1,0:T(8,128)(2,1)} %refs_7_.3, bf16[1,3,192,192]{3,2,1,0:T(8,128)(2,1)} %refs_6_.1, ...), custom_call_target="tpu_custom_call" | custom-call | flops 402653184 | bytes 1048576 | tf_op jit(solution)/shard_map/moments/pallas_call | solution.py:175
  8.9 4.3 %moments.6 = bf16[8,96,128]{2,1,0:T(8,128)(2,1)} custom-call(s32[32]{0:T(128)} %add.83.refs_0_, f32[3,32]{1,0:T(4,128)} %refs_1_.15, s32[32]{0:T(128)} %refs_2_.15, f32[64]{0:T(128)} %refs_3_.15, f32[1,3,2048]{2,1,0:T(4,128)} %copy.22.refs_4_, f32[3,2048]{1,0:T(4,128)} %get-tuple-element.4.refs_5_), custom_call_target="tpu_custom_call" | custom-call | flops 402653184 | bytes 1048576 | tf_op jit(solution)/shard_map/moments/pallas_call | solution.py:175
  13.7 4.5 %moments.7 = bf16[8,96,128]{2,1,0:T(8,128)(2,1)} custom-call(s32[32]{0:T(128)} %add.83.refs_0_, f32[3,32]{1,0:T(4,128)} %refs_1_.15, s32[32]{0:T(128)} %refs_2_.15, f32[64]{0:T(128)} %refs_3_.15, f32[1,3,2048]{2,1,0:T(4,128)} %copy.22.refs_4_, f32[3,2048]{1,0:T(4,128)} %get-tuple-element.4.refs_5_), custom_call_target="tpu_custom_call" | custom-call | flops 402653184 | bytes 1048576 | tf_op jit(solution)/shard_map/moments/pallas_call | solution.py:175
  19.2 2.7 %collective-permute-start.2 = (bf16[8,96,128]{2,1,0:T(8,128)(2,1)S(1)}, bf16[8,96,128]{2,1,0:T(8,128)(2,1)S(1)}, u32[]{:S(2)}, u32[]{:S(2)}) collective-permute-start(bf16[8,96,128]{2,1,0:T(8,128)(2,1)S(1)} %add.85), channel_id=1, source_target_pairs={{0,2},{2,0},{1,3},{3,1},{4,6},{6,4},{5,7},{7,5},{8,10},{10,8},{9,1... | collective-permute-start | bytes 589832 | tf_op jit(solution)/shard_map/ppermute | solution.py:387
  23.9 4.6 %moments.5 = bf16[8,96,128]{2,1,0:T(8,128)(2,1)} custom-call(s32[32]{0:T(128)} %add.83.refs_0_, f32[3,32]{1,0:T(4,128)} %refs_1_.15, s32[32]{0:T(128)} %refs_2_.15, f32[64]{0:T(128)} %refs_3_.15, f32[1,3,2048]{2,1,0:T(4,128)} %copy.22.refs_4_, f32[3,2048]{1,0:T(4,128)} %get-tuple-element.4.refs_5_), custom_call_target="tpu_custom_call" | custom-call | flops 402653184 | bytes 1048576 | tf_op jit(solution)/shard_map/moments/pallas_call | solution.py:175
  28.5 1.7 %add_convert_fusion = bf16[8,96,128]{2,1,0:T(8,128)(2,1)} fusion(bf16[8,96,128]{2,1,0:T(8,128)(2,1)S(1)} %collective-permute-done.2, bf16[8,96,128]{2,1,0:T(8,128)(2,1)S(1)} %collective-permute-done, bf16[8,96,128]{2,1,0:T(8,128)(2,1)} %moments.5), kind=kLoop, calls=%fused_computation.3 | loop fusion | flops 589824 | bytes 786432 | tf_op jit(solution)/shard_map/convert_element_type | solution.py:442
  30.2 5.8 %all-to-all-start = ((bf16[8,96,128]{2,1,0:T(8,128)(2,1)}), bf16[8,96,128]{2,1,0:T(8,128)(2,1)S(1)}, u32[]{:S(2)}, u32[]{:S(2)}) async-start(bf16[8,96,128]{2,1,0:T(8,128)(2,1)} %add_convert_fusion), calls=%async_computation | async-start | bytes 393216 | tf_op jit(solution)/shard_map/all_to_all | solution.py:443
  36.2 7.6 %all-to-all-done = bf16[8,96,128]{2,1,0:T(8,128)(2,1)S(1)} async-done(((bf16[8,96,128]{2,1,0:T(8,128)(2,1)}), bf16[8,96,128]{2,1,0:T(8,128)(2,1)S(1)}, u32[]{:S(2)}, u32[]{:S(2)}) %all-to-all-start) | async-done | bytes 196640 | tf_op jit(solution)/shard_map/all_to_all | solution.py:443
  46.0 3.6 %all-to-all-start.1 = ((bf16[8,96,128]{2,1,0:T(8,128)(2,1)}), bf16[8,96,128]{2,1,0:T(8,128)(2,1)S(1)}, u32[]{:S(2)}, u32[]{:S(2)}) async-start(bf16[8,96,128]{2,1,0:T(8,128)(2,1)} %broadcast_in_dim.5), calls=%async_computation.1 | async-start | bytes 393216 | tf_op jit(solution)/shard_map/all_to_all | solution.py:447
  50.3 6.8 %all-to-all-done.1.refs_5_ = bf16[8,96,128]{2,1,0:T(8,128)(2,1)S(1)} async-done(((bf16[8,96,128]{2,1,0:T(8,128)(2,1)}), bf16[8,96,128]{2,1,0:T(8,128)(2,1)S(1)}, u32[]{:S(2)}, u32[]{:S(2)}) %all-to-all-start.1) | async-done | bytes 196640 | tf_op jit(solution)/shard_map/all_to_all | solution.py:447
  59.0 4.7 %field.4.refs_6_ = f32[24,2048]{1,0:T(8,128)} custom-call(s32[32]{0:T(128)} %add.83.refs_0_, f32[3,32]{1,0:T(4,128)} %refs_1_.15, s32[32]{0:T(128)} %refs_2_.15, f32[64]{0:T(128)} %refs_3_.15, f32[1,3,2048]{2,1,0:T(4,128)} %copy.22.refs_4_, bf16[8,96,128]{2,1,0:T(8,128)(2,1)} %copy-done.1), custom_call_target="tpu_custom_call" | custom-call | flops 402653184 | bytes 1048576 | tf_op jit(solution)/shard_map/field/pallas_call | solution.py:284
  65.2 4.6 %field.5.refs_6_ = f32[24,2048]{1,0:T(8,128)} custom-call(s32[32]{0:T(128)} %add.83.refs_0_, f32[3,32]{1,0:T(4,128)} %refs_1_.15, s32[32]{0:T(128)} %refs_2_.15, f32[64]{0:T(128)} %refs_3_.15, f32[1,3,2048]{2,1,0:T(4,128)} %copy.22.refs_4_, bf16[8,96,128]{2,1,0:T(8,128)(2,1)} %copy-done.2, f32[24,2048]{1,0:T(8,128)} %field.4.refs_6_), custom_call_target="tpu_custom_call" | custom-call | flops 402653184 | bytes 1048576 | tf_op jit(solution)/shard_map/field/pallas_call | solution.py:284
  69.7 4.7 %field.6.refs_6_ = f32[24,2048]{1,0:T(8,128)} custom-call(s32[32]{0:T(128)} %add.83.refs_0_, f32[3,32]{1,0:T(4,128)} %refs_1_.15, s32[32]{0:T(128)} %refs_2_.15, f32[64]{0:T(128)} %refs_3_.15, f32[1,3,2048]{2,1,0:T(4,128)} %copy.22.refs_4_, bf16[8,96,128]{2,1,0:T(8,128)(2,1)} %copy-done.3, f32[24,2048]{1,0:T(8,128)} %field.5.refs_6_), custom_call_target="tpu_custom_call" | custom-call | flops 402653184 | bytes 1048576 | tf_op jit(solution)/shard_map/field/pallas_call | solution.py:284
  76.6 6.6 %field.7 = bf16[2,2,224,128]{3,2,1,0:T(8,128)(2,1)} custom-call(s32[32]{0:T(128)} %add.83.refs_0_, f32[3,32]{1,0:T(4,128)} %refs_1_.15, s32[32]{0:T(128)} %refs_2_.15, f32[64]{0:T(128)} %refs_3_.15, f32[1,3,2048]{2,1,0:T(4,128)} %copy.22.refs_4_, bf16[8,96,128]{2,1,0:T(8,128)(2,1)} %copy-done.4, f32[24,2048]{1,0:T(8,128)} %field.6.refs_6_, ...), custom_call_target="tpu_custom_call" | custom-call | flops 402653184 | bytes 1048576 | tf_op jit(solution)/shard_map/field/pallas_call | solution.py:284
  87.8 2.1 %collective-permute-done.7 = bf16[1,224,128]{2,1,0:T(8,128)(2,1)S(1)} collective-permute-done((bf16[1,224,128]{2,1,0:T(8,128)(2,1)S(1)}, bf16[1,224,128]{2,1,0:T(8,128)(2,1)S(1)}, u32[]{:S(2)}, u32[]{:S(2)}) %collective-permute-start.7) | collective-permute-done | bytes 57376 | tf_op jit(solution)/shard_map/ppermute | solution.py:387
  90.1 1.9 %collective-permute-start.11 = (bf16[4,224,128]{2,1,0:T(8,128)(2,1)S(1)}, bf16[4,224,128]{2,1,0:T(8,128)(2,1)S(1)}, u32[]{:S(2)}, u32[]{:S(2)}) collective-permute-start(bf16[4,224,128]{2,1,0:T(8,128)(2,1)S(1)} %pad_maximum_fusion.refs_0_), channel_id=1, source_target_pairs={{0,24},{4,28},{8,16},{12,20},{16,8},{20,12},{24,0},{28,4},{1,25},{... | collective-permute-start | bytes 688136 | tf_op jit(solution)/shard_map/ppermute | solution.py:387
  92.0 1.5 %collective-permute-start.9 = (bf16[4,224,128]{2,1,0:T(8,128)(2,1)S(1)}, bf16[4,224,128]{2,1,0:T(8,128)(2,1)S(1)}, u32[]{:S(2)}, u32[]{:S(2)}) collective-permute-start(bf16[4,224,128]{2,1,0:T(8,128)(2,1)S(1)} %pad_maximum_fusion.refs_0_), channel_id=1, source_target_pairs={{0,16},{4,20},{8,24},{12,28},{16,0},{20,4},{24,8},{28,12},{1,17},{... | collective-permute-start | bytes 688136 | tf_op jit(solution)/shard_map/ppermute | solution.py:387
  95.1 6.0 %collective-permute-done.14.refs_1_ = bf16[4,224,128]{2,1,0:T(8,128)(2,1)S(1)} collective-permute-done((bf16[4,224,128]{2,1,0:T(8,128)(2,1)S(1)}, bf16[4,224,128]{2,1,0:T(8,128)(2,1)S(1)}, u32[]{:S(2)}, u32[]{:S(2)}) %collective-permute-start.14) | collective-permute-done | bytes 229408 | tf_op jit(solution)/shard_map/ppermute | solution.py:387
  103.6 9.4 %collective-permute-done.9.refs_0_ = bf16[4,224,128]{2,1,0:T(8,128)(2,1)S(1)} collective-permute-done((bf16[4,224,128]{2,1,0:T(8,128)(2,1)S(1)}, bf16[4,224,128]{2,1,0:T(8,128)(2,1)S(1)}, u32[]{:S(2)}, u32[]{:S(2)}) %collective-permute-start.9) | collective-permute-done | bytes 229408 | tf_op jit(solution)/shard_map/ppermute | solution.py:387
  114.1 6.1 %place.4.refs_2_ = f32[3,768,768]{2,1,0:T(8,128)S(1)} custom-call(bf16[4,224,128]{2,1,0:T(8,128)(2,1)S(1)} %pad_maximum_fusion.refs_0_, bf16[4,224,128]{2,1,0:T(8,128)(2,1)S(1)} %collective-permute-done.14.refs_1_), custom_call_target="tpu_custom_call" | custom-call | flops 2717908992 | bytes 7077888 | tf_op jit(solution)/shard_map/place/pallas_call | solution.py:358
  120.2 6.8 %place.5.refs_2_ = f32[3,768,768]{2,1,0:T(8,128)S(1)} custom-call(bf16[4,224,128]{2,1,0:T(8,128)(2,1)S(1)} %collective-permute-done.13.refs_0_, bf16[4,224,128]{2,1,0:T(8,128)(2,1)S(1)} %collective-permute-done.15.refs_1_, f32[3,768,768]{2,1,0:T(8,128)S(1)} %place.4.refs_2_), custom_call_target="tpu_custom_call", output_to_operand_aliasing={{}: (2, {})} | custom-call | flops 2717908992 | bytes 7077888 | tf_op jit(solution)/shard_map/place/pallas_call | solution.py:358
  127.0 6.6 %place.6.refs_2_ = f32[3,768,768]{2,1,0:T(8,128)S(1)} custom-call(bf16[4,224,128]{2,1,0:T(8,128)(2,1)S(1)} %collective-permute-done.9.refs_0_, bf16[4,224,128]{2,1,0:T(8,128)(2,1)S(1)} %collective-permute-done.11.refs_1_, f32[3,768,768]{2,1,0:T(8,128)S(1)} %place.5.refs_2_), custom_call_target="tpu_custom_call", output_to_operand_aliasing={{}: (2, {})} | custom-call | flops 2717908992 | bytes 7077888 | tf_op jit(solution)/shard_map/place/pallas_call | solution.py:358
  133.6 7.9 %place.7 = bf16[3,768,768]{2,1,0:T(8,128)(2,1)} custom-call(bf16[4,224,128]{2,1,0:T(8,128)(2,1)S(1)} %collective-permute-done.10.refs_0_, bf16[4,224,128]{2,1,0:T(8,128)(2,1)S(1)} %collective-permute-done.12.refs_1_, f32[3,768,768]{2,1,0:T(8,128)S(1)} %place.6.refs_2_), custom_call_target="tpu_custom_call" | custom-call | flops 2717908992 | bytes 7077888 | tf_op jit(solution)/shard_map/place/pallas_call | solution.py:358
  (68 shorter events, 23.0 us)
Async XLA Ops:
  0.6 35.4 %copy-start = (bf16[4,8,4096]{2,1,0:T(8,128)(2,1)S(1)}, bf16[4,8,4096]{2,1,0:T(8,128)(2,1)}, u32[]{:S(2)}) copy-start(bf16[4,8,4096]{2,1,0:T(8,128)(2,1)} %param.18) | copy-start | bytes 786436
  8.6 9.6 %collective-permute-start.1 = (bf16[8,96,128]{2,1,0:T(8,128)(2,1)}, bf16[8,96,128]{2,1,0:T(8,128)(2,1)S(1)}, u32[]{:S(2)}, u32[]{:S(2)}) collective-permute-start(bf16[8,96,128]{2,1,0:T(8,128)(2,1)} %get-tuple-element.5), channel_id=1, source_target_pairs={{0,1},{1,0},{2,3},{3,2},{4,5},{5,4},{6,7},{7,6},{8,9},{9,8},{10,11... | collective-permute-start | bytes 589832 | tf_op jit(solution)/shard_map/ppermute | solution.py:387
  13.2 15.3 %collective-permute-start = (bf16[8,96,128]{2,1,0:T(8,128)(2,1)}, bf16[8,96,128]{2,1,0:T(8,128)(2,1)S(1)}, u32[]{:S(2)}, u32[]{:S(2)}) collective-permute-start(bf16[8,96,128]{2,1,0:T(8,128)(2,1)} %moments.6), channel_id=1, source_target_pairs={{0,1},{1,0},{2,3},{3,2},{4,5},{5,4},{6,7},{7,6},{8,9},{9,8},{10,11... | collective-permute-start | bytes 589832 | tf_op jit(solution)/shard_map/ppermute | solution.py:387
  19.2 9.3 %collective-permute-start.2 = (bf16[8,96,128]{2,1,0:T(8,128)(2,1)S(1)}, bf16[8,96,128]{2,1,0:T(8,128)(2,1)S(1)}, u32[]{:S(2)}, u32[]{:S(2)}) collective-permute-start(bf16[8,96,128]{2,1,0:T(8,128)(2,1)S(1)} %add.85), channel_id=1, source_target_pairs={{0,2},{2,0},{1,3},{3,1},{4,6},{6,4},{5,7},{7,5},{8,10},{10,8},{9,1... | collective-permute-start | bytes 589832 | tf_op jit(solution)/shard_map/ppermute | solution.py:387
  30.2 13.6 %all-to-all-start = ((bf16[8,96,128]{2,1,0:T(8,128)(2,1)}), bf16[8,96,128]{2,1,0:T(8,128)(2,1)S(1)}, u32[]{:S(2)}, u32[]{:S(2)}) async-start(bf16[8,96,128]{2,1,0:T(8,128)(2,1)} %add_convert_fusion), calls=%async_computation | async-start | bytes 393216 | tf_op jit(solution)/shard_map/all_to_all | solution.py:443
  46.0 11.1 %all-to-all-start.1 = ((bf16[8,96,128]{2,1,0:T(8,128)(2,1)}), bf16[8,96,128]{2,1,0:T(8,128)(2,1)S(1)}, u32[]{:S(2)}, u32[]{:S(2)}) async-start(bf16[8,96,128]{2,1,0:T(8,128)(2,1)} %broadcast_in_dim.5), calls=%async_computation.1 | async-start | bytes 393216 | tf_op jit(solution)/shard_map/all_to_all | solution.py:447
  57.1 1.9 %copy-start.1 = (bf16[8,96,128]{2,1,0:T(8,128)(2,1)}, bf16[8,96,128]{2,1,0:T(8,128)(2,1)S(1)}, u32[]{:S(2)}) copy-start(bf16[8,96,128]{2,1,0:T(8,128)(2,1)S(1)} %all-to-all-done.1.refs_5_) | copy-start | bytes 589828
  57.1 7.4 %collective-permute-start.4 = (bf16[8,96,128]{2,1,0:T(8,128)(2,1)S(1)}, bf16[8,96,128]{2,1,0:T(8,128)(2,1)S(1)}, u32[]{:S(2)}, u32[]{:S(2)}) collective-permute-start(bf16[8,96,128]{2,1,0:T(8,128)(2,1)S(1)} %all-to-all-done.1.refs_5_), channel_id=1, source_target_pairs={{0,1},{1,0},{2,3},{3,2},{4,5},{5,4},{6,7},{7,6},{8,9},{9,8},{10,11... | collective-permute-start | bytes 589832 | tf_op jit(solution)/shard_map/ppermute | solution.py:387
  57.1 7.3 %collective-permute-start.3 = (bf16[8,96,128]{2,1,0:T(8,128)(2,1)S(1)}, bf16[8,96,128]{2,1,0:T(8,128)(2,1)S(1)}, u32[]{:S(2)}, u32[]{:S(2)}) collective-permute-start(bf16[8,96,128]{2,1,0:T(8,128)(2,1)S(1)} %all-to-all-done.1.refs_5_), channel_id=1, source_target_pairs={{0,2},{2,0},{1,3},{3,1},{4,6},{6,4},{5,7},{7,5},{8,10},{10,8},{9,1... | collective-permute-start | bytes 589832 | tf_op jit(solution)/shard_map/ppermute | solution.py:387
  64.4 5.3 %copy-start.3 = (bf16[8,96,128]{2,1,0:T(8,128)(2,1)}, bf16[8,96,128]{2,1,0:T(8,128)(2,1)S(1)}, u32[]{:S(2)}) copy-start(bf16[8,96,128]{2,1,0:T(8,128)(2,1)S(1)} %collective-permute-done.3.refs_5_) | copy-start | bytes 589828
  64.4 11.5 %collective-permute-start.5 = (bf16[8,96,128]{2,1,0:T(8,128)(2,1)S(1)}, bf16[8,96,128]{2,1,0:T(8,128)(2,1)S(1)}, u32[]{:S(2)}, u32[]{:S(2)}) collective-permute-start(bf16[8,96,128]{2,1,0:T(8,128)(2,1)S(1)} %collective-permute-done.3.refs_5_), channel_id=1, source_target_pairs={{0,1},{1,0},{2,3},{3,2},{4,5},{5,4},{6,7},{7,6},{8,9},{9,8},{10,11... | collective-permute-start | bytes 589832 | tf_op jit(solution)/shard_map/ppermute | solution.py:387
  64.4 0.7 copy-start.2
  75.9 0.7 copy-start.4
  84.1 3.7 %collective-permute-start.8 = (bf16[1,224,128]{2,1,0:T(8,128)(2,1)S(1)}, bf16[1,224,128]{2,1,0:T(8,128)(2,1)S(1)}, u32[]{:S(2)}, u32[]{:S(2)}) collective-permute-start(bf16[1,224,128]{2,1,0:T(8,128)(2,1)S(1)} %get-tuple-element.7), channel_id=1, source_target_pairs={{0,3},{1,2},{2,1},{3,0},{4,7},{5,6},{6,5},{7,4},{8,11},{9,10},{10,... | collective-permute-start | bytes 172040 | tf_op jit(solution)/shard_map/ppermute | solution.py:514
  85.4 4.5 %collective-permute-start.7 = (bf16[1,224,128]{2,1,0:T(8,128)(2,1)S(1)}, bf16[1,224,128]{2,1,0:T(8,128)(2,1)S(1)}, u32[]{:S(2)}, u32[]{:S(2)}) collective-permute-start(bf16[1,224,128]{2,1,0:T(8,128)(2,1)S(1)} %get-tuple-element.8), channel_id=1, source_target_pairs={{0,2},{2,0},{1,3},{3,1},{4,6},{6,4},{5,7},{7,5},{8,10},{10,8},{9,1... | collective-permute-start | bytes 172040 | tf_op jit(solution)/shard_map/ppermute | solution.py:387
  86.5 3.4 %collective-permute-start.6 = (bf16[1,224,128]{2,1,0:T(8,128)(2,1)S(1)}, bf16[1,224,128]{2,1,0:T(8,128)(2,1)S(1)}, u32[]{:S(2)}, u32[]{:S(2)}) collective-permute-start(bf16[1,224,128]{2,1,0:T(8,128)(2,1)S(1)} %get-tuple-element.9), channel_id=1, source_target_pairs={{0,1},{1,0},{2,3},{3,2},{4,5},{5,4},{6,7},{7,6},{8,9},{9,8},{10,11... | collective-permute-start | bytes 172040 | tf_op jit(solution)/shard_map/ppermute | solution.py:387
  89.9 11.3 %collective-permute-start.14 = (bf16[4,224,128]{2,1,0:T(8,128)(2,1)S(1)}, bf16[4,224,128]{2,1,0:T(8,128)(2,1)S(1)}, u32[]{:S(2)}, u32[]{:S(2)}) collective-permute-start(bf16[4,224,128]{2,1,0:T(8,128)(2,1)S(1)} %pad_maximum_fusion.refs_0_), channel_id=1, source_target_pairs={{0,8},{4,12},{8,0},{12,4},{16,24},{20,28},{24,16},{28,20},{1,9},{5... | collective-permute-start | bytes 688136 | tf_op jit(solution)/shard_map/ppermute | solution.py:387
  90.1 13.3 %collective-permute-start.11 = (bf16[4,224,128]{2,1,0:T(8,128)(2,1)S(1)}, bf16[4,224,128]{2,1,0:T(8,128)(2,1)S(1)}, u32[]{:S(2)}, u32[]{:S(2)}) collective-permute-start(bf16[4,224,128]{2,1,0:T(8,128)(2,1)S(1)} %pad_maximum_fusion.refs_0_), channel_id=1, source_target_pairs={{0,24},{4,28},{8,16},{12,20},{16,8},{20,12},{24,0},{28,4},{1,25},{... | collective-permute-start | bytes 688136 | tf_op jit(solution)/shard_map/ppermute | solution.py:387
  92.0 21.1 %collective-permute-start.9 = (bf16[4,224,128]{2,1,0:T(8,128)(2,1)S(1)}, bf16[4,224,128]{2,1,0:T(8,128)(2,1)S(1)}, u32[]{:S(2)}, u32[]{:S(2)}) collective-permute-start(bf16[4,224,128]{2,1,0:T(8,128)(2,1)S(1)} %pad_maximum_fusion.refs_0_), channel_id=1, source_target_pairs={{0,16},{4,20},{8,24},{12,28},{16,0},{20,4},{24,8},{28,12},{1,17},{... | collective-permute-start | bytes 688136 | tf_op jit(solution)/shard_map/ppermute | solution.py:387
  94.1 26.0 %collective-permute-start.13 = (bf16[4,224,128]{2,1,0:T(8,128)(2,1)S(1)}, bf16[4,224,128]{2,1,0:T(8,128)(2,1)S(1)}, u32[]{:S(2)}, u32[]{:S(2)}) collective-permute-start(bf16[4,224,128]{2,1,0:T(8,128)(2,1)S(1)} %pad_maximum_fusion.refs_0_), channel_id=1, source_target_pairs={{0,4},{4,0},{8,12},{12,8},{16,20},{20,16},{24,28},{28,24},{1,5},{5... | collective-permute-start | bytes 688136 | tf_op jit(solution)/shard_map/ppermute | solution.py:387
  101.2 19.0 %collective-permute-start.15 = (bf16[4,224,128]{2,1,0:T(8,128)(2,1)S(1)}, bf16[4,224,128]{2,1,0:T(8,128)(2,1)S(1)}, u32[]{:S(2)}, u32[]{:S(2)}) collective-permute-start(bf16[4,224,128]{2,1,0:T(8,128)(2,1)S(1)} %collective-permute-done.14.refs_1_), channel_id=1, source_target_pairs={{0,4},{4,0},{8,12},{12,8},{16,20},{20,16},{24,28},{28,24},{1,5},{5... | collective-permute-start | bytes 688136 | tf_op jit(solution)/shard_map/ppermute | solution.py:387
  103.4 30.2 %collective-permute-start.12 = (bf16[4,224,128]{2,1,0:T(8,128)(2,1)S(1)}, bf16[4,224,128]{2,1,0:T(8,128)(2,1)S(1)}, u32[]{:S(2)}, u32[]{:S(2)}) collective-permute-start(bf16[4,224,128]{2,1,0:T(8,128)(2,1)S(1)} %collective-permute-done.11.refs_1_), channel_id=1, source_target_pairs={{0,4},{4,0},{8,12},{12,8},{16,20},{20,16},{24,28},{28,24},{1,5},{5... | collective-permute-start | bytes 688136 | tf_op jit(solution)/shard_map/ppermute | solution.py:387
  113.1 20.5 %collective-permute-start.10 = (bf16[4,224,128]{2,1,0:T(8,128)(2,1)S(1)}, bf16[4,224,128]{2,1,0:T(8,128)(2,1)S(1)}, u32[]{:S(2)}, u32[]{:S(2)}) collective-permute-start(bf16[4,224,128]{2,1,0:T(8,128)(2,1)S(1)} %collective-permute-done.9.refs_0_), channel_id=1, source_target_pairs={{0,4},{4,0},{8,12},{12,8},{16,20},{20,16},{24,28},{28,24},{1,5},{5... | collective-permute-start | bytes 688136 | tf_op jit(solution)/shard_map/ppermute | solution.py:387

commit v4 on v3

--- a/solution.py
+++ b/solution.py
@@ -6,6 +6,7 @@
 from jax.experimental import pallas as pl
 from jax.experimental.pallas import tpu as pltpu
 from jax.sharding import PartitionSpec as P
+
 
 S = 64
 DEG = 8
@@ -18,13 +19,14 @@
 VMEM = pl.BlockSpec(memory_space=pltpu.VMEM)
 
 
-def prepare(first, count, atoms_ref, pos_ref, pts_ref, dist_ref, polar_ref, side_ref):
+def prepare(chosen, atoms_ref, pos_ref, pts_ref, dist_ref, polar_ref, side_ref):
+    count = len(chosen)
     rows = lax.broadcasted_iota(jnp.int32, (count, LANES), 0)
     centre = []
     for axis in range(3):
         column = jnp.zeros((count, LANES), jnp.float32)
-        for k in range(count):
-            column = jnp.where(rows == k, pos_ref[axis, atoms_ref[first + k]], column)
+        for k, place in enumerate(chosen):
+            column = jnp.where(rows == k, pos_ref[axis, atoms_ref[place]], column)
         centre.append(column)
     for t in range(pts_ref.shape[2] // LANES):
         here = pl.ds(t * LANES, LANES)
@@ -109,7 +111,7 @@
                 product = jnp.dot(dens_ref[0, c], phi, preferred_element_type=jnp.float32)
                 density = jnp.sum(wide * product, axis=0, keepdims=True)
                 wd_ref[pl.ds(c, 1), here] = w_ref[:, here] * density
-    prepare(first, count, atoms_ref, pos_ref, pts_ref, dist_ref, polar_ref, side_ref)
+    prepare(range(first, first + count), atoms_ref, pos_ref, pts_ref, dist_ref, polar_ref, side_ref)
     prepare_shells(widths_ref, scale_ref)
 
     def body(k, carry):
@@ -183,29 +185,42 @@
     )(*args)
 
 
-def field_kernel(first, count, carried, last, *refs):
-    (atoms_ref, pos_ref, blocks_ref, widths_ref, pts_ref, tab_ref), refs = refs[:6], refs[6:]
+def field_kernel(firsts, size, carried, kept, last, *refs):
+    (atoms_ref, pos_ref, blocks_ref, widths_ref, flip_ref, pts_ref), refs = refs[:6], refs[6:]
+    tabs, refs = refs[: len(firsts)], refs[len(firsts) :]
+    count = len(firsts) * size
     if carried:
         acc_in, refs = refs[0], refs[1:]
+    if kept == 2:
+        plane_in, refs = refs[0], refs[1:]
     if last:
-        (
-            phi_ref, w_ref, marks_ref, flip_ref,
-            out_ref, dist_ref, polar_ref, side_ref, scale_ref, acc_ref, oper_ref,
-        ) = refs
+        (phi_ref, w_ref, marks_ref, out_ref), refs = refs[:4], refs[4:]
     else:
-        acc_ref, dist_ref, polar_ref, side_ref, scale_ref = refs
+        acc_ref, refs = refs[0], refs[1:]
+    if kept:
+        plane_ref, refs = refs[0], refs[1:]
+        rows = [tab[flip_ref[2]] for tab in tabs]
+        if kept == 2:
+            rows = [plane_in[0]] + rows
+        for order, value in enumerate(rows):
+            plane_ref[order if len(rows) == 1 else order ^ flip_ref[0]] = value
+    dist_ref, polar_ref, side_ref, scale_ref = refs[:4]
+    if last:
+        acc_ref, oper_ref = refs[4:]
     points = pts_ref.shape[2]
-    prepare(first, count, atoms_ref, pos_ref, pts_ref, dist_ref, polar_ref, side_ref)
+    chosen = [first + k for first in firsts for k in range(size)]
+    prepare(chosen, atoms_ref, pos_ref, pts_ref, dist_ref, polar_ref, side_ref)
     prepare_shells(widths_ref, scale_ref)
     acc_ref[...] = acc_in[...] if carried else jnp.zeros_like(acc_ref)
 
-    def body(k, carry):
-        blocks = blocks_ref[atoms_ref[first + k]]
+    def body(i, carry, tab_ref, first, base):
+        k = base + i
+        blocks = blocks_ref[atoms_ref[first + i]]
 
         def run(live):
             half = live // 2
             middle, scale = shell_columns(blocks, live, scale_ref)
-            table = tab_ref[k].astype(jnp.float32)
+            table = tab_ref[i].astype(jnp.float32)
             lines = []
             for c in range(3):
                 block = table[c * (S // 2) : c * (S // 2) + half]
@@ -230,7 +245,9 @@
         by_live(blocks, run)
         return carry
 
-    lax.fori_loop(0, count, body, 0)
+    for order, first in enumerate(firsts):
+        group = functools.partial(body, tab_ref=tabs[order], first=first, base=order * size)
+        lax.fori_loop(0, size, group, 0)
     if last:
         piece = phi_ref.shape[1] // 2
         third = piece // 3
@@ -265,27 +282,31 @@
                 out_ref[y ^ flip_ref[0], x ^ flip_ref[1]] = packed
 
 
-def field_call(first, count, shared, tables, acc=None, ends=None):
+def field_call(firsts, size, shared, flip, tables, acc=None, plane=None, keep=True, ends=None):
     points = shared[-1].shape[2]
     last = ends is not None
-    args = list(shared) + [tables] + ([] if acc is None else [acc])
-    plain = len(args)
+    count = len(firsts) * size
+    args = list(shared[:-1]) + [flip, shared[-1]] + list(tables)
+    args += [] if acc is None else [acc]
+    args += [] if plane is None else [plane]
     scratch = table_scratch(count, points)
     if last:
         args += ends
         third = ends[0].shape[1] // 6
-        out = jax.ShapeDtypeStruct((2, 2, 7 * third, LANES), jnp.bfloat16)
+        out = [jax.ShapeDtypeStruct((2, 2, 7 * third, LANES), jnp.bfloat16)]
         scratch += [pltpu.VMEM((24, points), jnp.float32), pltpu.VMEM(ends[0].shape[1:], jnp.bfloat16)]
     else:
-        out = jax.ShapeDtypeStruct((24, points), jnp.float32)
-    specs = [SMEM] * 4 + [VMEM] * (plain - 4)
-    if last:
-        specs += [VMEM] * 3 + [SMEM]
+        out = [jax.ShapeDtypeStruct((24, points), jnp.float32)]
+    kept = 0
+    if keep:
+        kept = 1 if plane is None else 2
+        rows = len(firsts) if plane is None else 2
+        out.append(jax.ShapeDtypeStruct((rows,) + tables[0].shape[1:], jnp.bfloat16))
     return pl.pallas_call(
-        functools.partial(field_kernel, first, count, acc is not None, last),
+        functools.partial(field_kernel, firsts, size, acc is not None, kept, last),
         out_shape=out,
-        in_specs=specs,
-        out_specs=VMEM,
+        in_specs=[SMEM] * 5 + [VMEM] * (len(args) - 5),
+        out_specs=[VMEM] * len(out),
         scratch_shapes=scratch,
         cost_estimate=table_cost(count, points),
         name="field",
@@ -367,7 +388,7 @@
         input_output_aliases={} if acc is None or final else {len(stacks): 0},
         compiler_params=pltpu.CompilerParams(vmem_limit_bytes=28 << 20),
         cost_estimate=pl.CostEstimate(
-            flops=2 * 3 * depth * tile * tile, bytes_accessed=12 * tile * tile, transcendentals=0
+            flops=8 * 3 * depth * tile * tile, bytes_accessed=12 * tile * tile, transcendentals=0
         ),
         name="place",
     )(*args)
@@ -452,15 +473,8 @@
             tiled=True,
         )
         beside = swap(own, "row")
-        tables = [own, beside, swap(own, "col"), swap(beside, "col")]
-        here = lax.axis_index("batch")
-        plane = jnp.stack(
-            [lax.dynamic_index_in_dim(table, here, 0, keepdims=False) for table in tables]
-        )
-        places = [(j // sides ^ row) + 2 * (j % sides ^ col) for j in range(holding)]
-        potential = jnp.concatenate(
-            [lax.dynamic_index_in_dim(plane, place, 0) for place in places]
-        ).reshape(holding, width)
+        across = swap(beside, "col")
+        tables = [own, beside, swap(own, "col"), across]
     else:
         moments = jnp.concatenate([moments_of(place, weighted) for place in range(3)] + [third])
         moments = moments.astype(jnp.float32).reshape(count, width)
@@ -504,11 +518,19 @@
     inner = labels.reshape(parts, 3, piece // 3) - jnp.arange(parts)[:, None, None] * tile
     marks = jnp.concatenate([inner // 32, inner % 32, inner[:, :2] * 0], axis=1)
     marks = marks.astype(jnp.float32)
-    field = None
-    for place in (0, 2, 1):
-        field = field_call(place * group, group, shared, tables[place], field)
-    ends = [basis_values, weights, marks, jnp.stack([col, row])]
-    load = field_call(3 * group, group, shared, tables[3], field, ends)
+    flip = jnp.stack([col, row, lax.axis_index("batch")])
+    ends = [basis_values, weights, marks]
+    spread = functools.partial(field_call, size=group, shared=shared, flip=flip, keep=dense)
+    field, *ours = spread((0, 2 * group), tables=[tables[0], tables[2]])
+    field, *half = spread((group,), tables=[tables[1]], acc=field)
+    load, *theirs = spread(
+        (3 * group,), tables=[tables[3]], acc=field, plane=half[0] if half else None, ends=ends
+    )
+    if dense:
+        ours, theirs = ours[0], theirs[0]
+        potential = jnp.concatenate(
+            [jnp.where(row == 0, ours, theirs), jnp.where(row == 0, theirs, ours)]
+        ).reshape(holding, width)
     plane = ("row", "col")
     across = [(i, i ^ 3) for i in range(parts * sides)]
     diagonal = lax.ppermute(load[1, 1:], plane, across)
@@ -516,8 +538,11 @@
         [load[0, :1], swap(load[1, :1], "col"), swap(load[0, 1:], "row"), diagonal], axis=0
     )
     if owners <= 8:
-        near = [plane_load] + [swap(plane_load, "batch", m) for m in range(2, owners, 2)]
-        far = [swap(line, "batch") for line in near]
+        near, far = [plane_load], []
+        for step in range(2, owners, 2):
+            near.append(swap(plane_load, "batch", step))
+        for line in near:
+            far.append(swap(line, "batch"))
         total = None
         for first in range(0, len(near), 2):
             for lines in (near, far):

time: 143 us -> 140 us (0.979)
  waiting for transfers between devices: 33.5 us -> 37 us
  local copies, waits for them, and re-layouts: 10.6 us -> 7.68 us
  Pallas kernels: 67.4 us -> 64.9 us
    ppermute x15, waiting for transfers between devices: 18.6 us -> 21.6 us  [swap(): return lax.ppermute(value, axis, [(i, i ^ mask) for i in range(size)])]
    dynamic_slice x5 -> x0, local copies, waits for them, and re-layouts: 2.96 us -> none  [the longest x4 2.96 us: on_device(): lax.dynamic_index_in_dim(table, here, 0, keepdims=False)]
    pallas_call x4 -> x3, Pallas kernels: 20.6 us -> 18.5 us  [field_call(): pl.pallas_call(functools.partial(field_kernel, firsts, size, acc is not N...]
    unnamed x13 -> x15, local copies, waits for them, and re-layouts: 3.97 us -> 3.92 us
  transfers between devices with their start and end apart: 18 -> 18, of which waited for: 7 -> 8; matrix products, arithmetic and copies ran while one was open for 6% -> 4% of each run, Pallas kernels for 33% -> 32%
where the time goes in v4:
time: 140 us; the launch traced here: 139 us
  Pallas kernels  64.9 us (46%)
  waiting for transfers between devices  37 us (26%)
  starting transfers between devices  22.9 us (16%)
  local copies, waits for them, and re-layouts  7.68 us (5%)
  other arithmetic  5.69 us (4%)
    pallas_call x4, Pallas kernels, place_call(): pl.pallas_call(functools.partial(place_kernel, len(stacks), acc is not No...  27.4 us
    ppermute x15, waiting for transfers between devices, swap(): return lax.ppermute(value, axis, [(i, i ^ mask) for i in range(size)])  21.6 us
    pallas_call x4, Pallas kernels, moments_call(): pl.pallas_call(functools.partial(moments_kernel, first, count, fresh), ou...  18.9 us
    pallas_call x3, Pallas kernels, field_call(): pl.pallas_call(functools.partial(field_kernel, firsts, size, acc is not N...  18.5 us
    ppermute x15, starting transfers between devices, swap(): return lax.ppermute(value, axis, [(i, i ^ mask) for i in range(size)])  13.5 us
    all_to_all x1, waiting for transfers between devices, on_device(): lax.all_to_all(held, 'batch', split_axis=0, concat_axis=0, tiled=True)  7.58 us
    all_to_all x1, waiting for transfers between devices, on_device(): lax.all_to_all(jnp.broadcast_to(mine, (owners, lines, LANES)), 'batch', s...  6.1 us
    all_to_all x1, starting transfers between devices, on_device(): lax.all_to_all(held, 'batch', split_axis=0, concat_axis=0, tiled=True)  5.85 us
  transfers between devices with their start and end apart: 18, of which 8 were waited for; matrix products, arithmetic and copies ran while one was open for 4% of the time, Pallas kernels for 32%

profile of v4, /device:TPU:0, one launch (start us, length us, event | category | flops | bytes accessed | tf_op | source)
XLA Modules:
  0.0 139.2 jit_solution(4072049359917991601)
XLA Ops:
  2.8 5.5 %moments.4 = (bf16[8,96,128]{2,1,0:T(8,128)(2,1)}, f32[3,2048]{1,0:T(4,128)}) custom-call(s32[32]{0:T(128)} %add.51.refs_0_, f32[3,32]{1,0:T(4,128)} %refs_1_.13, s32[32]{0:T(128)} %refs_2_.13, f32[64]{0:T(128)} %refs_3_.13, f32[1,3,2048]{2,1,0:T(4,128)} %copy.26.refs_4_.refs_5_, bf16[1,192,2048]{2,1,0:T(8,128)(2,1)} %refs_9_.1, ...), custom_call_target="tpu_custom_call" | custom-call | flops 402653184 | bytes 1048576 | tf_op jit(solution)/shard_map/moments/pallas_call | solution.py:177
  9.0 4.3 %moments.6 = bf16[8,96,128]{2,1,0:T(8,128)(2,1)} custom-call(s32[32]{0:T(128)} %add.51.refs_0_, f32[3,32]{1,0:T(4,128)} %refs_1_.13, s32[32]{0:T(128)} %refs_2_.13, f32[64]{0:T(128)} %refs_3_.13, f32[1,3,2048]{2,1,0:T(4,128)} %copy.26.refs_4_.refs_5_, f32[3,2048]{1,0:T(4,128)} %get-tuple-element.10.refs_5_), custom_call_target="tpu_custom_call" | custom-call | flops 402653184 | bytes 1048576 | tf_op jit(solution)/shard_map/moments/pallas_call | solution.py:177
  13.6 4.6 %moments.7 = bf16[8,96,128]{2,1,0:T(8,128)(2,1)} custom-call(s32[32]{0:T(128)} %add.51.refs_0_, f32[3,32]{1,0:T(4,128)} %refs_1_.13, s32[32]{0:T(128)} %refs_2_.13, f32[64]{0:T(128)} %refs_3_.13, f32[1,3,2048]{2,1,0:T(4,128)} %copy.26.refs_4_.refs_5_, f32[3,2048]{1,0:T(4,128)} %get-tuple-element.10.refs_5_), custom_call_target="tpu_custom_call" | custom-call | flops 402653184 | bytes 1048576 | tf_op jit(solution)/shard_map/moments/pallas_call | solution.py:177
  19.2 2.8 %collective-permute-start.2 = (bf16[8,96,128]{2,1,0:T(8,128)(2,1)S(1)}, bf16[8,96,128]{2,1,0:T(8,128)(2,1)S(1)}, u32[]{:S(2)}, u32[]{:S(2)}) collective-permute-start(bf16[8,96,128]{2,1,0:T(8,128)(2,1)S(1)} %add.53), channel_id=1, source_target_pairs={{0,2},{2,0},{1,3},{3,1},{4,6},{6,4},{5,7},{7,5},{8,10},{10,8},{9,1... | collective-permute-start | bytes 589832 | tf_op jit(solution)/shard_map/ppermute | solution.py:408
  22.0 4.6 %moments.5 = bf16[8,96,128]{2,1,0:T(8,128)(2,1)} custom-call(s32[32]{0:T(128)} %add.51.refs_0_, f32[3,32]{1,0:T(4,128)} %refs_1_.13, s32[32]{0:T(128)} %refs_2_.13, f32[64]{0:T(128)} %refs_3_.13, f32[1,3,2048]{2,1,0:T(4,128)} %copy.26.refs_4_.refs_5_, f32[3,2048]{1,0:T(4,128)} %get-tuple-element.10.refs_5_), custom_call_target="tpu_custom_call" | custom-call | flops 402653184 | bytes 1048576 | tf_op jit(solution)/shard_map/moments/pallas_call | solution.py:177
  28.5 5.9 %all-to-all-start = ((bf16[8,96,128]{2,1,0:T(8,128)(2,1)}), bf16[8,96,128]{2,1,0:T(8,128)(2,1)S(1)}, u32[]{:S(2)}, u32[]{:S(2)}) async-start(bf16[8,96,128]{2,1,0:T(8,128)(2,1)} %add_convert_fusion), calls=%async_computation | async-start | bytes 393216 | tf_op jit(solution)/shard_map/all_to_all | solution.py:464
  34.6 7.6 %all-to-all-done = bf16[8,96,128]{2,1,0:T(8,128)(2,1)S(1)} async-done(((bf16[8,96,128]{2,1,0:T(8,128)(2,1)}), bf16[8,96,128]{2,1,0:T(8,128)(2,1)S(1)}, u32[]{:S(2)}, u32[]{:S(2)}) %all-to-all-start) | async-done | bytes 196640 | tf_op jit(solution)/shard_map/all_to_all | solution.py:464
  44.3 3.6 %all-to-all-start.1 = ((bf16[8,96,128]{2,1,0:T(8,128)(2,1)}), bf16[8,96,128]{2,1,0:T(8,128)(2,1)S(1)}, u32[]{:S(2)}, u32[]{:S(2)}) async-start(bf16[8,96,128]{2,1,0:T(8,128)(2,1)} %broadcast_in_dim.5), calls=%async_computation.1 | async-start | bytes 393216 | tf_op jit(solution)/shard_map/all_to_all | solution.py:468
  49.3 6.1 %all-to-all-done.1.refs_6_ = bf16[8,96,128]{2,1,0:T(8,128)(2,1)S(1)} async-done(((bf16[8,96,128]{2,1,0:T(8,128)(2,1)}), bf16[8,96,128]{2,1,0:T(8,128)(2,1)S(1)}, u32[]{:S(2)}, u32[]{:S(2)}) %all-to-all-start.1) | async-done | bytes 196640 | tf_op jit(solution)/shard_map/all_to_all | solution.py:468
  55.4 1.7 %collective-permute-start.4 = (bf16[8,96,128]{2,1,0:T(8,128)(2,1)S(1)}, bf16[8,96,128]{2,1,0:T(8,128)(2,1)S(1)}, u32[]{:S(2)}, u32[]{:S(2)}) collective-permute-start(bf16[8,96,128]{2,1,0:T(8,128)(2,1)S(1)} %all-to-all-done.1.refs_6_), channel_id=1, source_target_pairs={{0,2},{2,0},{1,3},{3,1},{4,6},{6,4},{5,7},{7,5},{8,10},{10,8},{9,1... | collective-permute-start | bytes 589832 | tf_op jit(solution)/shard_map/ppermute | solution.py:408
  57.8 4.9 %collective-permute-done.4.refs_6_ = bf16[8,96,128]{2,1,0:T(8,128)(2,1)S(1)} collective-permute-done((bf16[8,96,128]{2,1,0:T(8,128)(2,1)S(1)}, bf16[8,96,128]{2,1,0:T(8,128)(2,1)S(1)}, u32[]{:S(2)}, u32[]{:S(2)}) %collective-permute-start.4) | collective-permute-done | bytes 196640 | tf_op jit(solution)/shard_map/ppermute | solution.py:408
  64.0 7.5 %field.3 = (f32[24,2048]{1,0:T(8,128)}, bf16[2,96,128]{2,1,0:T(8,128)(2,1)}) custom-call(s32[32]{0:T(128)} %add.51.refs_0_, f32[3,32]{1,0:T(4,128)} %refs_1_.13, s32[32]{0:T(128)} %refs_2_.13, f32[64]{0:T(128)} %refs_3_.13, s32[3]{0:T(128)} %pad_add_fusion.refs_4_, f32[1,3,2048]{2,1,0:T(4,128)} %copy.26.refs_4_.refs_5_, bf16[8,96,128]{2,1,0:T(8,128)(2,1)} %copy-done.1, ...), custom_call_target="tpu_custom_call" | custom-call | flops 805306368 | bytes 2097152 | tf_op jit(solution)/shard_map/field/pallas_call | solution.py:305
  71.5 4.8 %field.4 = (f32[24,2048]{1,0:T(8,128)}, bf16[1,96,128]{2,1,0:T(8,128)(2,1)}) custom-call(s32[32]{0:T(128)} %add.51.refs_0_, f32[3,32]{1,0:T(4,128)} %refs_1_.13, s32[32]{0:T(128)} %refs_2_.13, f32[64]{0:T(128)} %refs_3_.13, s32[3]{0:T(128)} %pad_add_fusion.refs_4_, f32[1,3,2048]{2,1,0:T(4,128)} %copy.26.refs_4_.refs_5_, bf16[8,96,128]{2,1,0:T(8,128)(2,1)} %copy-done.3, ...), custom_call_target="tpu_custom_call" | custom-call | flops 402653184 | bytes 1048576 | tf_op jit(solution)/shard_map/field/pallas_call | solution.py:305
  77.0 6.2 %field.5 = (bf16[2,2,224,128]{3,2,1,0:T(8,128)(2,1)}, bf16[2,96,128]{2,1,0:T(8,128)(2,1)}) custom-call(s32[32]{0:T(128)} %add.51.refs_0_, f32[3,32]{1,0:T(4,128)} %refs_1_.13, s32[32]{0:T(128)} %refs_2_.13, f32[64]{0:T(128)} %refs_3_.13, s32[3]{0:T(128)} %pad_add_fusion.refs_4_, f32[1,3,2048]{2,1,0:T(4,128)} %copy.26.refs_4_.refs_5_, ...), custom_call_target="tpu_custom_call" | custom-call | flops 402653184 | bytes 1048576 | tf_op jit(solution)/shard_map/field/pallas_call | solution.py:305
  84.8 1.7 %collective-permute-start.7 = (bf16[1,224,128]{2,1,0:T(8,128)(2,1)S(1)}, bf16[1,224,128]{2,1,0:T(8,128)(2,1)S(1)}, u32[]{:S(2)}, u32[]{:S(2)}) collective-permute-start(bf16[1,224,128]{2,1,0:T(8,128)(2,1)S(1)} %get-tuple-element.20), channel_id=1, source_target_pairs={{0,2},{2,0},{1,3},{3,1},{4,6},{6,4},{5,7},{7,5},{8,10},{10,8},{9,1... | collective-permute-start | bytes 172040 | tf_op jit(solution)/shard_map/ppermute | solution.py:408
  86.4 2.5 %collective-permute-done.7 = bf16[1,224,128]{2,1,0:T(8,128)(2,1)S(1)} collective-permute-done((bf16[1,224,128]{2,1,0:T(8,128)(2,1)S(1)}, bf16[1,224,128]{2,1,0:T(8,128)(2,1)S(1)}, u32[]{:S(2)}, u32[]{:S(2)}) %collective-permute-start.7) | collective-permute-done | bytes 57376 | tf_op jit(solution)/shard_map/ppermute | solution.py:408
  88.9 1.7 %collective-permute-done.8 = bf16[1,224,128]{2,1,0:T(8,128)(2,1)S(1)} collective-permute-done((bf16[1,224,128]{2,1,0:T(8,128)(2,1)S(1)}, bf16[1,224,128]{2,1,0:T(8,128)(2,1)S(1)}, u32[]{:S(2)}, u32[]{:S(2)}) %collective-permute-start.8) | collective-permute-done | bytes 57376 | tf_op jit(solution)/shard_map/ppermute | solution.py:536
  95.8 6.6 %collective-permute-done.14.refs_1_ = bf16[4,224,128]{2,1,0:T(8,128)(2,1)S(1)} collective-permute-done((bf16[4,224,128]{2,1,0:T(8,128)(2,1)S(1)}, bf16[4,224,128]{2,1,0:T(8,128)(2,1)S(1)}, u32[]{:S(2)}, u32[]{:S(2)}) %collective-permute-start.14) | collective-permute-done | bytes 229408 | tf_op jit(solution)/shard_map/ppermute | solution.py:408
  102.4 6.1 %place.4.refs_2_ = f32[3,768,768]{2,1,0:T(8,128)S(1)} custom-call(bf16[4,224,128]{2,1,0:T(8,128)(2,1)S(1)} %pad_maximum_fusion.refs_0_, bf16[4,224,128]{2,1,0:T(8,128)(2,1)S(1)} %collective-permute-done.14.refs_1_), custom_call_target="tpu_custom_call" | custom-call | flops 10871635968 | bytes 7077888 | tf_op jit(solution)/shard_map/place/pallas_call | solution.py:379
  108.5 7.3 %collective-permute-done.9.refs_0_ = bf16[4,224,128]{2,1,0:T(8,128)(2,1)S(1)} collective-permute-done((bf16[4,224,128]{2,1,0:T(8,128)(2,1)S(1)}, bf16[4,224,128]{2,1,0:T(8,128)(2,1)S(1)}, u32[]{:S(2)}, u32[]{:S(2)}) %collective-permute-start.9) | collective-permute-done | bytes 229408 | tf_op jit(solution)/shard_map/ppermute | solution.py:408
  115.8 1.7 %collective-permute-start.10 = (bf16[4,224,128]{2,1,0:T(8,128)(2,1)S(1)}, bf16[4,224,128]{2,1,0:T(8,128)(2,1)S(1)}, u32[]{:S(2)}, u32[]{:S(2)}) collective-permute-start(bf16[4,224,128]{2,1,0:T(8,128)(2,1)S(1)} %collective-permute-done.9.refs_0_), channel_id=1, source_target_pairs={{0,4},{4,0},{8,12},{12,8},{16,20},{20,16},{24,28},{28,24},{1,5},{5... | collective-permute-start | bytes 688136 | tf_op jit(solution)/shard_map/ppermute | solution.py:408
  117.9 6.8 %place.5.refs_2_ = f32[3,768,768]{2,1,0:T(8,128)S(1)} custom-call(bf16[4,224,128]{2,1,0:T(8,128)(2,1)S(1)} %collective-permute-done.13.refs_0_, bf16[4,224,128]{2,1,0:T(8,128)(2,1)S(1)} %collective-permute-done.15.refs_1_, f32[3,768,768]{2,1,0:T(8,128)S(1)} %place.4.refs_2_), custom_call_target="tpu_custom_call", output_to_operand_aliasing={{}: (2, {})} | custom-call | flops 10871635968 | bytes 7077888 | tf_op jit(solution)/shard_map/place/pallas_call | solution.py:379
  124.7 6.6 %place.6.refs_2_ = f32[3,768,768]{2,1,0:T(8,128)S(1)} custom-call(bf16[4,224,128]{2,1,0:T(8,128)(2,1)S(1)} %collective-permute-done.9.refs_0_, bf16[4,224,128]{2,1,0:T(8,128)(2,1)S(1)} %collective-permute-done.11.refs_1_, f32[3,768,768]{2,1,0:T(8,128)S(1)} %place.5.refs_2_), custom_call_target="tpu_custom_call", output_to_operand_aliasing={{}: (2, {})} | custom-call | flops 10871635968 | bytes 7077888 | tf_op jit(solution)/shard_map/place/pallas_call | solution.py:379
  131.3 7.9 %place.7 = bf16[3,768,768]{2,1,0:T(8,128)(2,1)} custom-call(bf16[4,224,128]{2,1,0:T(8,128)(2,1)S(1)} %collective-permute-done.10.refs_0_, bf16[4,224,128]{2,1,0:T(8,128)(2,1)S(1)} %collective-permute-done.12.refs_1_, f32[3,768,768]{2,1,0:T(8,128)S(1)} %place.6.refs_2_), custom_call_target="tpu_custom_call" | custom-call | flops 10871635968 | bytes 7077888 | tf_op jit(solution)/shard_map/place/pallas_call | solution.py:379
  (64 shorter events, 19.4 us)
Async XLA Ops:
  0.6 33.7 %copy-start = (bf16[4,8,4096]{2,1,0:T(8,128)(2,1)S(1)}, bf16[4,8,4096]{2,1,0:T(8,128)(2,1)}, u32[]{:S(2)}) copy-start(bf16[4,8,4096]{2,1,0:T(8,128)(2,1)} %param.18) | copy-start | bytes 786436
  0.6 47.8 %copy-start.2 = (s32[1,192]{1,0:T(1,128)S(1)}, s32[1,192]{1,0:T(1,128)}, u32[]{:S(2)}) copy-start(s32[1,192]{1,0:T(1,128)} %param.14) | copy-start | bytes 2308
  8.2 10.0 %collective-permute-start.1 = (bf16[8,96,128]{2,1,0:T(8,128)(2,1)}, bf16[8,96,128]{2,1,0:T(8,128)(2,1)S(1)}, u32[]{:S(2)}, u32[]{:S(2)}) collective-permute-start(bf16[8,96,128]{2,1,0:T(8,128)(2,1)} %get-tuple-element.11), channel_id=1, source_target_pairs={{0,1},{1,0},{2,3},{3,2},{4,5},{5,4},{6,7},{7,6},{8,9},{9,8},{10,11... | collective-permute-start | bytes 589832 | tf_op jit(solution)/shard_map/ppermute | solution.py:408
  13.4 13.2 %collective-permute-start = (bf16[8,96,128]{2,1,0:T(8,128)(2,1)}, bf16[8,96,128]{2,1,0:T(8,128)(2,1)S(1)}, u32[]{:S(2)}, u32[]{:S(2)}) collective-permute-start(bf16[8,96,128]{2,1,0:T(8,128)(2,1)} %moments.6), channel_id=1, source_target_pairs={{0,1},{1,0},{2,3},{3,2},{4,5},{5,4},{6,7},{7,6},{8,9},{9,8},{10,11... | collective-permute-start | bytes 589832 | tf_op jit(solution)/shard_map/ppermute | solution.py:408
  19.2 7.7 %collective-permute-start.2 = (bf16[8,96,128]{2,1,0:T(8,128)(2,1)S(1)}, bf16[8,96,128]{2,1,0:T(8,128)(2,1)S(1)}, u32[]{:S(2)}, u32[]{:S(2)}) collective-permute-start(bf16[8,96,128]{2,1,0:T(8,128)(2,1)S(1)} %add.53), channel_id=1, source_target_pairs={{0,2},{2,0},{1,3},{3,1},{4,6},{6,4},{5,7},{7,5},{8,10},{10,8},{9,1... | collective-permute-start | bytes 589832 | tf_op jit(solution)/shard_map/ppermute | solution.py:408
  28.5 13.6 %all-to-all-start = ((bf16[8,96,128]{2,1,0:T(8,128)(2,1)}), bf16[8,96,128]{2,1,0:T(8,128)(2,1)S(1)}, u32[]{:S(2)}, u32[]{:S(2)}) async-start(bf16[8,96,128]{2,1,0:T(8,128)(2,1)} %add_convert_fusion), calls=%async_computation | async-start | bytes 393216 | tf_op jit(solution)/shard_map/all_to_all | solution.py:464
  44.3 11.1 %all-to-all-start.1 = ((bf16[8,96,128]{2,1,0:T(8,128)(2,1)}), bf16[8,96,128]{2,1,0:T(8,128)(2,1)S(1)}, u32[]{:S(2)}, u32[]{:S(2)}) async-start(bf16[8,96,128]{2,1,0:T(8,128)(2,1)} %broadcast_in_dim.5), calls=%async_computation.1 | async-start | bytes 393216 | tf_op jit(solution)/shard_map/all_to_all | solution.py:468
  55.4 7.9 %copy-start.1 = (bf16[8,96,128]{2,1,0:T(8,128)(2,1)}, bf16[8,96,128]{2,1,0:T(8,128)(2,1)S(1)}, u32[]{:S(2)}) copy-start(bf16[8,96,128]{2,1,0:T(8,128)(2,1)S(1)} %all-to-all-done.1.refs_6_) | copy-start | bytes 589828
  55.4 7.9 %collective-permute-start.3 = (bf16[8,96,128]{2,1,0:T(8,128)(2,1)S(1)}, bf16[8,96,128]{2,1,0:T(8,128)(2,1)S(1)}, u32[]{:S(2)}, u32[]{:S(2)}) collective-permute-start(bf16[8,96,128]{2,1,0:T(8,128)(2,1)S(1)} %all-to-all-done.1.refs_6_), channel_id=1, source_target_pairs={{0,1},{1,0},{2,3},{3,2},{4,5},{5,4},{6,7},{7,6},{8,9},{9,8},{10,11... | collective-permute-start | bytes 589832 | tf_op jit(solution)/shard_map/ppermute | solution.py:408
  55.4 7.3 %collective-permute-start.4 = (bf16[8,96,128]{2,1,0:T(8,128)(2,1)S(1)}, bf16[8,96,128]{2,1,0:T(8,128)(2,1)S(1)}, u32[]{:S(2)}, u32[]{:S(2)}) collective-permute-start(bf16[8,96,128]{2,1,0:T(8,128)(2,1)S(1)} %all-to-all-done.1.refs_6_), channel_id=1, source_target_pairs={{0,2},{2,0},{1,3},{3,1},{4,6},{6,4},{5,7},{7,5},{8,10},{10,8},{9,1... | collective-permute-start | bytes 589832 | tf_op jit(solution)/shard_map/ppermute | solution.py:408
  62.7 8.8 %copy-start.3 = (bf16[8,96,128]{2,1,0:T(8,128)(2,1)}, bf16[8,96,128]{2,1,0:T(8,128)(2,1)S(1)}, u32[]{:S(2)}) copy-start(bf16[8,96,128]{2,1,0:T(8,128)(2,1)S(1)} %collective-permute-done.4.refs_6_) | copy-start | bytes 589828
  62.7 13.6 %collective-permute-start.5 = (bf16[8,96,128]{2,1,0:T(8,128)(2,1)S(1)}, bf16[8,96,128]{2,1,0:T(8,128)(2,1)S(1)}, u32[]{:S(2)}, u32[]{:S(2)}) collective-permute-start(bf16[8,96,128]{2,1,0:T(8,128)(2,1)S(1)} %collective-permute-done.4.refs_6_), channel_id=1, source_target_pairs={{0,1},{1,0},{2,3},{3,2},{4,5},{5,4},{6,7},{7,6},{8,9},{9,8},{10,11... | collective-permute-start | bytes 589832 | tf_op jit(solution)/shard_map/ppermute | solution.py:408
  63.4 0.7 copy-start.4
  76.3 0.7 copy-start.5
  84.1 2.3 %collective-permute-start.6 = (bf16[1,224,128]{2,1,0:T(8,128)(2,1)S(1)}, bf16[1,224,128]{2,1,0:T(8,128)(2,1)S(1)}, u32[]{:S(2)}, u32[]{:S(2)}) collective-permute-start(bf16[1,224,128]{2,1,0:T(8,128)(2,1)S(1)} %get-tuple-element.21), channel_id=1, source_target_pairs={{0,1},{1,0},{2,3},{3,2},{4,5},{5,4},{6,7},{7,6},{8,9},{9,8},{10,11... | collective-permute-start | bytes 172040 | tf_op jit(solution)/shard_map/ppermute | solution.py:408
  84.8 4.2 %collective-permute-start.7 = (bf16[1,224,128]{2,1,0:T(8,128)(2,1)S(1)}, bf16[1,224,128]{2,1,0:T(8,128)(2,1)S(1)}, u32[]{:S(2)}, u32[]{:S(2)}) collective-permute-start(bf16[1,224,128]{2,1,0:T(8,128)(2,1)S(1)} %get-tuple-element.20), channel_id=1, source_target_pairs={{0,2},{2,0},{1,3},{3,1},{4,6},{6,4},{5,7},{7,5},{8,10},{10,8},{9,1... | collective-permute-start | bytes 172040 | tf_op jit(solution)/shard_map/ppermute | solution.py:408
  86.4 4.2 %collective-permute-start.8 = (bf16[1,224,128]{2,1,0:T(8,128)(2,1)S(1)}, bf16[1,224,128]{2,1,0:T(8,128)(2,1)S(1)}, u32[]{:S(2)}, u32[]{:S(2)}) collective-permute-start(bf16[1,224,128]{2,1,0:T(8,128)(2,1)S(1)} %get-tuple-element.19), channel_id=1, source_target_pairs={{0,3},{1,2},{2,1},{3,0},{4,7},{5,6},{6,5},{7,4},{8,11},{9,10},{10,... | collective-permute-start | bytes 172040 | tf_op jit(solution)/shard_map/ppermute | solution.py:536
  90.7 11.8 %collective-permute-start.14 = (bf16[4,224,128]{2,1,0:T(8,128)(2,1)S(1)}, bf16[4,224,128]{2,1,0:T(8,128)(2,1)S(1)}, u32[]{:S(2)}, u32[]{:S(2)}) collective-permute-start(bf16[4,224,128]{2,1,0:T(8,128)(2,1)S(1)} %pad_maximum_fusion.refs_0_), channel_id=1, source_target_pairs={{0,8},{4,12},{8,0},{12,4},{16,24},{20,28},{24,16},{28,20},{1,9},{5... | collective-permute-start | bytes 688136 | tf_op jit(solution)/shard_map/ppermute | solution.py:408
  92.3 25.5 %collective-permute-start.13 = (bf16[4,224,128]{2,1,0:T(8,128)(2,1)S(1)}, bf16[4,224,128]{2,1,0:T(8,128)(2,1)S(1)}, u32[]{:S(2)}, u32[]{:S(2)}) collective-permute-start(bf16[4,224,128]{2,1,0:T(8,128)(2,1)S(1)} %pad_maximum_fusion.refs_0_), channel_id=1, source_target_pairs={{0,4},{4,0},{8,12},{12,8},{16,20},{20,16},{24,28},{28,24},{1,5},{5... | collective-permute-start | bytes 688136 | tf_op jit(solution)/shard_map/ppermute | solution.py:408
  93.7 23.9 %collective-permute-start.11 = (bf16[4,224,128]{2,1,0:T(8,128)(2,1)S(1)}, bf16[4,224,128]{2,1,0:T(8,128)(2,1)S(1)}, u32[]{:S(2)}, u32[]{:S(2)}) collective-permute-start(bf16[4,224,128]{2,1,0:T(8,128)(2,1)S(1)} %pad_maximum_fusion.refs_0_), channel_id=1, source_target_pairs={{0,24},{4,28},{8,16},{12,20},{16,8},{20,12},{24,0},{28,4},{1,25},{... | collective-permute-start | bytes 688136 | tf_op jit(solution)/shard_map/ppermute | solution.py:408
  94.2 21.6 %collective-permute-start.9 = (bf16[4,224,128]{2,1,0:T(8,128)(2,1)S(1)}, bf16[4,224,128]{2,1,0:T(8,128)(2,1)S(1)}, u32[]{:S(2)}, u32[]{:S(2)}) collective-permute-start(bf16[4,224,128]{2,1,0:T(8,128)(2,1)S(1)} %pad_maximum_fusion.refs_0_), channel_id=1, source_target_pairs={{0,16},{4,20},{8,24},{12,28},{16,0},{20,4},{24,8},{28,12},{1,17},{... | collective-permute-start | bytes 688136 | tf_op jit(solution)/shard_map/ppermute | solution.py:408
  102.4 15.4 %collective-permute-start.15 = (bf16[4,224,128]{2,1,0:T(8,128)(2,1)S(1)}, bf16[4,224,128]{2,1,0:T(8,128)(2,1)S(1)}, u32[]{:S(2)}, u32[]{:S(2)}) collective-permute-start(bf16[4,224,128]{2,1,0:T(8,128)(2,1)S(1)} %collective-permute-done.14.refs_1_), channel_id=1, source_target_pairs={{0,4},{4,0},{8,12},{12,8},{16,20},{20,16},{24,28},{28,24},{1,5},{5... | collective-permute-start | bytes 688136 | tf_op jit(solution)/shard_map/ppermute | solution.py:408
  115.8 15.5 %collective-permute-start.10 = (bf16[4,224,128]{2,1,0:T(8,128)(2,1)S(1)}, bf16[4,224,128]{2,1,0:T(8,128)(2,1)S(1)}, u32[]{:S(2)}, u32[]{:S(2)}) collective-permute-start(bf16[4,224,128]{2,1,0:T(8,128)(2,1)S(1)} %collective-permute-done.9.refs_0_), channel_id=1, source_target_pairs={{0,4},{4,0},{8,12},{12,8},{16,20},{20,16},{24,28},{28,24},{1,5},{5... | collective-permute-start | bytes 688136 | tf_op jit(solution)/shard_map/ppermute | solution.py:408
  117.6 13.7 %collective-permute-start.12 = (bf16[4,224,128]{2,1,0:T(8,128)(2,1)S(1)}, bf16[4,224,128]{2,1,0:T(8,128)(2,1)S(1)}, u32[]{:S(2)}, u32[]{:S(2)}) collective-permute-start(bf16[4,224,128]{2,1,0:T(8,128)(2,1)S(1)} %collective-permute-done.11.refs_1_), channel_id=1, source_target_pairs={{0,4},{4,0},{8,12},{12,8},{16,20},{20,16},{24,28},{28,24},{1,5},{5... | collective-permute-start | bytes 688136 | tf_op jit(solution)/shard_map/ppermute | solution.py:408

commit v5 on v4

--- a/solution.py
+++ b/solution.py
@@ -19,14 +19,24 @@
 VMEM = pl.BlockSpec(memory_space=pltpu.VMEM)
 
 
-def prepare(chosen, atoms_ref, pos_ref, pts_ref, dist_ref, polar_ref, side_ref):
+def atom_finder(group, atoms_ref):
+    if isinstance(group, int):
+        return lambda i: atoms_ref[group + i]
+    stride, row_flip, col_flip = group
+    base = lax.axis_index("col") ^ col_flip
+    if row_flip is not None:
+        base = base + (lax.axis_index("row") ^ row_flip) * 2
+    return lambda i: base + i * stride
+
+
+def prepare(chosen, pos_ref, pts_ref, dist_ref, polar_ref, side_ref):
     count = len(chosen)
     rows = lax.broadcasted_iota(jnp.int32, (count, LANES), 0)
     centre = []
     for axis in range(3):
         column = jnp.zeros((count, LANES), jnp.float32)
-        for k, place in enumerate(chosen):
-            column = jnp.where(rows == k, pos_ref[axis, atoms_ref[place]], column)
+        for k, atom in enumerate(chosen):
+            column = jnp.where(rows == k, pos_ref[axis, atom], column)
         centre.append(column)
     for t in range(pts_ref.shape[2] // LANES):
         here = pl.ds(t * LANES, LANES)
@@ -90,7 +100,7 @@
             run(live)
 
 
-def moments_kernel(first, count, fresh, *refs):
+def moments_kernel(group, count, fresh, *refs):
     if fresh:
         (
             atoms_ref, pos_ref, blocks_ref, widths_ref, pts_ref, phi_ref, dens_ref, w_ref,
@@ -111,11 +121,12 @@
                 product = jnp.dot(dens_ref[0, c], phi, preferred_element_type=jnp.float32)
                 density = jnp.sum(wide * product, axis=0, keepdims=True)
                 wd_ref[pl.ds(c, 1), here] = w_ref[:, here] * density
-    prepare(range(first, first + count), atoms_ref, pos_ref, pts_ref, dist_ref, polar_ref, side_ref)
+    atom_at = atom_finder(group, atoms_ref)
+    prepare([atom_at(i) for i in range(count)], pos_ref, pts_ref, dist_ref, polar_ref, side_ref)
     prepare_shells(widths_ref, scale_ref)
 
     def body(k, carry):
-        blocks = blocks_ref[atoms_ref[first + k]]
+        blocks = blocks_ref[atom_at(k)]
 
         def run(live):
             middle, scale = shell_columns(blocks, live, scale_ref)
@@ -164,7 +175,7 @@
     return pl.CostEstimate(flops=cells * 3 * S * 2, bytes_accessed=cells, transcendentals=cells)
 
 
-def moments_call(first, count, shared, wd=None, phi=None, dens=None, w=None):
+def moments_call(group, count, shared, wd=None, phi=None, dens=None, w=None):
     points = shared[-1].shape[2]
     fresh = wd is None
     out = [jax.ShapeDtypeStruct((count, 3 * S // 2, LANES), jnp.bfloat16)]
@@ -175,7 +186,7 @@
     else:
         args += [wd]
     return pl.pallas_call(
-        functools.partial(moments_kernel, first, count, fresh),
+        functools.partial(moments_kernel, group, count, fresh),
         out_shape=out,
         in_specs=[SMEM] * 4 + [VMEM] * (len(args) - 4),
         out_specs=[VMEM] * len(out),
@@ -185,37 +196,32 @@
     )(*args)
 
 
-def field_kernel(firsts, size, carried, kept, last, *refs):
-    (atoms_ref, pos_ref, blocks_ref, widths_ref, flip_ref, pts_ref), refs = refs[:6], refs[6:]
-    tabs, refs = refs[: len(firsts)], refs[len(firsts) :]
-    count = len(firsts) * size
+def field_kernel(groups, size, carried, kept, last, *refs):
+    (atoms_ref, pos_ref, blocks_ref, widths_ref, pts_ref), refs = refs[:5], refs[5:]
+    tabs, refs = refs[: len(groups)], refs[len(groups) :]
+    count = len(groups) * size
     if carried:
         acc_in, refs = refs[0], refs[1:]
-    if kept == 2:
-        plane_in, refs = refs[0], refs[1:]
     if last:
-        (phi_ref, w_ref, marks_ref, out_ref), refs = refs[:4], refs[4:]
+        (phi_ref, w_ref, marks_ref), outs, refs = refs[:3], refs[3:7], refs[7:]
     else:
         acc_ref, refs = refs[0], refs[1:]
     if kept:
         plane_ref, refs = refs[0], refs[1:]
-        rows = [tab[flip_ref[2]] for tab in tabs]
-        if kept == 2:
-            rows = [plane_in[0]] + rows
-        for order, value in enumerate(rows):
-            plane_ref[order if len(rows) == 1 else order ^ flip_ref[0]] = value
+        for order, tab in enumerate(tabs):
+            plane_ref[order ^ lax.axis_index("col")] = tab[lax.axis_index("batch")]
     dist_ref, polar_ref, side_ref, scale_ref = refs[:4]
     if last:
         acc_ref, oper_ref = refs[4:]
     points = pts_ref.shape[2]
-    chosen = [first + k for first in firsts for k in range(size)]
-    prepare(chosen, atoms_ref, pos_ref, pts_ref, dist_ref, polar_ref, side_ref)
+    finders = [atom_finder(group, atoms_ref) for group in groups]
+    prepare([atom_at(i) for atom_at in finders for i in range(size)], pos_ref, pts_ref, dist_ref, polar_ref, side_ref)
     prepare_shells(widths_ref, scale_ref)
     acc_ref[...] = acc_in[...] if carried else jnp.zeros_like(acc_ref)
 
-    def body(i, carry, tab_ref, first, base):
+    def body(i, carry, tab_ref, atom_at, base):
         k = base + i
-        blocks = blocks_ref[atoms_ref[first + i]]
+        blocks = blocks_ref[atom_at(i)]
 
         def run(live):
             half = live // 2
@@ -245,12 +251,15 @@
         by_live(blocks, run)
         return carry
 
-    for order, first in enumerate(firsts):
-        group = functools.partial(body, tab_ref=tabs[order], first=first, base=order * size)
-        lax.fori_loop(0, size, group, 0)
+    for order, atom_at in enumerate(finders):
+        step = functools.partial(body, tab_ref=tabs[order], atom_at=atom_at, base=order * size)
+        lax.fori_loop(0, size, step, 0)
     if last:
         piece = phi_ref.shape[1] // 2
         third = piece // 3
+        sides = (lax.axis_index("row"), lax.axis_index("col"))
+        halves = [[flip ^ side for flip in range(2)] for side in sides]
+        spans = [[pl.ds(pl.multiple_of(h * piece, 32), piece) for h in pair] for pair in halves]
         quads = {}
         for c in range(3):
             for start in range(0, points, 256):
@@ -261,51 +270,44 @@
             for x in range(2):
                 for y in range(2):
                     quads[c, x, y] = lax.dot_general(
-                        oper_ref[pl.ds(x * piece, piece), :],
-                        phi_ref[0, pl.ds(y * piece, piece), :],
+                        oper_ref[spans[0][x], :],
+                        phi_ref[0, spans[1][y], :],
                         NT,
                         preferred_element_type=jnp.float32,
                     )
         for x in range(2):
             for y in range(2):
                 q0, q1, q2 = (quads[c, x, y] for c in range(3))
-                marks = jnp.concatenate(
-                    [marks_ref[x], marks_ref[y], jnp.zeros((third - 16, third), jnp.float32)], axis=0
-                )
+                marks = [marks_ref[halves[0][x]], marks_ref[halves[1][y]]]
+                marks = jnp.concatenate(marks + [jnp.zeros((third - 16, third), jnp.float32)], axis=0)
                 parts = [q2[b * third : (b + 1) * third, 2 * third :] for b in range(3)] + [marks]
                 blocks = [
                     jnp.concatenate([q0, q2[:, :third]], axis=1),
                     jnp.concatenate([q1, q2[:, third : 2 * third]], axis=1),
                     jnp.concatenate(parts, axis=1),
                 ]
-                packed = jnp.concatenate(blocks, axis=0).astype(jnp.bfloat16)
-                out_ref[y ^ flip_ref[0], x ^ flip_ref[1]] = packed
-
-
-def field_call(firsts, size, shared, flip, tables, acc=None, plane=None, keep=True, ends=None):
+                outs[2 * y + x][0] = jnp.concatenate(blocks, axis=0).astype(jnp.bfloat16)
+
+
+def field_call(groups, size, shared, tables, acc=None, keep=True, ends=None):
     points = shared[-1].shape[2]
     last = ends is not None
-    count = len(firsts) * size
-    args = list(shared[:-1]) + [flip, shared[-1]] + list(tables)
-    args += [] if acc is None else [acc]
-    args += [] if plane is None else [plane]
+    count = len(groups) * size
+    args = list(shared) + list(tables) + ([] if acc is None else [acc])
     scratch = table_scratch(count, points)
     if last:
         args += ends
         third = ends[0].shape[1] // 6
-        out = [jax.ShapeDtypeStruct((2, 2, 7 * third, LANES), jnp.bfloat16)]
+        out = [jax.ShapeDtypeStruct((1, 7 * third, LANES), jnp.bfloat16)] * 4
         scratch += [pltpu.VMEM((24, points), jnp.float32), pltpu.VMEM(ends[0].shape[1:], jnp.bfloat16)]
     else:
         out = [jax.ShapeDtypeStruct((24, points), jnp.float32)]
-    kept = 0
     if keep:
-        kept = 1 if plane is None else 2
-        rows = len(firsts) if plane is None else 2
-        out.append(jax.ShapeDtypeStruct((rows,) + tables[0].shape[1:], jnp.bfloat16))
+        out.append(jax.ShapeDtypeStruct((len(groups),) + tables[0].shape[1:], jnp.bfloat16))
     return pl.pallas_call(
-        functools.partial(field_kernel, firsts, size, acc is not None, kept, last),
+        functools.partial(field_kernel, groups, size, acc is not None, keep, last),
         out_shape=out,
-        in_specs=[SMEM] * 5 + [VMEM] * (len(args) - 5),
+        in_specs=[SMEM] * 4 + [VMEM] * (len(args) - 4),
         out_specs=[VMEM] * len(out),
         scratch_shapes=scratch,
         cost_estimate=table_cost(count, points),
@@ -408,12 +410,6 @@
     return lax.ppermute(value, axis, [(i, i ^ mask) for i in range(size)])
 
 
-def plane_atoms(owners, row, col):
-    flips = jnp.arange(4)
-    inner = ((flips & 1) ^ row) * 2 + ((flips >> 1) ^ col)
-    return (jnp.arange(owners)[None, :] * 4 + inner[:, None]).reshape(-1)
-
-
 def on_device(
     basis_values,
     density_matrix,
@@ -440,28 +436,20 @@
     lines = width // LANES
     highest = lax.Precision.HIGHEST
     dense = count == every_atom and holding == parts * sides
+    plane = ("row", "col")
+    across = [(i, i ^ 3) for i in range(parts * sides)]
+    half, group = count // 2, count // 4
+    shared = (atoms, atom_positions, shell_blocks, shell_widths, points)
+    wanted = ((sides, None, 0), (sides, None, 1)) if dense else (0, half)
+    listed = [(holding, f & 1, f >> 1) if dense else f * group for f in range(4)]
+    other, weighted = moments_call(
+        wanted[1], half, shared, phi=basis_values, dens=density_matrix, w=weights
+    )
+    mate = swap(other, "col") if dense else other
+    first = moments_call(wanted[0], half, shared, wd=weighted)[0]
     if dense:
-        atoms = plane_atoms(owners, row, col)
-    group = count // 4
-    shared = (atoms, atom_positions, shell_blocks, shell_widths, points)
-
-    def moments_of(place, weighted):
-        return moments_call(place * group, group, shared, wd=weighted)[0]
-
-    third, weighted = moments_call(
-        3 * group, group, shared, phi=basis_values, dens=density_matrix, w=weights
-    )
-    if dense:
-        from_third = swap(third, "col")
-        first = moments_of(1, weighted) + from_third
-        from_first = swap(first, "row")
-        from_second = swap(moments_of(2, weighted), "col")
-        held = (
-            moments_of(0, weighted).astype(jnp.float32)
-            + from_second.astype(jnp.float32)
-            + from_first.astype(jnp.float32)
-        ).astype(jnp.bfloat16)
-        shares = lax.all_to_all(held, "batch", split_axis=0, concat_axis=0, tiled=True)
+        held = first + mate
+        shares = lax.all_to_all(held, ("batch", "row"), split_axis=0, concat_axis=0, tiled=True)
         charges = jnp.sum(shares.astype(jnp.float32), axis=0)
         kernels = lax.dynamic_index_in_dim(green, row * sides + col, 0, keepdims=True)
         mine = apply_green(charges.reshape(1, width), kernels).reshape(1, lines, LANES)
@@ -473,10 +461,10 @@
             tiled=True,
         )
         beside = swap(own, "row")
-        across = swap(beside, "col")
-        tables = [own, beside, swap(own, "col"), across]
+        beyond = lax.ppermute(own, plane, across)
+        tables = [own, beside, swap(own, "col"), beyond]
     else:
-        moments = jnp.concatenate([moments_of(place, weighted) for place in range(3)] + [third])
+        moments = jnp.concatenate([first, other])
         moments = moments.astype(jnp.float32).reshape(count, width)
         home = atoms // holding
         local_slot = atoms % holding
@@ -518,36 +506,28 @@
     inner = labels.reshape(parts, 3, piece // 3) - jnp.arange(parts)[:, None, None] * tile
     marks = jnp.concatenate([inner // 32, inner % 32, inner[:, :2] * 0], axis=1)
     marks = marks.astype(jnp.float32)
-    flip = jnp.stack([col, row, lax.axis_index("batch")])
     ends = [basis_values, weights, marks]
-    spread = functools.partial(field_call, size=group, shared=shared, flip=flip, keep=dense)
-    field, *ours = spread((0, 2 * group), tables=[tables[0], tables[2]])
-    field, *half = spread((group,), tables=[tables[1]], acc=field)
-    load, *theirs = spread(
-        (3 * group,), tables=[tables[3]], acc=field, plane=half[0] if half else None, ends=ends
-    )
+    spread = functools.partial(field_call, size=group, shared=shared, keep=dense)
+    field, *ours = spread((listed[0], listed[2]), tables=[tables[0], tables[2]])
+    load = spread((listed[1], listed[3]), tables=[tables[1], tables[3]], acc=field, ends=ends)
     if dense:
-        ours, theirs = ours[0], theirs[0]
+        ours, theirs = ours[0], load[4]
         potential = jnp.concatenate(
             [jnp.where(row == 0, ours, theirs), jnp.where(row == 0, theirs, ours)]
         ).reshape(holding, width)
-    plane = ("row", "col")
-    across = [(i, i ^ 3) for i in range(parts * sides)]
-    diagonal = lax.ppermute(load[1, 1:], plane, across)
-    plane_load = jnp.concatenate(
-        [load[0, :1], swap(load[1, :1], "col"), swap(load[0, 1:], "row"), diagonal], axis=0
-    )
+    got = [swap(load[2], "col"), swap(load[1], "row"), lax.ppermute(load[3], plane, across)]
+    plane_load = jnp.concatenate([load[0]] + got, axis=0)
     if owners <= 8:
         near, far = [plane_load], []
         for step in range(2, owners, 2):
             near.append(swap(plane_load, "batch", step))
         for line in near:
             far.append(swap(line, "batch"))
+        stages = [near[:1], far[:1] + near[1:2], far[1:2], near[2:], far[2:]]
+        stages = [lines for lines in stages if lines]
         total = None
-        for first in range(0, len(near), 2):
-            for lines in (near, far):
-                last = lines is far and first + 2 >= len(near)
-                total = place_call(lines[first : first + 2], piece, tile, total, final=last)
+        for order, lines in enumerate(stages):
+            total = place_call(lines, piece, tile, total, final=lines is stages[-1])
         hamiltonian = total
     else:
         everyone = lax.all_gather(plane_load, "batch", axis=0)

time: 140 us -> 132 us (0.943)
  the two profiles are of different devices: /device:TPU:0 before, /device:TPU:8 now
where the time goes in v5:
time: 132 us; the launch traced here: 131 us
  Pallas kernels  63.6 us (48%)
  waiting for transfers between devices  32.6 us (25%)
  starting transfers between devices  22.9 us (17%)
  local copies, waits for them, and re-layouts  7.01 us (5%)
  other arithmetic  4.16 us (3%)
    pallas_call x5, Pallas kernels, place_call(): pl.pallas_call(functools.partial(place_kernel, len(stacks), acc is not No...  30.1 us
    pallas_call x2, Pallas kernels, field_call(): pl.pallas_call(functools.partial(field_kernel, groups, size, acc is not N...  17.1 us
    pallas_call x2, Pallas kernels, moments_call(): pl.pallas_call(functools.partial(moments_kernel, group, count, fresh), ou...  16.4 us
    ppermute x12, waiting for transfers between devices, swap(): return lax.ppermute(value, axis, [(i, i ^ mask) for i in range(size)])  16.4 us
    all_to_all x1, waiting for transfers between devices, on_device(): lax.all_to_all(held, ('batch', 'row'), split_axis=0, concat_axis=0, tiled...  11.3 us
    ppermute x12, starting transfers between devices, swap(): return lax.ppermute(value, axis, [(i, i ^ mask) for i in range(size)])  9.05 us
    all_to_all x1, starting transfers between devices, on_device(): lax.all_to_all(held, ('batch', 'row'), split_axis=0, concat_axis=0, tiled...  7.23 us
    unnamed x18, local copies, waits for them, and re-layouts  4.82 us
  transfers between devices with their start and end apart: 16, of which 7 were waited for; matrix products, arithmetic and copies ran while one was open for 4% of the time, Pallas kernels for 29%

profile of v5, /device:TPU:8, one launch (start us, length us, event | category | flops | bytes accessed | tf_op | source)
XLA Modules:
  0.0 131.3 jit_solution(1581855906747933089)
XLA Ops:
  0.7 1.4 %copy.23.refs_4_ = f32[1,3,2048]{2,1,0:T(4,128)} copy(f32[1,3,2048]{2,0,1:T(1,128)} %param.12) | data formatting | bytes 49152 | tf_op args[2]
  2.1 8.5 %moments.2 = (bf16[16,96,128]{2,1,0:T(8,128)(2,1)}, f32[3,2048]{1,0:T(4,128)}) custom-call(s32[32]{0:T(128)} %bitcast.16, f32[3,32]{1,0:T(4,128)} %refs_1_.7, s32[32]{0:T(128)} %refs_2_.7, f32[64]{0:T(128)} %refs_3_.7, f32[1,3,2048]{2,1,0:T(4,128)} %copy.23.refs_4_, bf16[1,192,2048]{2,1,0:T(8,128)(2,1)} %refs_8_.1, bf16[1,3,192,192]{3,2,1,0:T(8,128)(2,1)} %refs_6_.1, ...), custom_call_target="tpu_custom_call" | custom-call | flops 805306368 | bytes 2097152 | tf_op jit(solution)/shard_map/moments/pallas_call | solution.py:188
  11.0 7.9 %moments.3 = bf16[16,96,128]{2,1,0:T(8,128)(2,1)} custom-call(s32[32]{0:T(128)} %bitcast.17, f32[3,32]{1,0:T(4,128)} %refs_1_.7, s32[32]{0:T(128)} %refs_2_.7, f32[64]{0:T(128)} %refs_3_.7, f32[1,3,2048]{2,1,0:T(4,128)} %copy.23.refs_4_, f32[3,2048]{1,0:T(4,128)} %get-tuple-element.11.refs_5_), custom_call_target="tpu_custom_call" | custom-call | flops 805306368 | bytes 2097152 | tf_op jit(solution)/shard_map/moments/pallas_call | solution.py:188
  18.9 1.8 %add.17 = bf16[16,96,128]{2,1,0:T(8,128)(2,1)} add(bf16[16,96,128]{2,1,0:T(8,128)(2,1)} %moments.3, bf16[16,96,128]{2,1,0:T(8,128)(2,1)S(1)} %collective-permute-done) | non-fusion elementwise | flops 196608 | bytes 1179648 | tf_op jit(solution)/shard_map/add | solution.py:451
  20.8 7.2 %all-to-all-start = ((bf16[16,96,128]{2,1,0:T(8,128)(2,1)}), bf16[16,96,128]{2,1,0:T(8,128)(2,1)S(1)}, u32[]{:S(2)}, u32[]{:S(2)}) async-start(bf16[16,96,128]{2,1,0:T(8,128)(2,1)} %add.17), calls=%async_computation | async-start | bytes 786432 | tf_op jit(solution)/shard_map/all_to_all | solution.py:452
  28.2 11.3 %all-to-all-done = bf16[16,96,128]{2,1,0:T(8,128)(2,1)S(1)} async-done(((bf16[16,96,128]{2,1,0:T(8,128)(2,1)}), bf16[16,96,128]{2,1,0:T(8,128)(2,1)S(1)}, u32[]{:S(2)}, u32[]{:S(2)}) %all-to-all-start) | async-done | bytes 393248 | tf_op jit(solution)/shard_map/all_to_all | solution.py:452
  41.6 4.4 %all-to-all-start.1 = ((bf16[8,96,128]{2,1,0:T(8,128)(2,1)}), bf16[8,96,128]{2,1,0:T(8,128)(2,1)S(1)}, u32[]{:S(2)}, u32[]{:S(2)}) async-start(bf16[8,96,128]{2,1,0:T(8,128)(2,1)} %broadcast_in_dim.9), calls=%async_computation.1 | async-start | bytes 393216 | tf_op jit(solution)/shard_map/all_to_all | solution.py:456
  47.5 4.4 %all-to-all-done.1.refs_5_ = bf16[8,96,128]{2,1,0:T(8,128)(2,1)S(1)} async-done(((bf16[8,96,128]{2,1,0:T(8,128)(2,1)}), bf16[8,96,128]{2,1,0:T(8,128)(2,1)S(1)}, u32[]{:S(2)}, u32[]{:S(2)}) %all-to-all-start.1) | async-done | bytes 196640 | tf_op jit(solution)/shard_map/all_to_all | solution.py:456
  52.4 1.3 collective-permute-start.3
  55.1 7.5 %field.2 = (f32[24,2048]{1,0:T(8,128)}, bf16[2,96,128]{2,1,0:T(8,128)(2,1)}) custom-call(s32[32]{0:T(128)} %bitcast.18, f32[3,32]{1,0:T(4,128)} %refs_1_.7, s32[32]{0:T(128)} %refs_2_.7, f32[64]{0:T(128)} %refs_3_.7, f32[1,3,2048]{2,1,0:T(4,128)} %copy.23.refs_4_, bf16[8,96,128]{2,1,0:T(8,128)(2,1)} %copy-done.1, bf16[8,96,128]{2,1,0:T(8,128)(2,1)} %copy-done.5), custom_call_target="tpu_custom_call" | custom-call | flops 805306368 | bytes 2097152 | tf_op jit(solution)/shard_map/field/pallas_call | solution.py:307
  63.6 9.5 %field.3 = (bf16[1,224,128]{2,1,0:T(8,128)(2,1)}, bf16[1,224,128]{2,1,0:T(8,128)(2,1)}, bf16[1,224,128]{2,1,0:T(8,128)(2,1)}, bf16[1,224,128]{2,1,0:T(8,128)(2,1)}, bf16[2,96,128]{2,1,0:T(8,128)(2,1)}) custom-call(s32[32]{0:T(128)} %bitcast.19, f32[3,32]{1,0:T(4,128)} %refs_1_.7, s32[32]{0:T(128)} %refs_2_.7, f32[64]{0:T(128)} %refs_3_.7, ...), custom_call_target="tpu_custom_call" | custom-call | flops 805306368 | bytes 2097152 | tf_op jit(solution)/shard_map/field/pallas_call | solution.py:307
  74.1 0.9 collective-permute-start.6
  77.4 0.9 collective-permute-done.5
  78.6 2.0 %collective-permute-start.11 = (bf16[4,224,128]{2,1,0:T(8,128)(2,1)S(1)}, bf16[4,224,128]{2,1,0:T(8,128)(2,1)S(1)}, u32[]{:S(2)}, u32[]{:S(2)}) collective-permute-start(bf16[4,224,128]{2,1,0:T(8,128)(2,1)S(1)} %constant_dynamic-update-slice_fusion.refs_0_), channel_id=1, source_target_pairs={{0,8},{4,12},{8,0},{12,4},{16,24},{20,28},{24,16},{28,20},{1,9},{5... | collective-permute-start | bytes 688136 | tf_op jit(solution)/shard_map/ppermute | solution.py:410
  81.4 2.0 %collective-permute-start.9 = (bf16[4,224,128]{2,1,0:T(8,128)(2,1)S(1)}, bf16[4,224,128]{2,1,0:T(8,128)(2,1)S(1)}, u32[]{:S(2)}, u32[]{:S(2)}) collective-permute-start(bf16[4,224,128]{2,1,0:T(8,128)(2,1)S(1)} %constant_dynamic-update-slice_fusion.refs_0_), channel_id=1, source_target_pairs={{0,24},{4,28},{8,16},{12,20},{16,8},{20,12},{24,0},{28,4},{1,25},{... | collective-permute-start | bytes 688136 | tf_op jit(solution)/shard_map/ppermute | solution.py:410
  83.5 4.3 %place.5.refs_2_ = f32[3,768,768]{2,1,0:T(8,128)S(1)} custom-call(bf16[4,224,128]{2,1,0:T(8,128)(2,1)S(1)} %constant_dynamic-update-slice_fusion.refs_0_), custom_call_target="tpu_custom_call" | custom-call | flops 5435817984 | bytes 7077888 | tf_op jit(solution)/shard_map/place/pallas_call | solution.py:381
  87.8 1.2 collective-permute-done.11.refs_1_
  89.2 14.3 %collective-permute-done.9.refs_1_ = bf16[4,224,128]{2,1,0:T(8,128)(2,1)S(1)} collective-permute-done((bf16[4,224,128]{2,1,0:T(8,128)(2,1)S(1)}, bf16[4,224,128]{2,1,0:T(8,128)(2,1)S(1)}, u32[]{:S(2)}, u32[]{:S(2)}) %collective-permute-start.9) | collective-permute-done | bytes 229408 | tf_op jit(solution)/shard_map/ppermute | solution.py:410
  103.5 1.0 collective-permute-start.10
  104.5 1.0 collective-permute-start.8
  105.5 6.6 %place.6.refs_1_ = f32[3,768,768]{2,1,0:T(8,128)S(1)} custom-call(bf16[4,224,128]{2,1,0:T(8,128)(2,1)S(1)} %collective-permute-done.13.refs_0_, bf16[4,224,128]{2,1,0:T(8,128)(2,1)S(1)} %collective-permute-done.11.refs_1_, f32[3,768,768]{2,1,0:T(8,128)S(1)} %place.5.refs_2_), custom_call_target="tpu_custom_call", output_to_operand_aliasing={{}: (2, {})} | custom-call | flops 10871635968 | bytes 7077888 | tf_op jit(solution)/shard_map/place/pallas_call | solution.py:381
  112.1 4.7 %place.7.refs_2_ = f32[3,768,768]{2,1,0:T(8,128)S(1)} custom-call(bf16[4,224,128]{2,1,0:T(8,128)(2,1)S(1)} %collective-permute-done.12.refs_0_, f32[3,768,768]{2,1,0:T(8,128)S(1)} %place.6.refs_1_), custom_call_target="tpu_custom_call", output_to_operand_aliasing={{}: (1, {})} | custom-call | flops 5435817984 | bytes 7077888 | tf_op jit(solution)/shard_map/place/pallas_call | solution.py:381
  116.8 6.6 %place.8.refs_2_ = f32[3,768,768]{2,1,0:T(8,128)S(1)} custom-call(bf16[4,224,128]{2,1,0:T(8,128)(2,1)S(1)} %collective-permute-done.7.refs_0_, bf16[4,224,128]{2,1,0:T(8,128)(2,1)S(1)} %collective-permute-done.9.refs_1_, f32[3,768,768]{2,1,0:T(8,128)S(1)} %place.7.refs_2_), custom_call_target="tpu_custom_call", output_to_operand_aliasing={{}: (2, {})} | custom-call | flops 10871635968 | bytes 7077888 | tf_op jit(solution)/shard_map/place/pallas_call | solution.py:381
  123.4 7.9 %place.9 = bf16[3,768,768]{2,1,0:T(8,128)(2,1)} custom-call(bf16[4,224,128]{2,1,0:T(8,128)(2,1)S(1)} %collective-permute-done.8.refs_0_, bf16[4,224,128]{2,1,0:T(8,128)(2,1)S(1)} %collective-permute-done.10.refs_1_, f32[3,768,768]{2,1,0:T(8,128)S(1)} %place.8.refs_2_), custom_call_target="tpu_custom_call" | custom-call | flops 10871635968 | bytes 7077888 | tf_op jit(solution)/shard_map/place/pallas_call | solution.py:381
  (54 shorter events, 11.7 us)
Async XLA Ops:
  0.6 27.4 %copy-start = (bf16[4,8,4096]{2,1,0:T(8,128)(2,1)S(1)}, bf16[4,8,4096]{2,1,0:T(8,128)(2,1)}, u32[]{:S(2)}) copy-start(bf16[4,8,4096]{2,1,0:T(8,128)(2,1)} %param.19) | copy-start | bytes 786436
  0.6 45.9 %copy-start.2 = (s32[1,192]{1,0:T(1,128)S(1)}, s32[1,192]{1,0:T(1,128)}, u32[]{:S(2)}) copy-start(s32[1,192]{1,0:T(1,128)} %param.15) | copy-start | bytes 2308
  10.6 8.3 %collective-permute-start = (bf16[16,96,128]{2,1,0:T(8,128)(2,1)}, bf16[16,96,128]{2,1,0:T(8,128)(2,1)S(1)}, u32[]{:S(2)}, u32[]{:S(2)}) collective-permute-start(bf16[16,96,128]{2,1,0:T(8,128)(2,1)} %get-tuple-element.12), channel_id=1, source_target_pairs={{0,1},{1,0},{2,3},{3,2},{4,5},{5,4},{6,7},{7,6},{8,9},{9,8},{10,11... | collective-permute-start | bytes 1179656 | tf_op jit(solution)/shard_map/ppermute | solution.py:410
  20.8 18.7 %all-to-all-start = ((bf16[16,96,128]{2,1,0:T(8,128)(2,1)}), bf16[16,96,128]{2,1,0:T(8,128)(2,1)S(1)}, u32[]{:S(2)}, u32[]{:S(2)}) async-start(bf16[16,96,128]{2,1,0:T(8,128)(2,1)} %add.17), calls=%async_computation | async-start | bytes 786432 | tf_op jit(solution)/shard_map/all_to_all | solution.py:452
  41.6 10.2 %all-to-all-start.1 = ((bf16[8,96,128]{2,1,0:T(8,128)(2,1)}), bf16[8,96,128]{2,1,0:T(8,128)(2,1)S(1)}, u32[]{:S(2)}, u32[]{:S(2)}) async-start(bf16[8,96,128]{2,1,0:T(8,128)(2,1)} %broadcast_in_dim.9), calls=%async_computation.1 | async-start | bytes 393216 | tf_op jit(solution)/shard_map/all_to_all | solution.py:456
  51.9 2.5 %copy-start.1 = (bf16[8,96,128]{2,1,0:T(8,128)(2,1)}, bf16[8,96,128]{2,1,0:T(8,128)(2,1)S(1)}, u32[]{:S(2)}) copy-start(bf16[8,96,128]{2,1,0:T(8,128)(2,1)S(1)} %all-to-all-done.1.refs_5_) | copy-start | bytes 589828
  51.9 2.5 %collective-permute-start.1 = (bf16[8,96,128]{2,1,0:T(8,128)(2,1)S(1)}, bf16[8,96,128]{2,1,0:T(8,128)(2,1)S(1)}, u32[]{:S(2)}, u32[]{:S(2)}) collective-permute-start(bf16[8,96,128]{2,1,0:T(8,128)(2,1)S(1)} %all-to-all-done.1.refs_5_), channel_id=1, source_target_pairs={{0,1},{1,0},{2,3},{3,2},{4,5},{5,4},{6,7},{7,6},{8,9},{9,8},{10,11... | collective-permute-start | bytes 589832 | tf_op jit(solution)/shard_map/ppermute | solution.py:410
  51.9 10.8 %collective-permute-start.2 = (bf16[8,96,128]{2,1,0:T(8,128)(2,1)S(1)}, bf16[8,96,128]{2,1,0:T(8,128)(2,1)S(1)}, u32[]{:S(2)}, u32[]{:S(2)}) collective-permute-start(bf16[8,96,128]{2,1,0:T(8,128)(2,1)S(1)} %all-to-all-done.1.refs_5_), channel_id=1, source_target_pairs={{0,2},{2,0},{1,3},{3,1},{4,6},{6,4},{5,7},{7,5},{8,10},{10,8},{9,1... | collective-permute-start | bytes 589832 | tf_op jit(solution)/shard_map/ppermute | solution.py:410
  52.4 10.5 %collective-permute-start.3 = (bf16[8,96,128]{2,1,0:T(8,128)(2,1)S(1)}, bf16[8,96,128]{2,1,0:T(8,128)(2,1)S(1)}, u32[]{:S(2)}, u32[]{:S(2)}) collective-permute-start(bf16[8,96,128]{2,1,0:T(8,128)(2,1)S(1)} %all-to-all-done.1.refs_5_), channel_id=1, source_target_pairs={{0,3},{1,2},{2,1},{3,0},{4,7},{5,6},{6,5},{7,4},{8,11},{9,10},{10,... | collective-permute-start | bytes 589832 | tf_op jit(solution)/shard_map/ppermute | solution.py:464
  54.4 0.7 copy-start.5
  62.6 0.7 copy-start.3
  62.9 0.7 copy-start.4
  73.1 4.2 %collective-permute-start.4 = (bf16[1,224,128]{2,1,0:T(8,128)(2,1)}, bf16[1,224,128]{2,1,0:T(8,128)(2,1)S(1)}, u32[]{:S(2)}, u32[]{:S(2)}) collective-permute-start(bf16[1,224,128]{2,1,0:T(8,128)(2,1)} %get-tuple-element.17), channel_id=1, source_target_pairs={{0,1},{1,0},{2,3},{3,2},{4,5},{5,4},{6,7},{7,6},{8,9},{9,8},{10,11... | collective-permute-start | bytes 172040 | tf_op jit(solution)/shard_map/ppermute | solution.py:410
  73.4 4.9 %collective-permute-start.5 = (bf16[1,224,128]{2,1,0:T(8,128)(2,1)}, bf16[1,224,128]{2,1,0:T(8,128)(2,1)S(1)}, u32[]{:S(2)}, u32[]{:S(2)}) collective-permute-start(bf16[1,224,128]{2,1,0:T(8,128)(2,1)} %get-tuple-element.18), channel_id=1, source_target_pairs={{0,2},{2,0},{1,3},{3,1},{4,6},{6,4},{5,7},{7,5},{8,10},{10,8},{9,1... | collective-permute-start | bytes 172040 | tf_op jit(solution)/shard_map/ppermute | solution.py:410
  74.1 4.4 %collective-permute-start.6 = (bf16[1,224,128]{2,1,0:T(8,128)(2,1)}, bf16[1,224,128]{2,1,0:T(8,128)(2,1)S(1)}, u32[]{:S(2)}, u32[]{:S(2)}) collective-permute-start(bf16[1,224,128]{2,1,0:T(8,128)(2,1)} %get-tuple-element.19), channel_id=1, source_target_pairs={{0,3},{1,2},{2,1},{3,0},{4,7},{5,6},{6,5},{7,4},{8,11},{9,10},{10,... | collective-permute-start | bytes 172040 | tf_op jit(solution)/shard_map/ppermute | solution.py:518
  78.6 10.5 %collective-permute-start.11 = (bf16[4,224,128]{2,1,0:T(8,128)(2,1)S(1)}, bf16[4,224,128]{2,1,0:T(8,128)(2,1)S(1)}, u32[]{:S(2)}, u32[]{:S(2)}) collective-permute-start(bf16[4,224,128]{2,1,0:T(8,128)(2,1)S(1)} %constant_dynamic-update-slice_fusion.refs_0_), channel_id=1, source_target_pairs={{0,8},{4,12},{8,0},{12,4},{16,24},{20,28},{24,16},{28,20},{1,9},{5... | collective-permute-start | bytes 688136 | tf_op jit(solution)/shard_map/ppermute | solution.py:410
  80.6 24.9 %collective-permute-start.13 = (bf16[4,224,128]{2,1,0:T(8,128)(2,1)S(1)}, bf16[4,224,128]{2,1,0:T(8,128)(2,1)S(1)}, u32[]{:S(2)}, u32[]{:S(2)}) collective-permute-start(bf16[4,224,128]{2,1,0:T(8,128)(2,1)S(1)} %constant_dynamic-update-slice_fusion.refs_0_), channel_id=1, source_target_pairs={{0,4},{4,0},{8,12},{12,8},{16,20},{20,16},{24,28},{28,24},{1,5},{5... | collective-permute-start | bytes 688136 | tf_op jit(solution)/shard_map/ppermute | solution.py:410
  81.4 23.0 %collective-permute-start.7 = (bf16[4,224,128]{2,1,0:T(8,128)(2,1)S(1)}, bf16[4,224,128]{2,1,0:T(8,128)(2,1)S(1)}, u32[]{:S(2)}, u32[]{:S(2)}) collective-permute-start(bf16[4,224,128]{2,1,0:T(8,128)(2,1)S(1)} %constant_dynamic-update-slice_fusion.refs_0_), channel_id=1, source_target_pairs={{0,16},{4,20},{8,24},{12,28},{16,0},{20,4},{24,8},{28,12},{1,17},{... | collective-permute-start | bytes 688136 | tf_op jit(solution)/shard_map/ppermute | solution.py:410
  81.4 22.0 %collective-permute-start.9 = (bf16[4,224,128]{2,1,0:T(8,128)(2,1)S(1)}, bf16[4,224,128]{2,1,0:T(8,128)(2,1)S(1)}, u32[]{:S(2)}, u32[]{:S(2)}) collective-permute-start(bf16[4,224,128]{2,1,0:T(8,128)(2,1)S(1)} %constant_dynamic-update-slice_fusion.refs_0_), channel_id=1, source_target_pairs={{0,24},{4,28},{8,16},{12,20},{16,8},{20,12},{24,0},{28,4},{1,25},{... | collective-permute-start | bytes 688136 | tf_op jit(solution)/shard_map/ppermute | solution.py:410
  89.0 23.0 %collective-permute-start.12 = (bf16[4,224,128]{2,1,0:T(8,128)(2,1)S(1)}, bf16[4,224,128]{2,1,0:T(8,128)(2,1)S(1)}, u32[]{:S(2)}, u32[]{:S(2)}) collective-permute-start(bf16[4,224,128]{2,1,0:T(8,128)(2,1)S(1)} %collective-permute-done.11.refs_1_), channel_id=1, source_target_pairs={{0,4},{4,0},{8,12},{12,8},{16,20},{20,16},{24,28},{28,24},{1,5},{5... | collective-permute-start | bytes 688136 | tf_op jit(solution)/shard_map/ppermute | solution.py:410
  103.5 19.9 %collective-permute-start.10 = (bf16[4,224,128]{2,1,0:T(8,128)(2,1)S(1)}, bf16[4,224,128]{2,1,0:T(8,128)(2,1)S(1)}, u32[]{:S(2)}, u32[]{:S(2)}) collective-permute-start(bf16[4,224,128]{2,1,0:T(8,128)(2,1)S(1)} %collective-permute-done.9.refs_1_), channel_id=1, source_target_pairs={{0,4},{4,0},{8,12},{12,8},{16,20},{20,16},{24,28},{28,24},{1,5},{5... | collective-permute-start | bytes 688136 | tf_op jit(solution)/shard_map/ppermute | solution.py:410
  104.5 19.0 %collective-permute-start.8 = (bf16[4,224,128]{2,1,0:T(8,128)(2,1)S(1)}, bf16[4,224,128]{2,1,0:T(8,128)(2,1)S(1)}, u32[]{:S(2)}, u32[]{:S(2)}) collective-permute-start(bf16[4,224,128]{2,1,0:T(8,128)(2,1)S(1)} %collective-permute-done.7.refs_0_), channel_id=1, source_target_pairs={{0,4},{4,0},{8,12},{12,8},{16,20},{20,16},{24,28},{28,24},{1,5},{5... | collective-permute-start | bytes 688136 | tf_op jit(solution)/shard_map/ppermute | solution.py:410
